TPU v7x, 128 devices: a whole 4x4x4 slice. The times are simulated.
128 devices in a mesh: row: 8 (over y_hi, x), col: 16 (over y_lo, z, core).
Axes of the slice: x: 4, y: 4 (y_hi: 2, y_lo: 2; y = y_hi * 2 + y_lo), z: 4, core: 2. Of those that a mesh axis runs over, the one named last changes fastest.
Arguments:
- eigvecs: float32 [512, 65536], P(('row', 'col')), may hold values from -6 to 6
- reflectors: float32 [24, 256, 128], replicated, as said below
- offsets: int32 [24], replicated, may hold values from 0 to 65280, as said below
- lengths: int32 [24], replicated, may hold values from 128 to 256, as said below
- panels: float32 [65536, 1024], P(('row', 'col')), as said below
Outputs:
- vectors: float32 [512, 65536], P(('row', 'col'))
Inputs may be any that keep to these rules, and one draw needn't show every extreme that they name: `reflectors`: block b's column c is zero in rows above c and in rows c + 128 and below, and 1 in row c. `panels`: column c is zero in rows above 128 + c and 1 in row 128 + c. `offsets`: both ends are reached in every draw. `lengths`: both ends are reached in every draw.
All inputs are finite; a program needn't handle non-finite values.
Results may differ from a plain program's by a relative error of at most 0.0003.
Values sent between devices are 32-bit elements; how exact they have to be, the bound alone decides.
No kernel may reach another device: no remote copies, remote signals or barrier semaphores. Data moves between devices by JAX's collectives and lax.ppermute only.
A program may use at most 128 MiB of HBM per device.

v0:
```python
import jax
import jax.numpy as jnp
from jax import lax
from jax.sharding import PartitionSpec as P

B = 128
NPAN = 8


exact_mode = lax.Precision.HIGHEST


def unit_inverse(triangle):
    dimension = triangle.shape[-1]
    identity = jnp.eye(dimension, dtype=triangle.dtype)
    diagonal = jnp.sum(triangle * identity, axis=-1)
    nilpotent = triangle / diagonal[..., :, None] - identity
    result = identity - nilpotent
    power = nilpotent
    reach = 2
    while reach < dimension:
        power = jnp.matmul(power, power, precision=exact_mode)
        result = result + jnp.matmul(result, power, precision=exact_mode)
        reach = reach * 2
    return result / diagonal[..., None, :]


def wy_inverse(correlation, width):
    dimension = correlation.shape[-1]
    identity = jnp.eye(dimension, dtype=correlation.dtype)
    triangle = jnp.triu(correlation, 1) + 0.5 * correlation * identity
    count = dimension // width
    if count == 1:
        return unit_inverse(triangle)
    diagonal_blocks = jnp.stack(
        [triangle[i * width : (i + 1) * width, i * width : (i + 1) * width] for i in range(count)]
    )
    inverses = unit_inverse(diagonal_blocks)
    columns = []
    for j in range(count):
        pieces = [None] * count
        pieces[j] = inverses[j]
        for i in range(j - 1, -1, -1):
            total = jnp.zeros((width, width), correlation.dtype)
            for k in range(i + 1, j + 1):
                total = total + jnp.dot(
                    triangle[i * width : (i + 1) * width, k * width : (k + 1) * width],
                    pieces[k],
                    precision=exact_mode,
                )
            pieces[i] = -jnp.dot(inverses[i], total, precision=exact_mode)
        for i in range(j + 1, count):
            pieces[i] = jnp.zeros((width, width), correlation.dtype)
        columns.append(jnp.concatenate(pieces, axis=0))
    return jnp.concatenate(columns, axis=1)


def chase_blocks(current, reflectors, offsets, lengths):
    extent = reflectors.shape[1]
    row_index = jnp.arange(extent, dtype=jnp.int32)[None, :, None]
    masked = jnp.where(
        row_index < lengths[:, None, None], reflectors, jnp.zeros((), reflectors.dtype)
    )
    correlations = jnp.einsum("brc,brd->bcd", masked, masked, precision=exact_mode)
    factors = wy_inverse(correlations, reflectors.shape[2])

    def apply_block(carried, scanned):
        vectors, factor, offset = scanned
        window = lax.dynamic_slice_in_dim(carried, offset, extent, 1)
        projected = jnp.dot(window, vectors, precision=exact_mode)
        window = window - jnp.dot(
            jnp.dot(projected, factor.T, precision=exact_mode), vectors.T, precision=exact_mode
        )
        return (lax.dynamic_update_slice_in_dim(carried, window, offset, 1), None)

    result, unused = lax.scan(apply_block, current, (masked, factors, offsets))
    return result


def update_with(current, projected, factor, vectors):
    return current - jnp.dot(
        jnp.dot(projected, factor.T, precision=exact_mode), vectors.T, precision=exact_mode
    )


def panels_grid(current, panel_rows, panel_factors):
    for panel_index in range(NPAN - 1, -1, -1):
        column_start = panel_index * B
        vectors = panel_rows[:, column_start : column_start + B]
        factor = panel_factors[column_start : column_start + B, column_start : column_start + B]
        projected = lax.psum(jnp.dot(current, vectors, precision=exact_mode), "row")
        current = update_with(current, projected, factor, vectors)
    return current


def body(eigvecs, reflectors, offsets, lengths, panels):
    chased = chase_blocks(eigvecs, reflectors, offsets, lengths)
    correlations = lax.psum(jnp.dot(panels.T, panels, precision=exact_mode), ("row", "col"))
    panel_factors = wy_inverse(correlations, B)
    panel_rows = lax.all_gather(panels, "col", axis=0, tiled=True)
    blocked = lax.all_to_all(chased, "row", split_axis=1, concat_axis=0, tiled=True)
    blocked = panels_grid(blocked, panel_rows, panel_factors)
    return lax.all_to_all(blocked, "row", split_axis=0, concat_axis=1, tiled=True)


def solution(mesh):
    return jax.shard_map(
        body,
        mesh=mesh,
        in_specs=(P(("row", "col"), None), P(), P(), P(), P(("row", "col"), None)),
        out_specs=P(("row", "col"), None),
        check_vma=False,
    )
```

profile of v0, /device:TPU:0, one launch (start us, length us, event | category | flops | bytes accessed | tf_op | source)
XLA Modules:
  0.0 737.0 jit_solution(1960948095201372097)
XLA Ops:
  9.8 8.3 %fusion.69 = f32[1024,1024]{1,0:T(8,128)} fusion(f32[512,1024]{1,0:T(8,128)S(1)} %copy-done), kind=kOutput, calls=%fused_computation.118 | convolution fusion | flops 6442450944 | bytes 6291456 | tf_op jit(solution)/shard_map/dot_general | solution.py:98
  22.7 5.2 multiply_reduce_fusion
  53.6 4.2 fusion.37
  57.8 164.1 %while.10 = (s32[]{:T(128)}, f32[4,65536]{1,0:T(4,128)}, s32[24]{0:T(128)S(1)}, f32[24,256,128]{2,1,0:T(8,128)S(1)}, f32[24,128,128]{1,2,0:T(8,128)}, /*index=5*/s32[]{:T(128)}, s32[]{:T(128)}, s32[]{:T(128)}) while((s32[]{:T(128)}, f32[4,65536]{1,0:T(4,128)}, s32[24]{0:T(128)S(1)}, f32[24,256,128]{2,1,0:T(8,128)S(1)}, ...), condition=%wide.region_2.3_spmd, body=%wide.region_1.2_spmd.sunk | while | flops 3933189 | bytes 357523 | solution.py:76
  221.9 7.5 %all-to-all-start = ((f32[4,8,8192]{2,0,1:T(4,128)}), f32[4,8,8192]{2,0,1:T(4,128)S(1)}, u32[]{:S(2)}, u32[]{:S(2)}) async-start(f32[4,8,8192]{2,0,1:T(4,128)} %bitcast.155), calls=%async_computation | async-start | bytes 2097152 | tf_op jit(solution)/shard_map/all_to_all | solution.py:101
  229.5 17.1 %all-to-all-done = f32[4,8,8192]{2,0,1:T(4,128)S(1)} async-done(((f32[4,8,8192]{2,0,1:T(4,128)}), f32[4,8,8192]{2,0,1:T(4,128)S(1)}, u32[]{:S(2)}, u32[]{:S(2)}) %all-to-all-start) | async-done | bytes 1048608 | tf_op jit(solution)/shard_map/all_to_all | solution.py:101
  247.0 68.1 %all-reduce.2.cloned.1.call-done = f32[1024,1024]{1,0:T(8,128)} async-done(((f32[1024,1024]{1,0:T(8,128)}), f32[1024,1024]{1,0:T(8,128)}) %all-reduce.2.cloned.1.call-update) | async-done | bytes 4194320 | tf_op jit(solution)/shard_map/psum | solution.py:98
  326.2 4.2 fusion.34
  330.4 41.0 %psum.63 = f32[32,128]{1,0:T(8,128)S(1)} all-reduce(f32[32,128]{1,0:T(8,128)S(1)} %fusion.34), channel_id=1, replica_groups=mesh['row'=8,'col'=16] {'row'}, use_global_device_ids=true, to_apply=%region_3.4 | all-reduce | flops 4096 | bytes 32768 | tf_op jit(solution)/shard_map/psum | solution.py:91
  371.6 6.0 convolution_subtract_fusion.8
  377.6 4.0 fusion.31
  381.7 36.6 %psum.65 = f32[32,128]{1,0:T(8,128)S(1)} all-reduce(f32[32,128]{1,0:T(8,128)S(1)} %fusion.31), channel_id=1, replica_groups=mesh['row'=8,'col'=16] {'row'}, use_global_device_ids=true, to_apply=%region_6.7 | all-reduce | flops 4096 | bytes 32768 | tf_op jit(solution)/shard_map/psum | solution.py:91
  419.4 6.0 convolution_subtract_fusion.7
  425.4 4.0 fusion.28
  429.5 36.6 %psum.66 = f32[32,128]{1,0:T(8,128)S(1)} all-reduce(f32[32,128]{1,0:T(8,128)S(1)} %fusion.28), channel_id=1, replica_groups=mesh['row'=8,'col'=16] {'row'}, use_global_device_ids=true, to_apply=%region_7.8 | all-reduce | flops 4096 | bytes 32768 | tf_op jit(solution)/shard_map/psum | solution.py:91
  467.1 6.0 convolution_subtract_fusion.6
  473.2 4.0 fusion.25
  477.2 36.9 %psum.67 = f32[32,128]{1,0:T(8,128)S(1)} all-reduce(f32[32,128]{1,0:T(8,128)S(1)} %fusion.25), channel_id=1, replica_groups=mesh['row'=8,'col'=16] {'row'}, use_global_device_ids=true, to_apply=%region_8.9 | all-reduce | flops 4096 | bytes 32768 | tf_op jit(solution)/shard_map/psum | solution.py:91
  515.1 6.0 convolution_subtract_fusion.5
  521.2 4.0 fusion.22
  525.2 36.7 %psum.68 = f32[32,128]{1,0:T(8,128)S(1)} all-reduce(f32[32,128]{1,0:T(8,128)S(1)} %fusion.22), channel_id=1, replica_groups=mesh['row'=8,'col'=16] {'row'}, use_global_device_ids=true, to_apply=%region_9.10 | all-reduce | flops 4096 | bytes 32768 | tf_op jit(solution)/shard_map/psum | solution.py:91
  562.9 6.0 convolution_subtract_fusion.4
  569.0 4.0 fusion.19
  573.0 36.6 %psum.69 = f32[32,128]{1,0:T(8,128)S(1)} all-reduce(f32[32,128]{1,0:T(8,128)S(1)} %fusion.19), channel_id=1, replica_groups=mesh['row'=8,'col'=16] {'row'}, use_global_device_ids=true, to_apply=%region_10.11 | all-reduce | flops 4096 | bytes 32768 | tf_op jit(solution)/shard_map/psum | solution.py:91
  610.7 6.0 convolution_subtract_fusion.3
  616.8 4.0 fusion.16
  620.8 36.9 %psum.70 = f32[32,128]{1,0:T(8,128)S(1)} all-reduce(f32[32,128]{1,0:T(8,128)S(1)} %fusion.16), channel_id=1, replica_groups=mesh['row'=8,'col'=16] {'row'}, use_global_device_ids=true, to_apply=%region_11.12 | all-reduce | flops 4096 | bytes 32768 | tf_op jit(solution)/shard_map/psum | solution.py:91
  658.7 6.0 convolution_subtract_fusion.2
  664.8 4.0 fusion.13
  668.8 36.6 %psum.71 = f32[32,128]{1,0:T(8,128)S(1)} all-reduce(f32[32,128]{1,0:T(8,128)S(1)} %fusion.13), channel_id=1, replica_groups=mesh['row'=8,'col'=16] {'row'}, use_global_device_ids=true, to_apply=%region_12.13 | all-reduce | flops 4096 | bytes 32768 | tf_op jit(solution)/shard_map/psum | solution.py:91
  706.5 6.0 convolution_subtract_fusion.1
  712.9 15.4 %all_to_all.38 = f32[8,4,8192]{2,1,0:T(4,128)S(1)} all-to-all(f32[8,4,8192]{2,1,0:T(4,128)S(1)} %all_to_all.32), channel_id=1, replica_groups=mesh['row'=8,'col'=16] {'row'}, dimensions={0} | all-to-all | bytes 2097152 | tf_op jit(solution)/shard_map/all_to_all | solution.py:103
  (184 shorter events, 170.7 us)
Async XLA Ops:
  7.4 2.4 copy-start
  7.4 307.8 %all-reduce.2.cloned.1.call-start = ((), (), s32[]{:S(2)}) async-start(), calls=%async_computation.3 | async-start | bytes 8388608 | tf_op jit(solution)/shard_map/psum | solution.py:98
  18.1 0.7 copy-start.2
  18.1 308.1 %all-gather.2.cloned.1.call-start = ((), (), s32[]{:S(2)}) async-start(), calls=%async_computation.2 | async-start | bytes 35651584 | tf_op jit(solution)/shard_map/all_gather | solution.py:100
  53.6 4.3 copy-start.3
  221.9 24.7 %all-to-all-start = ((f32[4,8,8192]{2,0,1:T(4,128)}), f32[4,8,8192]{2,0,1:T(4,128)S(1)}, u32[]{:S(2)}, u32[]{:S(2)}) async-start(f32[4,8,8192]{2,0,1:T(4,128)} %bitcast.155), calls=%async_computation | async-start | bytes 2097152 | tf_op jit(solution)/shard_map/all_to_all | solution.py:101
  326.2 45.2 %copy-start.1 = (f32[8,128,128]{2,1,0:T(8,128)}, f32[8,128,128]{2,1,0:T(8,128)S(1)}, u32[]{:S(2)}) copy-start(f32[8,128,128]{2,1,0:T(8,128)S(1)} %fusion.38) | copy-start | bytes 1572868
Sparse Core Ops, SparseCore 0:
  18.2 296.8 all-reduce.1
Sparse Core Ops, SparseCore 1:
  20.3 178.9 all-gather.1
where the time goes:
time: 746 us; the launch traced here: 737 us
  blocking collectives  313 us (42%)
  matrix products  207 us (28%)
  waiting for transfers between devices  85.8 us (12%)
  local copies, waits for them, and re-layouts  55.1 us (7%)
  loops' own time  46 us (6%)
  between operations  15.7 us (2%)
  starting transfers between devices  7.53 us (1%)
    psum x8, blocking collectives, panels_grid(): projected = lax.psum(jnp.dot(current, vectors, precision=exact_mode), 'row')  298 us
    psum x1, waiting for transfers between devices, body(): lax.psum(jnp.dot(panels.T, panels, precision=exact_mode), ('row', 'col'))  68.1 us
    dot_general x8, matrix products, update_with(): jnp.dot(jnp.dot(projected, factor.T, precision=exact_mode), vectors.T, pr...  48.3 us
    another operation x1, loops' own time, chase_blocks(): result, unused = lax.scan(apply_block, current, (masked, factors, offsets))  46 us
    dynamic_update_slice x24, local copies, waits for them, and re-layouts, apply_block(): return (lax.dynamic_update_slice_in_dim(carried, window, offset, 1), None)  36.3 us
    dot_general x8, matrix products, panels_grid(): projected = lax.psum(jnp.dot(current, vectors, precision=exact_mode), 'row')  32.4 us
    dot_general x24, matrix products, apply_block(): jnp.dot(projected, factor.T, precision=exact_mode)  24.1 us
    dot_general x12, matrix products, unit_inverse(): result = result + jnp.matmul(result, power, precision=exact_mode)  22.5 us
  transfers between devices with their start and end apart: 3, of which 2 were waited for; matrix products, arithmetic and copies ran while one was open for 23% of the time, Pallas kernels for 0%

commit v1 on v0

v1 whole, which is shorter than its diff:
```python
import jax
import jax.numpy as jnp
from jax import lax
from jax.experimental import pallas as pl
from jax.experimental.pallas import tpu as pltpu
from jax.sharding import Mesh, PartitionSpec as P

F32 = jnp.float32
BF16 = jnp.bfloat16
AXES = ("yh", "x", "yl", "z", "c")
CHIPS = ("yh", "x", "yl", "z")
VMEM_LIMIT = 48 * 1024 * 1024

NN = (((1,), (0,)), ((), ()))
NT = (((1,), (1,)), ((), ()))
TN = (((0,), (0,)), ((), ()))


def dg(a, b, dims=NN):
    return lax.dot_general(a, b, dims, preferred_element_type=F32)


def split(a):
    high = a.astype(BF16)
    low = (a - high.astype(F32)).astype(BF16)
    return high, low


def dot3(a, b, dims=NN):
    (ah, al), (bh, bl) = a, b
    return dg(ah, bh, dims) + (dg(ah, bl, dims) + dg(al, bh, dims))


def dot3_stacked(a, b):
    (ah, al), (bh, bl) = a, b
    return dg(jnp.concatenate([ah, ah, al], axis=1), jnp.concatenate([bh, bl, bh], axis=0))


def iotas(n):
    return (
        lax.broadcasted_iota(jnp.int32, (n, n), 0),
        lax.broadcasted_iota(jnp.int32, (n, n), 1),
    )


def inverse_of_half(grams):
    n = grams[0].shape[0]
    row, col = iotas(n)
    eye = (row == col).astype(F32)
    upper = row < col
    inverses, strict, scale = [], [], []
    for gram in grams:
        diagonal = gram * (0.5 * eye)
        by_row = jnp.sum(diagonal, axis=1, keepdims=True)
        by_col = jnp.sum(diagonal, axis=0, keepdims=True)
        nil = jnp.where(upper, gram / by_row, 0.0)
        strict.append(nil)
        scale.append(1.0 / by_col)
        first = ((row ^ col) == 1) & ((row & 1) == 0)
        inverses.append(eye - jnp.where(first, nil, 0.0))
    size = 2
    while size < n:
        corner = ((row // (2 * size)) == (col // (2 * size))) & ((row & size) == 0) & ((col & size) != 0)
        halves = [split(x) for x in inverses]
        corners = [split(jnp.where(corner, nil, 0.0)) for nil in strict]
        middles = [split(dot3_stacked(x, m)) for x, m in zip(halves, corners)]
        inverses = [x - dot3_stacked(y, h) for x, y, h in zip(inverses, middles, halves)]
        size *= 2
    return [x * s for x, s in zip(inverses, scale)]


TOGETHER = 4


def chase_kernel(offsets, lengths, e_ref, m_ref, o_ref, kh_ref, kl_ref):
    blocks, extent, width = m_ref.shape
    o_ref[...] = e_ref[...]
    row = lax.broadcasted_iota(jnp.int32, (extent, width), 0)

    def prepare(group, carry):
        masked = []
        for u in range(TOGETHER):
            b = group * TOGETHER + u
            masked.append(split(jnp.where(row < lengths[b], m_ref[b], 0.0)))
        grams = [dot3(m, m, TN) for m in masked]
        factors = [split(f) for f in inverse_of_half(grams)]
        lefts = [split(dot3(m, f, NT)) for m, f in zip(masked, factors)]
        for u in range(TOGETHER):
            high, low = split(dot3(lefts[u], masked[u], NT))
            b = group * TOGETHER + u
            kh_ref[b] = high
            kl_ref[b] = low
        return carry

    lax.fori_loop(0, blocks // TOGETHER, prepare, 0)

    rows = e_ref.shape[1]
    tiles = e_ref.shape[0]
    lane = lax.broadcasted_iota(jnp.int32, (rows, 128), 1)

    def step(b, carry):
        offset = offsets[b]
        tile = jnp.minimum(offset // 128, tiles - 3)
        shift = offset - tile * 128
        v0, v1, v2 = o_ref[tile], o_ref[tile + 1], o_ref[tile + 2]
        left = (128 - shift) & 127
        r0 = pltpu.roll(v0, left, 1)
        r1 = pltpu.roll(v1, left, 1)
        r2 = pltpu.roll(v2, left, 1)
        inside = lane < 128 - shift
        window = jnp.concatenate([jnp.where(inside, r0, r1), jnp.where(inside, r1, r2)], axis=1)
        high = window.astype(BF16).astype(F32)
        both = jnp.concatenate([high, window - high], axis=0).astype(BF16)
        change = dg(both, kh_ref[b]) + dg(both, kl_ref[b])
        change = change[:rows] + change[rows:]
        right = shift & 127
        q0 = pltpu.roll(change[:, :128], right, 1)
        q1 = pltpu.roll(change[:, 128:], right, 1)
        after = lane >= shift
        o_ref[tile] = v0 - jnp.where(after, q0, 0.0)
        o_ref[tile + 1] = v1 - jnp.where(after, q1, q0)
        o_ref[tile + 2] = v2 - jnp.where(after, 0.0, q1)
        return carry

    lax.fori_loop(0, blocks, step, 0)


def vmem():
    return pl.BlockSpec(memory_space=pltpu.VMEM)


def smem():
    return pl.BlockSpec(memory_space=pltpu.SMEM)


def params():
    return pltpu.CompilerParams(vmem_limit_bytes=VMEM_LIMIT)


def chase(tiles, reflectors, offsets, lengths):
    blocks, extent, width = reflectors.shape
    return pl.pallas_call(
        chase_kernel,
        out_shape=jax.ShapeDtypeStruct(tiles.shape, F32),
        in_specs=[smem(), smem(), vmem(), vmem()],
        out_specs=vmem(),
        scratch_shapes=[pltpu.VMEM((blocks, extent, extent), BF16)] * 2,
        compiler_params=params(),
        cost_estimate=pl.CostEstimate(flops=20 * 10**9, bytes_accessed=5 << 20, transcendentals=0),
        name="chase",
    )(offsets, lengths, tiles, reflectors)


WIDE = 256
PAIRS = [(i, j) for i in range(4) for j in range(i, 4)]


def gram_kernel(v_ref, g_ref):
    halves = [split(v_ref[:, i * WIDE : (i + 1) * WIDE]) for i in range(4)]
    for at, (i, j) in enumerate(PAIRS):
        block = dot3(halves[i], halves[j], TN)
        for h in range(2):
            g_ref[pl.ds((at * 2 + h) * WIDE, WIDE), :] = block[:, h * 128 : (h + 1) * 128]


def gram(panels):
    return pl.pallas_call(
        gram_kernel,
        out_shape=jax.ShapeDtypeStruct((len(PAIRS) * 2 * WIDE, 128), F32),
        in_specs=[vmem()],
        out_specs=vmem(),
        compiler_params=params(),
        cost_estimate=pl.CostEstimate(flops=2 * 10**9, bytes_accessed=4 << 20, transcendentals=0),
        name="gram",
    )(panels)


def factor_kernel(g_ref, th_ref, tl_ref, sh_ref, sl_ref):
    def block(at):
        return jnp.concatenate(
            [g_ref[pl.ds((at * 2 + h) * WIDE, WIDE), :] for h in range(2)], axis=1
        )

    other = 0
    diagonals = []
    for at, (i, j) in enumerate(PAIRS):
        if i == j:
            diagonals.append(block(at))
        else:
            high, low = split(block(at).T)
            sh_ref[other] = high
            sl_ref[other] = low
            other += 1
    small = []
    for d in diagonals:
        small.extend([d[:128, :128], d[128:, 128:]])
    inverses = inverse_of_half(small[:4]) + inverse_of_half(small[4:])
    for p, d in enumerate(diagonals):
        a, c = inverses[2 * p], inverses[2 * p + 1]
        corner = -dot3_stacked(split(dot3_stacked(split(a), split(d[:128, 128:]))), split(c))
        whole = jnp.concatenate(
            [
                jnp.concatenate([a.T, jnp.zeros((128, 128), F32)], axis=1),
                jnp.concatenate([corner.T, c.T], axis=1),
            ],
            axis=0,
        )
        high, low = split(whole)
        th_ref[p] = high
        tl_ref[p] = low


def factor(g):
    shapes = [(4, WIDE, WIDE)] * 2 + [(6, WIDE, WIDE)] * 2
    return pl.pallas_call(
        factor_kernel,
        out_shape=[jax.ShapeDtypeStruct(s, BF16) for s in shapes],
        in_specs=[vmem()],
        out_specs=[vmem()] * 4,
        compiler_params=params(),
        cost_estimate=pl.CostEstimate(flops=8 * 10**9, bytes_accessed=5 << 20, transcendentals=0),
        name="factor",
    )(g)


def rows_of(ref, j):
    return jnp.concatenate([ref[pl.ds(j * 4 + r, 64, stride=32), :] for r in range(4)], axis=0)


def project_kernel(core, e_ref, own_ref, other_ref, p_ref):
    c = core[0]
    total = [jnp.zeros((256, WIDE), F32) for _ in range(4)]
    for v_ref, first in ((own_ref, 4 * c), (other_ref, 4 - 4 * c)):
        left = split(jnp.concatenate([rows_of(e_ref, first + k) for k in range(4)], axis=1))
        for n in range(4):
            total[n] += dot3(left, split(v_ref[:, n * WIDE : (n + 1) * WIDE]))
    for n in range(8):
        block = total[n // 2][:, (n % 2) * 128 : (n % 2) * 128 + 128]
        for r in range(4):
            p_ref[pl.ds(n * 4 + r, 64, stride=32), :] = block[r * 64 : (r + 1) * 64]


def project(core, e, own, other):
    return pl.pallas_call(
        project_kernel,
        out_shape=jax.ShapeDtypeStruct(e.shape, F32),
        in_specs=[smem(), vmem(), vmem(), vmem()],
        out_specs=vmem(),
        compiler_params=params(),
        cost_estimate=pl.CostEstimate(flops=2 * 10**9, bytes_accessed=6 << 20, transcendentals=0),
        name="project",
    )(core, e, own, other)


def solve_kernel(p_ref, th_ref, tl_ref, sh_ref, sl_ref, w_ref):
    total = p_ref[0]
    for s in range(1, p_ref.shape[0]):
        total = total + p_ref[s]
    rest = [
        jnp.concatenate([total[8 * p : 8 * p + 4], total[8 * p + 4 : 8 * p + 8]], axis=1)
        for p in range(4)
    ]

    def times(a, bh, bl):
        high = a.astype(BF16).astype(F32)
        both = jnp.concatenate([high, a - high], axis=0).astype(BF16)
        product = dg(both, bh) + dg(both, bl)
        return product[:4] + product[4:]

    others = [(i, j) for (i, j) in PAIRS if i != j]
    pieces = [None] * 4
    for q in range(3, -1, -1):
        solved = times(rest[q], th_ref[q], tl_ref[q])
        pieces[q] = jnp.concatenate([solved[:, :128], solved[:, 128:]], axis=0)
        for p in range(q):
            at = others.index((p, q))
            rest[p] = rest[p] - times(solved, sh_ref[at], sl_ref[at])
    result = jnp.concatenate(pieces, axis=0)
    w_ref[...] = jnp.broadcast_to(result[None], w_ref.shape)


def solve(p, factors):
    return pl.pallas_call(
        solve_kernel,
        out_shape=jax.ShapeDtypeStruct(p.shape, F32),
        in_specs=[vmem()] * 5,
        out_specs=vmem(),
        compiler_params=params(),
        cost_estimate=pl.CostEstimate(flops=10**9, bytes_accessed=4 << 20, transcendentals=0),
        name="solve",
    )(p, *factors)


def update_kernel(core, e_ref, w_ref, own_ref, other_ref, o_ref):
    c = core[0]
    left = split(jnp.concatenate([rows_of(w_ref, n) for n in range(8)], axis=1))
    for v_ref, first in ((own_ref, 4 * c), (other_ref, 4 - 4 * c)):
        for k in range(2):
            change = dot3(left, split(v_ref[k * WIDE : (k + 1) * WIDE, :]), NT)
            for h in range(2):
                j = first + 2 * k + h
                for r in range(4):
                    at = pl.ds(j * 4 + r, 64, stride=32)
                    o_ref[at, :] = e_ref[at, :] - change[r * 64 : (r + 1) * 64, h * 128 : (h + 1) * 128]


def update(core, e, w, own, other):
    return pl.pallas_call(
        update_kernel,
        out_shape=jax.ShapeDtypeStruct(e.shape, F32),
        in_specs=[smem(), vmem(), vmem(), vmem(), vmem()],
        out_specs=vmem(),
        compiler_params=params(),
        cost_estimate=pl.CostEstimate(flops=2 * 10**9, bytes_accessed=7 << 20, transcendentals=0),
        name="update",
    )(core, e, w, own, other)


def to_chips(a):
    return lax.all_to_all(a, CHIPS, split_axis=0, concat_axis=0, tiled=True)


def body(eigvecs, reflectors, offsets, lengths, panels):
    core = lax.axis_index("c").astype(jnp.int32).reshape(1)
    other = lax.ppermute(panels, "c", [(0, 1), (1, 0)])
    partial = gram(panels).reshape(128, 40, 128)
    partial = lax.all_to_all(partial, AXES, split_axis=0, concat_axis=0, tiled=True)
    share = jnp.sum(partial, axis=0)
    whole = jnp.broadcast_to(share[None], (128, 40, 128))
    whole = lax.all_to_all(whole, AXES, split_axis=0, concat_axis=0, tiled=True)
    factors = factor(whole.reshape(5120, 128))

    tiles = eigvecs.reshape(4, 512, 128).transpose(1, 0, 2)
    chased = chase(tiles, reflectors, offsets, lengths)
    mine = to_chips(chased.reshape(64, 32, 128)).reshape(2048, 128)
    projected = to_chips(project(core, mine, panels, other).reshape(64, 32, 128))
    weights = to_chips(solve(projected, factors)).reshape(2048, 128)
    result = to_chips(update(core, mine, weights, panels, other).reshape(64, 32, 128))
    return result.reshape(512, 4, 128).transpose(1, 0, 2).reshape(4, 65536)


def solution(mesh):
    fine = Mesh(mesh.devices.reshape(2, 4, 2, 4, 2), AXES)
    return jax.shard_map(
        body,
        mesh=fine,
        in_specs=(P(AXES, None), P(), P(), P(), P(AXES, None)),
        out_specs=P(AXES, None),
        check_vma=False,
    )
```

time: 746 us -> 200 us (0.27); the launches traced: 737 us -> 200 us
  blocking collectives: 313 us -> 45 us
  matrix products: 207 us -> 0 us
  loops' own time: 46 us -> 0 us
  Pallas kernels: 0 us -> 44.3 us
  local copies, waits for them, and re-layouts: 55.1 us -> 15.2 us
  waiting for transfers between devices: 85.8 us -> 65.1 us
  starting transfers between devices: 7.53 us -> 27.9 us
  between operations: 15.7 us -> 0.15 us
    psum x8 -> x0, blocking collectives: 298 us -> none  [panels_grid(): projected = lax.psum(jnp.dot(current, vectors, precision=exact_mode), 'row')]
    dot_general x122 -> x0, matrix products: 207 us -> none  [the longest x8 48.3 us: update_with(): jnp.dot(jnp.dot(projected, factor.T, precision=exact_mode), vectors.T, pr...]
    psum x1 -> x0, waiting for transfers between devices: 68.1 us -> none  [body(): lax.psum(jnp.dot(panels.T, panels, precision=exact_mode), ('row', 'col'))]
    another operation x1 -> x0, loops' own time: 46 us -> none  [chase_blocks(): result, unused = lax.scan(apply_block, current, (masked, factors, offsets))]
    pallas_call x0 -> x6, Pallas kernels: none -> 44.3 us  [the longest x1 25.4 us: chase(): pl.pallas_call(chase_kernel, out_shape=jax.ShapeDtypeStruct(tiles.shape,...]
    all_to_all x1 -> x4, waiting for transfers between devices: 17.1 us -> 60.6 us  [the longest x2 28.9 us: to_chips(): return lax.all_to_all(a, CHIPS, split_axis=0, concat_axis=0, tiled=True)]
    dynamic_update_slice x24 -> x0, local copies, waits for them, and re-layouts: 36.3 us -> none  [apply_block(): return (lax.dynamic_update_slice_in_dim(carried, window, offset, 1), None)]
    all_to_all x1 -> x2, blocking collectives: 15.4 us -> 45 us  [to_chips(): return lax.all_to_all(a, CHIPS, split_axis=0, concat_axis=0, tiled=True)]
  transfers between devices with their start and end apart: 3 -> 5, of which waited for: 2 -> 5; matrix products, arithmetic and copies ran while one was open for 23% -> 1% of each run, Pallas kernels for 0% -> 17%
where the time goes in v1:
time: 200 us
  waiting for transfers between devices  65.1 us (33%)
  blocking collectives  45 us (22%)
  Pallas kernels  44.3 us (22%)
  starting transfers between devices  27.9 us (14%)
  local copies, waits for them, and re-layouts  15.2 us (8%)
    all_to_all x2, blocking collectives, to_chips(): return lax.all_to_all(a, CHIPS, split_axis=0, concat_axis=0, tiled=True)  45 us
    all_to_all x2, waiting for transfers between devices, to_chips(): return lax.all_to_all(a, CHIPS, split_axis=0, concat_axis=0, tiled=True)  28.9 us
    pallas_call x1, Pallas kernels, chase(): pl.pallas_call(chase_kernel, out_shape=jax.ShapeDtypeStruct(tiles.shape,...  25.4 us
    all_to_all x1, waiting for transfers between devices, body(): whole = lax.all_to_all(whole, AXES, split_axis=0, concat_axis=0, tiled=True)  22.9 us
    unnamed x31, local copies, waits for them, and re-layouts  13.4 us
    all_to_all x1, starting transfers between devices, body(): lax.all_to_all(partial, AXES, split_axis=0, concat_axis=0, tiled=True)  11.6 us
    all_to_all x2, starting transfers between devices, to_chips(): return lax.all_to_all(a, CHIPS, split_axis=0, concat_axis=0, tiled=True)  11 us
    all_to_all x1, waiting for transfers between devices, body(): lax.all_to_all(partial, AXES, split_axis=0, concat_axis=0, tiled=True)  8.85 us
  transfers between devices with their start and end apart: 5, of which 5 were waited for; matrix products, arithmetic and copies ran while one was open for 1% of the time, Pallas kernels for 17%

profile of v1, /device:TPU:0, one launch (start us, length us, event | category | flops | bytes accessed | tf_op | source)
XLA Modules:
  0.0 199.6 jit_solution(4535791293517409418)
XLA Ops:
  0.0 1.6 copy-done.9
  1.6 3.8 %gram.1 = f32[5120,128]{1,0:T(8,128)} custom-call(f32[512,1024]{1,0:T(8,128)S(1)} %copy-done.9), custom_call_target="tpu_custom_call" | custom-call | flops 2000000000 | bytes 4194304 | tf_op jit(solution)/shard_map/gram/pallas_call | solution.py:167
  5.4 11.6 %all-to-all-start.2 = ((f32[128,40,128]{2,1,0:T(8,128)}), f32[128,40,128]{2,1,0:T(8,128)}, u32[]{:S(2)}, u32[]{:S(2)}) async-start(f32[128,40,128]{2,1,0:T(8,128)} %bitcast.6), calls=%async_computation.2 | async-start | bytes 5242880 | tf_op jit(solution)/shard_map/all_to_all | solution.py:327
  17.0 1.2 copy-done.12
  18.3 25.4 %chase.1 = f32[512,4,128]{2,1,0:T(4,128)} custom-call(s32[24]{0:T(128)S(1)} %copy-done.13, s32[24]{0:T(128)S(1)} %copy-done.14, f32[512,4,128]{2,1,0:T(4,128)S(1)} %bitcast.25, f32[24,256,128]{2,1,0:T(8,128)S(1)} %copy-done.8), custom_call_target="tpu_custom_call" | custom-call | flops 20000000000 | bytes 5242880 | tf_op jit(solution)/shard_map/chase/pallas_call | solution.py:142
  43.6 8.9 %all-to-all-done.2 = f32[128,40,128]{2,1,0:T(8,128)} async-done(((f32[128,40,128]{2,1,0:T(8,128)}), f32[128,40,128]{2,1,0:T(8,128)}, u32[]{:S(2)}, u32[]{:S(2)}) %all-to-all-start.2) | async-done | bytes 2621472 | tf_op jit(solution)/shard_map/all_to_all | solution.py:327
  52.5 5.4 %all-to-all-start = ((f32[64,32,128]{2,1,0:T(8,128)}), f32[64,32,128]{2,1,0:T(8,128)S(1)}, u32[]{:S(2)}, u32[]{:S(2)}) async-start(f32[64,32,128]{2,1,0:T(8,128)} %bitcast.3), calls=%async_computation | async-start | bytes 2097152 | tf_op jit(solution)/shard_map/all_to_all | solution.py:320
  57.9 2.0 reduce_sum.9
  59.9 16.9 %all-to-all-done = f32[64,32,128]{2,1,0:T(8,128)S(1)} async-done(((f32[64,32,128]{2,1,0:T(8,128)}), f32[64,32,128]{2,1,0:T(8,128)S(1)}, u32[]{:S(2)}, u32[]{:S(2)}) %all-to-all-start) | async-done | bytes 1048608 | tf_op jit(solution)/shard_map/all_to_all | solution.py:320
  76.7 1.8 broadcast_in_dim.2
  78.5 0.0 copy-done.2
  78.5 5.1 %all-to-all-start.3 = ((f32[128,40,128]{2,1,0:T(8,128)}), f32[128,40,128]{2,1,0:T(8,128)S(1)}, u32[]{:S(2)}, u32[]{:S(2)}) async-start(f32[128,40,128]{2,1,0:T(8,128)} %broadcast_in_dim.2), calls=%async_computation.3 | async-start | bytes 5242880 | tf_op jit(solution)/shard_map/all_to_all | solution.py:330
  83.7 0.1 collective-permute-start
  83.8 4.5 %collective-permute-done.other_ref = f32[512,1024]{1,0:T(8,128)} collective-permute-done((f32[512,1024]{1,0:T(8,128)}, f32[512,1024]{1,0:T(8,128)}, u32[]{:S(2)}, u32[]{:S(2)}) %collective-permute-start) | collective-permute-done | bytes 2097184 | tf_op jit(solution)/shard_map/ppermute | solution.py:325
  88.3 1.2 copy-done.3
  89.5 1.6 copy-done.10
  91.1 4.6 %project.1 = f32[2048,128]{1,0:T(8,128)S(1)} custom-call(s32[1]{0:T(128)} %bitcast.core, f32[2048,128]{1,0:T(8,128)S(1)} %bitcast.20, f32[512,1024]{1,0:T(8,128)S(1)} %copy-done.10, f32[512,1024]{1,0:T(8,128)} %collective-permute-done.other_ref), custom_call_target="tpu_custom_call" | custom-call | flops 2000000000 | bytes 6291456 | tf_op jit(solution)/shard_map/project/pallas_call | solution.py:244
  95.7 1.0 copy-done.5
  96.7 22.9 %all-to-all-done.3 = f32[128,40,128]{2,1,0:T(8,128)S(1)} async-done(((f32[128,40,128]{2,1,0:T(8,128)}), f32[128,40,128]{2,1,0:T(8,128)S(1)}, u32[]{:S(2)}, u32[]{:S(2)}) %all-to-all-start.3) | async-done | bytes 2621472 | tf_op jit(solution)/shard_map/all_to_all | solution.py:330
  119.5 1.5 copy-done
  121.0 5.6 %all-to-all-start.1 = ((f32[64,32,128]{2,1,0:T(8,128)}), f32[64,32,128]{2,1,0:T(8,128)S(1)}, u32[]{:S(2)}, u32[]{:S(2)}) async-start(f32[64,32,128]{2,1,0:T(8,128)} %bitcast.22), calls=%async_computation.1 | async-start | bytes 2097152 | tf_op jit(solution)/shard_map/all_to_all | solution.py:320
  126.6 1.7 copy-done.1
  128.4 4.0 %factor.1 = (bf16[4,256,256]{2,1,0:T(8,128)(2,1)S(1)}, bf16[4,256,256]{2,1,0:T(8,128)(2,1)S(1)}, bf16[6,256,256]{2,1,0:T(8,128)(2,1)S(1)}, bf16[6,256,256]{2,1,0:T(8,128)(2,1)S(1)}) custom-call(f32[5120,128]{1,0:T(8,128)S(1)} %bitcast.19), custom_call_target="tpu_custom_call" | custom-call | flops 8000000000 | bytes 5242880 | tf_op jit(solution)/shard_map/factor/pallas_call | solution.py:215
  132.4 0.8 copy-done.6
  133.2 12.0 %all-to-all-done.1.p_ref = f32[64,32,128]{2,1,0:T(8,128)S(1)} async-done(((f32[64,32,128]{2,1,0:T(8,128)}), f32[64,32,128]{2,1,0:T(8,128)S(1)}, u32[]{:S(2)}, u32[]{:S(2)}) %all-to-all-start.1) | async-done | bytes 1048608 | tf_op jit(solution)/shard_map/all_to_all | solution.py:320
  145.3 1.0 copy-done.7
  146.3 1.3 solve.1
  147.6 22.8 %all_to_all.30 = f32[64,32,128]{2,1,0:T(8,128)S(1)} all-to-all(f32[64,32,128]{2,1,0:T(8,128)S(1)} %solve.1), channel_id=1, replica_groups=mesh['yh'=2,'x'=4,'yl'=2,'z'=4,'c'=2] {'yh','x','yl','z'}, dimensions={0} | all-to-all | bytes 2097152 | tf_op jit(solution)/shard_map/all_to_all | solution.py:320
  170.4 5.2 %update.1 = f32[2048,128]{1,0:T(8,128)S(1)} custom-call(s32[1]{0:T(128)} %bitcast.core, f32[2048,128]{1,0:T(8,128)S(1)} %bitcast.21, f32[2048,128]{1,0:T(8,128)S(1)} %bitcast.23, f32[512,1024]{1,0:T(8,128)S(1)} %copy-done.11, f32[512,1024]{1,0:T(8,128)} %collective-permute-done.other_ref), custom_call_target="tpu_custom_call" | custom-call | flops 2000000000 | bytes 7340032 | tf_op jit(solution)/shard_map/update/pallas_call | solution.py:308
  175.7 22.1 %all_to_all.31 = f32[64,32,128]{2,1,0:T(8,128)S(1)} all-to-all(f32[64,32,128]{2,1,0:T(8,128)S(1)} %bitcast.24), channel_id=1, replica_groups=mesh['yh'=2,'x'=4,'yl'=2,'z'=4,'c'=2] {'yh','x','yl','z'}, dimensions={0} | all-to-all | bytes 2097152 | tf_op jit(solution)/shard_map/all_to_all | solution.py:320
  197.8 0.1 copy.11
  197.9 1.6 copy.10
  (20 shorter events, 0.0 us)
Async XLA Ops:
  0.0 1.6 copy-start.9
  5.4 11.6 %copy-start.8 = (f32[24,256,128]{2,1,0:T(8,128)S(1)}, f32[24,256,128]{2,1,0:T(8,128)}, u32[]{:S(2)}) copy-start(f32[24,256,128]{2,1,0:T(8,128)} %m_ref.1) | copy-start | bytes 9437188
  5.4 11.6 %copy-start.13 = (s32[24]{0:T(128)S(1)}, s32[24]{0:T(128)}, u32[]{:S(2)}) copy-start(s32[24]{0:T(128)} %offsets.1) | copy-start | bytes 292
  5.4 11.6 %copy-start.14 = (s32[24]{0:T(128)S(1)}, s32[24]{0:T(128)}, u32[]{:S(2)}) copy-start(s32[24]{0:T(128)} %lengths.1) | copy-start | bytes 292
  5.4 47.1 %all-to-all-start.2 = ((f32[128,40,128]{2,1,0:T(8,128)}), f32[128,40,128]{2,1,0:T(8,128)}, u32[]{:S(2)}, u32[]{:S(2)}) async-start(f32[128,40,128]{2,1,0:T(8,128)} %bitcast.6), calls=%async_computation.2 | async-start | bytes 5242880 | tf_op jit(solution)/shard_map/all_to_all | solution.py:327
  17.0 1.2 copy-start.12
  52.5 24.3 %all-to-all-start = ((f32[64,32,128]{2,1,0:T(8,128)}), f32[64,32,128]{2,1,0:T(8,128)S(1)}, u32[]{:S(2)}, u32[]{:S(2)}) async-start(f32[64,32,128]{2,1,0:T(8,128)} %bitcast.3), calls=%async_computation | async-start | bytes 2097152 | tf_op jit(solution)/shard_map/all_to_all | solution.py:320
  76.7 1.8 copy-start.2
  78.5 41.0 %all-to-all-start.3 = ((f32[128,40,128]{2,1,0:T(8,128)}), f32[128,40,128]{2,1,0:T(8,128)S(1)}, u32[]{:S(2)}, u32[]{:S(2)}) async-start(f32[128,40,128]{2,1,0:T(8,128)} %broadcast_in_dim.2), calls=%async_computation.3 | async-start | bytes 5242880 | tf_op jit(solution)/shard_map/all_to_all | solution.py:330
  83.7 4.6 %collective-permute-start = (f32[512,1024]{1,0:T(8,128)}, f32[512,1024]{1,0:T(8,128)}, u32[]{:S(2)}, u32[]{:S(2)}) collective-permute-start(f32[512,1024]{1,0:T(8,128)} %own_ref.3), channel_id=1, source_target_pairs={{0,1},{1,0},{2,3},{3,2},{4,5},{5,4},{6,7},{7,6},{8,9},{9,8},{10,11... | collective-permute-start | bytes 6291464 | tf_op jit(solution)/shard_map/ppermute | solution.py:325
  88.3 1.2 copy-start.3
  89.5 1.6 copy-start.10
  95.7 1.0 copy-start.5
  119.5 1.5 copy-start
  121.0 24.2 %all-to-all-start.1 = ((f32[64,32,128]{2,1,0:T(8,128)}), f32[64,32,128]{2,1,0:T(8,128)S(1)}, u32[]{:S(2)}, u32[]{:S(2)}) async-start(f32[64,32,128]{2,1,0:T(8,128)} %bitcast.22), calls=%async_computation.1 | async-start | bytes 2097152 | tf_op jit(solution)/shard_map/all_to_all | solution.py:320
  126.6 1.7 copy-start.1
  132.4 0.8 copy-start.6
  145.3 1.0 copy-start.7
  146.3 24.1 %copy-start.4 = (f32[64,32,128]{2,1,0:T(8,128)S(1)}, f32[64,32,128]{2,1,0:T(8,128)}, u32[]{:S(2)}) copy-start(f32[64,32,128]{2,1,0:T(8,128)} %copy-done.2) | copy-start | bytes 3145732
  146.3 24.1 %copy-start.11 = (f32[512,1024]{1,0:T(8,128)S(1)}, f32[512,1024]{1,0:T(8,128)}, u32[]{:S(2)}) copy-start(f32[512,1024]{1,0:T(8,128)} %own_ref.3) | copy-start | bytes 6291460

commit v2 on v1

--- a/solution.py
+++ b/solution.py
@@ -9,7 +9,7 @@
 BF16 = jnp.bfloat16
 AXES = ("yh", "x", "yl", "z", "c")
 CHIPS = ("yh", "x", "yl", "z")
-VMEM_LIMIT = 48 * 1024 * 1024
+VMEM_LIMIT = 20 * 1024 * 1024
 
 NN = (((1,), (0,)), ((), ()))
 NT = (((1,), (1,)), ((), ()))
@@ -72,9 +72,15 @@
 TOGETHER = 4
 
 
+def place(tile):
+    return (tile // 8) * 18 + tile % 8
+
+
 def chase_kernel(offsets, lengths, e_ref, m_ref, o_ref, kh_ref, kl_ref):
     blocks, extent, width = m_ref.shape
-    o_ref[...] = e_ref[...]
+    tiles, rows = e_ref.shape[0], e_ref.shape[1]
+    for s in range(tiles // 8):
+        o_ref[s * 18 : s * 18 + 8] = e_ref[s * 8 : s * 8 + 8]
     row = lax.broadcasted_iota(jnp.int32, (extent, width), 0)
 
     def prepare(group, carry):
@@ -93,16 +99,14 @@
         return carry
 
     lax.fori_loop(0, blocks // TOGETHER, prepare, 0)
-
-    rows = e_ref.shape[1]
-    tiles = e_ref.shape[0]
     lane = lax.broadcasted_iota(jnp.int32, (rows, 128), 1)
 
     def step(b, carry):
         offset = offsets[b]
         tile = jnp.minimum(offset // 128, tiles - 3)
         shift = offset - tile * 128
-        v0, v1, v2 = o_ref[tile], o_ref[tile + 1], o_ref[tile + 2]
+        at = [place(tile + k) for k in range(3)]
+        v0, v1, v2 = [o_ref[k] for k in at]
         left = (128 - shift) & 127
         r0 = pltpu.roll(v0, left, 1)
         r1 = pltpu.roll(v1, left, 1)
@@ -117,12 +121,28 @@
         q0 = pltpu.roll(change[:, :128], right, 1)
         q1 = pltpu.roll(change[:, 128:], right, 1)
         after = lane >= shift
-        o_ref[tile] = v0 - jnp.where(after, q0, 0.0)
-        o_ref[tile + 1] = v1 - jnp.where(after, q1, q0)
-        o_ref[tile + 2] = v2 - jnp.where(after, 0.0, q1)
+        o_ref[at[0]] = v0 - jnp.where(after, q0, 0.0)
+        o_ref[at[1]] = v1 - jnp.where(after, q1, q0)
+        o_ref[at[2]] = v2 - jnp.where(after, 0.0, q1)
         return carry
 
     lax.fori_loop(0, blocks, step, 0)
+
+
+def join_kernel(e_ref, g_ref, o_ref, share_ref, sems):
+    chips = o_ref.shape[0] // 18
+    share = g_ref[0:10]
+    for s in range(1, chips):
+        share = share + g_ref[s * 10 : s * 10 + 10]
+    share_ref[...] = share
+    copies = [
+        pltpu.make_async_copy(share_ref, o_ref.at[pl.ds(s * 18 + 8, 10)], sems.at[s])
+        for s in range(chips)
+    ]
+    for copy in copies:
+        copy.start()
+    for copy in copies:
+        copy.wait()
 
 
 def vmem():
@@ -137,60 +157,92 @@
     return pltpu.CompilerParams(vmem_limit_bytes=VMEM_LIMIT)
 
 
+def hbm():
+    return pl.BlockSpec(memory_space=pltpu.HBM)
+
+
 def chase(tiles, reflectors, offsets, lengths):
     blocks, extent, width = reflectors.shape
     return pl.pallas_call(
         chase_kernel,
-        out_shape=jax.ShapeDtypeStruct(tiles.shape, F32),
+        out_shape=jax.ShapeDtypeStruct((64 * 18, 4, 128), F32),
         in_specs=[smem(), smem(), vmem(), vmem()],
         out_specs=vmem(),
         scratch_shapes=[pltpu.VMEM((blocks, extent, extent), BF16)] * 2,
         compiler_params=params(),
-        cost_estimate=pl.CostEstimate(flops=20 * 10**9, bytes_accessed=5 << 20, transcendentals=0),
+        cost_estimate=pl.CostEstimate(flops=20 * 10**9, bytes_accessed=6 << 20, transcendentals=0),
         name="chase",
     )(offsets, lengths, tiles, reflectors)
 
 
+def join(chased, parts):
+    return pl.pallas_call(
+        join_kernel,
+        out_shape=jax.ShapeDtypeStruct(chased.shape, F32),
+        in_specs=[hbm(), vmem()],
+        out_specs=hbm(),
+        scratch_shapes=[pltpu.VMEM((10, 4, 128), F32), pltpu.SemaphoreType.DMA((64,))],
+        input_output_aliases={0: 0},
+        compiler_params=params(),
+        cost_estimate=pl.CostEstimate(flops=10**6, bytes_accessed=3 << 20, transcendentals=0),
+        name="join",
+    )(chased, parts)
+
+
 WIDE = 256
-PAIRS = [(i, j) for i in range(4) for j in range(i, 4)]
-
-
-def gram_kernel(v_ref, g_ref):
-    halves = [split(v_ref[:, i * WIDE : (i + 1) * WIDE]) for i in range(4)]
-    for at, (i, j) in enumerate(PAIRS):
-        block = dot3(halves[i], halves[j], TN)
+ORDER = ((0, 1, 2, 3), (2, 0, 3, 1))
+LOCAL = ((0, 1), (1, 2), (2, 3), (1, 1), (2, 2))
+MADE = [(ORDER[c][i], ORDER[c][j]) for c in range(2) for (i, j) in LOCAL]
+UPPER = [(i, j) for i in range(4) for j in range(i + 1, 4)]
+
+
+def gram_kernel(core, own_ref, other_ref, g_ref):
+    c = core[0]
+    order = (2 * c, 1 - c, 2 + c, 3 - 2 * c)
+    blocks = [None] * len(LOCAL)
+    for ref in (own_ref, other_ref):
+        halves = [split(ref[:, pl.ds(pl.multiple_of(o * WIDE, WIDE), WIDE)]) for o in order]
+        for at, (i, j) in enumerate(LOCAL):
+            block = dot3(halves[i], halves[j], TN)
+            blocks[at] = block if blocks[at] is None else blocks[at] + block
+    for at, block in enumerate(blocks):
         for h in range(2):
             g_ref[pl.ds((at * 2 + h) * WIDE, WIDE), :] = block[:, h * 128 : (h + 1) * 128]
 
 
-def gram(panels):
+def gram(core, own, other):
     return pl.pallas_call(
         gram_kernel,
-        out_shape=jax.ShapeDtypeStruct((len(PAIRS) * 2 * WIDE, 128), F32),
-        in_specs=[vmem()],
+        out_shape=jax.ShapeDtypeStruct((len(LOCAL) * 2 * WIDE, 128), F32),
+        in_specs=[smem(), vmem(), vmem()],
         out_specs=vmem(),
         compiler_params=params(),
-        cost_estimate=pl.CostEstimate(flops=2 * 10**9, bytes_accessed=4 << 20, transcendentals=0),
+        cost_estimate=pl.CostEstimate(flops=2 * 10**9, bytes_accessed=5 << 20, transcendentals=0),
         name="gram",
-    )(panels)
-
-
-def factor_kernel(g_ref, th_ref, tl_ref, sh_ref, sl_ref):
-    def block(at):
-        return jnp.concatenate(
-            [g_ref[pl.ds((at * 2 + h) * WIDE, WIDE), :] for h in range(2)], axis=1
-        )
-
-    other = 0
-    diagonals = []
-    for at, (i, j) in enumerate(PAIRS):
+    )(core, own, other)
+
+
+def factor_kernel(core, own_ref, other_ref, th_ref, tl_ref, sh_ref, sl_ref):
+    first = core[0] == 0
+
+    def block(c, at):
+        halves = []
+        for h in range(2):
+            rows = pl.ds((at * 2 + h) * WIDE, WIDE)
+            mine, theirs = own_ref[rows, :], other_ref[rows, :]
+            halves.append(jnp.where(first, mine, theirs) if c == 0 else jnp.where(first, theirs, mine))
+        return jnp.concatenate(halves, axis=1)
+
+    diagonals = [None] * 4
+    for at, (i, j) in enumerate(MADE):
+        value = block(at // len(LOCAL), at % len(LOCAL))
         if i == j:
-            diagonals.append(block(at))
+            diagonals[i] = value
         else:
-            high, low = split(block(at).T)
-            sh_ref[other] = high
-            sl_ref[other] = low
-            other += 1
+            high, low = split(value.T if i < j else value)
+            slot = UPPER.index((min(i, j), max(i, j)))
+            sh_ref[slot] = high
+            sl_ref[slot] = low
     small = []
     for d in diagonals:
         small.extend([d[:128, :128], d[128:, 128:]])
@@ -210,21 +262,22 @@
         tl_ref[p] = low
 
 
-def factor(g):
+def factor(core, own, other):
     shapes = [(4, WIDE, WIDE)] * 2 + [(6, WIDE, WIDE)] * 2
     return pl.pallas_call(
         factor_kernel,
         out_shape=[jax.ShapeDtypeStruct(s, BF16) for s in shapes],
-        in_specs=[vmem()],
+        in_specs=[smem(), vmem(), vmem()],
         out_specs=[vmem()] * 4,
         compiler_params=params(),
         cost_estimate=pl.CostEstimate(flops=8 * 10**9, bytes_accessed=5 << 20, transcendentals=0),
         name="factor",
-    )(g)
+    )(core, own, other)
 
 
 def rows_of(ref, j):
-    return jnp.concatenate([ref[pl.ds(j * 4 + r, 64, stride=32), :] for r in range(4)], axis=0)
+    stride = ref.shape[0] // 64
+    return jnp.concatenate([ref[pl.ds(j * 4 + r, 64, stride=stride), :] for r in range(4)], axis=0)
 
 
 def project_kernel(core, e_ref, own_ref, other_ref, p_ref):
@@ -243,7 +296,7 @@
 def project(core, e, own, other):
     return pl.pallas_call(
         project_kernel,
-        out_shape=jax.ShapeDtypeStruct(e.shape, F32),
+        out_shape=jax.ShapeDtypeStruct((2048, 128), F32),
         in_specs=[smem(), vmem(), vmem(), vmem()],
         out_specs=vmem(),
         compiler_params=params(),
@@ -252,7 +305,11 @@
     )(core, e, own, other)
 
 
-def solve_kernel(p_ref, th_ref, tl_ref, sh_ref, sl_ref, w_ref):
+def solve_kernel(p_ref, th_hbm, tl_hbm, sh_hbm, sl_hbm, w_ref, th_ref, tl_ref, sh_ref, sl_ref, sems):
+    pairs = ((th_hbm, th_ref), (tl_hbm, tl_ref), (sh_hbm, sh_ref), (sl_hbm, sl_ref))
+    copies = [pltpu.make_async_copy(a, b, sems.at[i]) for i, (a, b) in enumerate(pairs)]
+    for copy in copies:
+        copy.start()
     total = p_ref[0]
     for s in range(1, p_ref.shape[0]):
         total = total + p_ref[s]
@@ -267,13 +324,14 @@
         product = dg(both, bh) + dg(both, bl)
         return product[:4] + product[4:]
 
-    others = [(i, j) for (i, j) in PAIRS if i != j]
+    for copy in copies:
+        copy.wait()
     pieces = [None] * 4
     for q in range(3, -1, -1):
         solved = times(rest[q], th_ref[q], tl_ref[q])
         pieces[q] = jnp.concatenate([solved[:, :128], solved[:, 128:]], axis=0)
         for p in range(q):
-            at = others.index((p, q))
+            at = UPPER.index((p, q))
             rest[p] = rest[p] - times(solved, sh_ref[at], sl_ref[at])
     result = jnp.concatenate(pieces, axis=0)
     w_ref[...] = jnp.broadcast_to(result[None], w_ref.shape)
@@ -283,8 +341,10 @@
     return pl.pallas_call(
         solve_kernel,
         out_shape=jax.ShapeDtypeStruct(p.shape, F32),
-        in_specs=[vmem()] * 5,
+        in_specs=[vmem()] + [hbm()] * 4,
         out_specs=vmem(),
+        scratch_shapes=[pltpu.VMEM((n, WIDE, WIDE), BF16) for n in (4, 4, 6, 6)]
+        + [pltpu.SemaphoreType.DMA((4,))],
         compiler_params=params(),
         cost_estimate=pl.CostEstimate(flops=10**9, bytes_accessed=4 << 20, transcendentals=0),
         name="solve",
@@ -300,14 +360,15 @@
             for h in range(2):
                 j = first + 2 * k + h
                 for r in range(4):
-                    at = pl.ds(j * 4 + r, 64, stride=32)
-                    o_ref[at, :] = e_ref[at, :] - change[r * 64 : (r + 1) * 64, h * 128 : (h + 1) * 128]
+                    before = e_ref[pl.ds(j * 4 + r, 64, stride=e_ref.shape[0] // 64), :]
+                    part = change[r * 64 : (r + 1) * 64, h * 128 : (h + 1) * 128]
+                    o_ref[pl.ds(j * 4 + r, 64, stride=32), :] = before - part
 
 
 def update(core, e, w, own, other):
     return pl.pallas_call(
         update_kernel,
-        out_shape=jax.ShapeDtypeStruct(e.shape, F32),
+        out_shape=jax.ShapeDtypeStruct((2048, 128), F32),
         in_specs=[smem(), vmem(), vmem(), vmem(), vmem()],
         out_specs=vmem(),
         compiler_params=params(),
@@ -320,23 +381,25 @@
     return lax.all_to_all(a, CHIPS, split_axis=0, concat_axis=0, tiled=True)
 
 
+def swap_cores(a):
+    return lax.ppermute(a, "c", [(0, 1), (1, 0)])
+
+
 def body(eigvecs, reflectors, offsets, lengths, panels):
     core = lax.axis_index("c").astype(jnp.int32).reshape(1)
-    other = lax.ppermute(panels, "c", [(0, 1), (1, 0)])
-    partial = gram(panels).reshape(128, 40, 128)
-    partial = lax.all_to_all(partial, AXES, split_axis=0, concat_axis=0, tiled=True)
-    share = jnp.sum(partial, axis=0)
-    whole = jnp.broadcast_to(share[None], (128, 40, 128))
-    whole = lax.all_to_all(whole, AXES, split_axis=0, concat_axis=0, tiled=True)
-    factors = factor(whole.reshape(5120, 128))
-
+    other = swap_cores(panels)
+    parts = to_chips(gram(core, panels, other).reshape(64, 40, 128))
     tiles = eigvecs.reshape(4, 512, 128).transpose(1, 0, 2)
     chased = chase(tiles, reflectors, offsets, lengths)
-    mine = to_chips(chased.reshape(64, 32, 128)).reshape(2048, 128)
+    sent = join(chased, parts.reshape(640, 4, 128))
+    mine = to_chips(sent.reshape(64, 72, 128))
+    half = mine[:, 32:].reshape(2560, 128)
+    factors = factor(core, half, swap_cores(half))
+    mine = mine.reshape(4608, 128)
     projected = to_chips(project(core, mine, panels, other).reshape(64, 32, 128))
     weights = to_chips(solve(projected, factors)).reshape(2048, 128)
     result = to_chips(update(core, mine, weights, panels, other).reshape(64, 32, 128))
-    return result.reshape(512, 4, 128).transpose(1, 0, 2).reshape(4, 65536)
+    return result.reshape(64, 8, 4, 128).transpose(2, 0, 1, 3).reshape(4, 65536)
 
 
 def solution(mesh):

time: 200 us -> 184 us (0.920)
  waiting for transfers between devices: 65.1 us -> 13.2 us
  blocking collectives: 45 us -> 87.2 us
  starting transfers between devices: 27.9 us -> 18.9 us
  local copies, waits for them, and re-layouts: 15.2 us -> 18.1 us
    all_to_all x2 -> x3, blocking collectives: 45 us -> 87.2 us  [to_chips(): return lax.all_to_all(a, CHIPS, split_axis=0, concat_axis=0, tiled=True)]
    all_to_all x2 -> x0, waiting for transfers between devices: 31.7 us -> none  [the longest x1 22.9 us: body(): whole = lax.all_to_all(whole, AXES, split_axis=0, concat_axis=0, tiled=True)]
    all_to_all x2, waiting for transfers between devices: 28.9 us -> 8.87 us  [to_chips(): return lax.all_to_all(a, CHIPS, split_axis=0, concat_axis=0, tiled=True)]
    all_to_all x2 -> x0, starting transfers between devices: 16.7 us -> none  [the longest x1 11.6 us: body(): lax.all_to_all(partial, AXES, split_axis=0, concat_axis=0, tiled=True)]
    all_to_all x2, starting transfers between devices: 11 us -> 18.9 us  [to_chips(): return lax.all_to_all(a, CHIPS, split_axis=0, concat_axis=0, tiled=True)]
    unnamed x31 -> x41, local copies, waits for them, and re-layouts: 13.4 us -> 16.9 us
    pallas_call x4 -> x5, Pallas kernels: 38.9 us -> 37.8 us  [the longest x1 24.8 us: chase(): pl.pallas_call(chase_kernel, out_shape=jax.ShapeDtypeStruct((64 * 18, 4,...]
    ppermute x1 -> x2, waiting for transfers between devices: 4.48 us -> 4.37 us  [swap_cores(): return lax.ppermute(a, 'c', [(0, 1), (1, 0)])]
  transfers between devices with their start and end apart: 5 -> 4, of which waited for: 5 -> 2; matrix products, arithmetic and copies ran while one was open for 1% -> 0% of each run, Pallas kernels for 17% -> 18%
where the time goes in v2:
time: 184 us; the launch traced here: 183 us
  blocking collectives  87.2 us (47%)
  Pallas kernels  45.2 us (25%)
  starting transfers between devices  18.9 us (10%)
  local copies, waits for them, and re-layouts  18.1 us (10%)
  waiting for transfers between devices  13.2 us (7%)
    all_to_all x3, blocking collectives, to_chips(): return lax.all_to_all(a, CHIPS, split_axis=0, concat_axis=0, tiled=True)  87.2 us
    pallas_call x1, Pallas kernels, chase(): pl.pallas_call(chase_kernel, out_shape=jax.ShapeDtypeStruct((64 * 18, 4,...  24.8 us
    all_to_all x2, starting transfers between devices, to_chips(): return lax.all_to_all(a, CHIPS, split_axis=0, concat_axis=0, tiled=True)  18.9 us
    unnamed x41, local copies, waits for them, and re-layouts  16.9 us
    all_to_all x2, waiting for transfers between devices, to_chips(): return lax.all_to_all(a, CHIPS, split_axis=0, concat_axis=0, tiled=True)  8.87 us
    pallas_call x1, Pallas kernels, factor(): pl.pallas_call(factor_kernel, out_shape=[jax.ShapeDtypeStruct(s, BF16) fo...  5.89 us
    ppermute x2, waiting for transfers between devices, swap_cores(): return lax.ppermute(a, 'c', [(0, 1), (1, 0)])  4.37 us
    pallas_call x1, Pallas kernels, join(): pl.pallas_call(join_kernel, out_shape=jax.ShapeDtypeStruct(chased.shape,...  3.87 us
  transfers between devices with their start and end apart: 4, of which 2 were waited for; matrix products, arithmetic and copies ran while one was open for 0% of the time, Pallas kernels for 18%

profile of v2, /device:TPU:0, one launch (start us, length us, event | category | flops | bytes accessed | tf_op | source)
XLA Modules:
  0.0 182.8 jit_solution(17381025304117231019)
XLA Ops:
  0.0 4.4 %collective-permute-done.other_ref = f32[512,1024]{1,0:T(8,128)S(1)} collective-permute-done((f32[512,1024]{1,0:T(8,128)}, f32[512,1024]{1,0:T(8,128)S(1)}, u32[]{:S(2)}, u32[]{:S(2)}) %collective-permute-start) | collective-permute-done | bytes 2097184 | tf_op jit(solution)/shard_map/ppermute | solution.py:385
  4.4 2.3 %copy-done.1 = f32[512,1024]{1,0:T(8,128)S(1)} copy-done((f32[512,1024]{1,0:T(8,128)S(1)}, f32[512,1024]{1,0:T(8,128)}, u32[]{:S(2)}) %copy-start.1) | copy-done | bytes 2097176
  6.7 3.5 %gram.1 = f32[2560,128]{1,0:T(8,128)} custom-call(s32[1]{0:T(128)} %bitcast.core, f32[512,1024]{1,0:T(8,128)S(1)} %copy-done.1, f32[512,1024]{1,0:T(8,128)S(1)} %collective-permute-done.other_ref), custom_call_target="tpu_custom_call" | custom-call | flops 2000000000 | bytes 5242880 | tf_op jit(solution)/shard_map/gram/pallas_call | solution.py:214
  10.2 11.9 %all-to-all-start = ((f32[64,40,128]{2,1,0:T(8,128)}), f32[64,40,128]{2,1,0:T(8,128)}, u32[]{:S(2)}, u32[]{:S(2)}) async-start(f32[64,40,128]{2,1,0:T(8,128)} %bitcast.3), calls=%async_computation | async-start | bytes 2621440 | tf_op jit(solution)/shard_map/all_to_all | solution.py:381
  22.1 0.0 copy-start.16
  22.1 1.9 %copy-done.16 = f32[24,256,128]{2,1,0:T(8,128)S(1)} copy-done((f32[24,256,128]{2,1,0:T(8,128)S(1)}, f32[24,256,128]{2,1,0:T(8,128)}, u32[]{:S(2)}) %copy-start.16) | copy-done | bytes 3145752
  24.0 24.8 %chase.1.e_ref = f32[1152,4,128]{2,1,0:T(4,128)S(1)} custom-call(s32[24]{0:T(128)S(1)} %copy-done.18, s32[24]{0:T(128)S(1)} %copy-done.19, f32[512,4,128]{2,1,0:T(4,128)S(1)} %bitcast.27, f32[24,256,128]{2,1,0:T(8,128)S(1)} %copy-done.16), custom_call_target="tpu_custom_call" | custom-call | flops 20000000000 | bytes 6291456 | tf_op jit(solution)/shard_map/chase/pallas_call | solution.py:166
  48.8 3.9 %join.1 = f32[1152,4,128]{2,1,0:T(4,128)S(1)} custom-call(f32[1152,4,128]{2,1,0:T(4,128)S(1)} %chase.1.e_ref, f32[640,4,128]{2,1,0:T(4,128)} %bitcast.4.g_ref), custom_call_target="tpu_custom_call", output_to_operand_aliasing={{}: (0, {})} | custom-call | flops 1000000 | bytes 3145728 | tf_op jit(solution)/shard_map/join/pallas_call | solution.py:179
  52.7 1.4 copy-done
  54.1 42.9 %all_to_all.25 = f32[64,72,128]{2,1,0:T(8,128)S(1)} all-to-all(f32[64,72,128]{2,1,0:T(8,128)} %bitcast.23), channel_id=1, replica_groups=mesh['yh'=2,'x'=4,'yl'=2,'z'=4,'c'=2] {'yh','x','yl','z'}, dimensions={0} | all-to-all | bytes 4718592 | tf_op jit(solution)/shard_map/all_to_all | solution.py:381
  97.0 1.2 slice.4
  98.2 0.9 copy-done.2
  99.1 2.4 %project.1 = f32[2048,128]{1,0:T(8,128)S(1)} custom-call(s32[1]{0:T(128)} %bitcast.core, f32[4608,128]{1,0:T(8,128)S(1)} %bitcast.21, f32[512,1024]{1,0:T(8,128)S(1)} %copy-done.2, f32[512,1024]{1,0:T(8,128)S(1)} %copy-done.5), custom_call_target="tpu_custom_call" | custom-call | flops 2000000000 | bytes 6291456 | tf_op jit(solution)/shard_map/project/pallas_call | solution.py:297
  101.6 0.0 copy-start.7
  101.6 1.0 copy-done.7
  102.5 7.0 %all-to-all-start.2 = ((f32[64,32,128]{2,1,0:T(8,128)}), f32[64,32,128]{2,1,0:T(8,128)S(1)}, u32[]{:S(2)}, u32[]{:S(2)}) async-start(f32[64,32,128]{2,1,0:T(8,128)} %bitcast.26), calls=%async_computation.2 | async-start | bytes 2097152 | tf_op jit(solution)/shard_map/all_to_all | solution.py:381
  109.5 5.9 %factor.1 = (bf16[4,256,256]{2,1,0:T(8,128)(2,1)S(1)}, bf16[4,256,256]{2,1,0:T(8,128)(2,1)S(1)}, bf16[6,256,256]{2,1,0:T(8,128)(2,1)S(1)}, bf16[6,256,256]{2,1,0:T(8,128)(2,1)S(1)}) custom-call(s32[1]{0:T(128)} %bitcast.core, f32[2560,128]{1,0:T(8,128)} %bitcast.8.own_ref, f32[2560,128]{1,0:T(8,128)} %collective-permute-done.1.other_ref), custom_call_target="tpu_custom_call" | custom-call | flops 8000000000 | bytes 5242880 | tf_op jit(solution)/shard_map/factor/pallas_call | solution.py:267
  115.4 0.9 copy-done.8
  116.3 0.9 copy-done.10
  117.2 0.8 copy-done.12
  118.0 0.8 copy-done.14
  118.8 8.9 %all-to-all-done.2.p_ref = f32[64,32,128]{2,1,0:T(8,128)S(1)} async-done(((f32[64,32,128]{2,1,0:T(8,128)}), f32[64,32,128]{2,1,0:T(8,128)S(1)}, u32[]{:S(2)}, u32[]{:S(2)}) %all-to-all-start.2) | async-done | bytes 1048608 | tf_op jit(solution)/shard_map/all_to_all | solution.py:381
  127.7 1.1 copy-done.9
  128.8 1.1 copy-done.11
  129.9 1.0 copy-done.13
  131.0 1.0 copy-done.15
  132.0 1.6 solve.1
  133.6 22.2 %all_to_all.26 = f32[64,32,128]{2,1,0:T(8,128)S(1)} all-to-all(f32[64,32,128]{2,1,0:T(8,128)S(1)} %solve.1), channel_id=1, replica_groups=mesh['yh'=2,'x'=4,'yl'=2,'z'=4,'c'=2] {'yh','x','yl','z'}, dimensions={0} | all-to-all | bytes 2097152 | tf_op jit(solution)/shard_map/all_to_all | solution.py:381
  155.8 3.2 %update.1 = f32[2048,128]{1,0:T(8,128)S(1)} custom-call(s32[1]{0:T(128)} %bitcast.core, f32[4608,128]{1,0:T(8,128)S(1)} %bitcast.22, f32[2048,128]{1,0:T(8,128)S(1)} %bitcast.24, f32[512,1024]{1,0:T(8,128)S(1)} %copy-done.3, f32[512,1024]{1,0:T(8,128)S(1)} %copy-done.6), custom_call_target="tpu_custom_call" | custom-call | flops 2000000000 | bytes 7340032 | tf_op jit(solution)/shard_map/update/pallas_call | solution.py:369
  159.0 22.0 %all_to_all.27 = f32[64,32,128]{2,1,0:T(8,128)S(1)} all-to-all(f32[64,32,128]{2,1,0:T(8,128)S(1)} %bitcast.25), channel_id=1, replica_groups=mesh['yh'=2,'x'=4,'yl'=2,'z'=4,'c'=2] {'yh','x','yl','z'}, dimensions={0} | all-to-all | bytes 2097152 | tf_op jit(solution)/shard_map/all_to_all | solution.py:381
  181.1 0.1 copy.12
  181.1 1.6 copy.11
  (29 shorter events, 0.1 us)
Async XLA Ops:
  0.0 4.4 %collective-permute-start = (f32[512,1024]{1,0:T(8,128)}, f32[512,1024]{1,0:T(8,128)S(1)}, u32[]{:S(2)}, u32[]{:S(2)}) collective-permute-start(f32[512,1024]{1,0:T(8,128)} %own_ref.5), channel_id=1, source_target_pairs={{0,1},{1,0},{2,3},{3,2},{4,5},{5,4},{6,7},{7,6},{8,9},{9,8},{10,11... | collective-permute-start | bytes 6291464 | tf_op jit(solution)/shard_map/ppermute | solution.py:385
  4.4 5.8 %copy-start.4 = (f32[512,1024]{1,0:T(8,128)}, f32[512,1024]{1,0:T(8,128)S(1)}, u32[]{:S(2)}) copy-start(f32[512,1024]{1,0:T(8,128)S(1)} %collective-permute-done.other_ref) | copy-start | bytes 6291460
  4.4 2.3 %copy-start.1 = (f32[512,1024]{1,0:T(8,128)S(1)}, f32[512,1024]{1,0:T(8,128)}, u32[]{:S(2)}) copy-start(f32[512,1024]{1,0:T(8,128)} %own_ref.5) | copy-start | bytes 6291460
  10.2 11.9 %copy-start.17 = (f32[4,65536]{1,0:T(4,128)S(1)}, f32[4,65536]{1,0:T(4,128)}, u32[]{:S(2)}) copy-start(f32[4,65536]{1,0:T(4,128)} %param.5) | copy-start | bytes 3145732
  10.2 11.9 %copy-start.18 = (s32[24]{0:T(128)S(1)}, s32[24]{0:T(128)}, u32[]{:S(2)}) copy-start(s32[24]{0:T(128)} %offsets.1) | copy-start | bytes 292
  10.2 11.9 %copy-start.19 = (s32[24]{0:T(128)S(1)}, s32[24]{0:T(128)}, u32[]{:S(2)}) copy-start(s32[24]{0:T(128)} %lengths.1) | copy-start | bytes 292
  10.2 38.6 %all-to-all-start = ((f32[64,40,128]{2,1,0:T(8,128)}), f32[64,40,128]{2,1,0:T(8,128)}, u32[]{:S(2)}, u32[]{:S(2)}) async-start(f32[64,40,128]{2,1,0:T(8,128)} %bitcast.3), calls=%async_computation | async-start | bytes 2621440 | tf_op jit(solution)/shard_map/all_to_all | solution.py:381
  22.1 1.9 %copy-start.16 = (f32[24,256,128]{2,1,0:T(8,128)S(1)}, f32[24,256,128]{2,1,0:T(8,128)}, u32[]{:S(2)}) copy-start(f32[24,256,128]{2,1,0:T(8,128)} %m_ref.1) | copy-start | bytes 9437188
  52.7 1.4 copy-start
  54.1 44.1 %copy-start.5 = (f32[512,1024]{1,0:T(8,128)S(1)}, f32[512,1024]{1,0:T(8,128)}, u32[]{:S(2)}) copy-start(f32[512,1024]{1,0:T(8,128)} %copy-done.4) | copy-start | bytes 6291460
  97.0 2.1 %copy-start.2 = (f32[512,1024]{1,0:T(8,128)S(1)}, f32[512,1024]{1,0:T(8,128)}, u32[]{:S(2)}) copy-start(f32[512,1024]{1,0:T(8,128)} %own_ref.5) | copy-start | bytes 6291460
  98.2 11.3 %collective-permute-start.1 = (f32[2560,128]{1,0:T(8,128)}, f32[2560,128]{1,0:T(8,128)}, u32[]{:S(2)}, u32[]{:S(2)}) collective-permute-start(f32[2560,128]{1,0:T(8,128)} %bitcast.8.own_ref), channel_id=1, source_target_pairs={{0,1},{1,0},{2,3},{3,2},{4,5},{5,4},{6,7},{7,6},{8,9},{9,8},{10,11... | collective-permute-start | bytes 3932168 | tf_op jit(solution)/shard_map/ppermute | solution.py:385
  101.6 1.0 copy-start.7
  102.5 25.2 %all-to-all-start.2 = ((f32[64,32,128]{2,1,0:T(8,128)}), f32[64,32,128]{2,1,0:T(8,128)S(1)}, u32[]{:S(2)}, u32[]{:S(2)}) async-start(f32[64,32,128]{2,1,0:T(8,128)} %bitcast.26), calls=%async_computation.2 | async-start | bytes 2097152 | tf_op jit(solution)/shard_map/all_to_all | solution.py:381
  115.4 0.9 copy-start.8
  116.3 0.9 copy-start.10
  117.2 0.8 copy-start.12
  118.0 0.8 copy-start.14
  127.7 1.1 copy-start.9
  128.8 1.1 copy-start.11
  129.9 1.0 copy-start.13
  131.0 1.0 copy-start.15
  132.0 23.8 %copy-start.6 = (f32[512,1024]{1,0:T(8,128)S(1)}, f32[512,1024]{1,0:T(8,128)}, u32[]{:S(2)}) copy-start(f32[512,1024]{1,0:T(8,128)} %copy-done.4) | copy-start | bytes 6291460
  133.6 22.2 %copy-start.3 = (f32[512,1024]{1,0:T(8,128)S(1)}, f32[512,1024]{1,0:T(8,128)}, u32[]{:S(2)}) copy-start(f32[512,1024]{1,0:T(8,128)} %own_ref.5) | copy-start | bytes 6291460

commit v3 on v2

--- a/solution.py
+++ b/solution.py
@@ -10,6 +10,7 @@
 AXES = ("yh", "x", "yl", "z", "c")
 CHIPS = ("yh", "x", "yl", "z")
 VMEM_LIMIT = 20 * 1024 * 1024
+LARGE = 58 * 1024 * 1024
 
 NN = (((1,), (0,)), ((), ()))
 NT = (((1,), (1,)), ((), ()))
@@ -72,41 +73,44 @@
 TOGETHER = 4
 
 
-def place(tile):
-    return (tile // 8) * 18 + tile % 8
-
-
-def chase_kernel(offsets, lengths, e_ref, m_ref, o_ref, kh_ref, kl_ref):
-    blocks, extent, width = m_ref.shape
+def masked_block(lengths, m_ref, b):
+    row = lax.broadcasted_iota(jnp.int32, m_ref.shape[1:], 0)
+    return split(jnp.where(row < lengths[b], m_ref[b], 0.0))
+
+
+def invert_kernel(lengths, m_ref, fh_ref, fl_ref):
+    def group_of(group, carry):
+        blocks = [group * TOGETHER + u for u in range(TOGETHER)]
+        masked = [masked_block(lengths, m_ref, b) for b in blocks]
+        grams = [dot3(m, m, TN) for m in masked]
+        for b, f in zip(blocks, inverse_of_half(grams)):
+            fh_ref[b], fl_ref[b] = split(f)
+        return carry
+
+    lax.fori_loop(0, m_ref.shape[0] // TOGETHER, group_of, 0)
+
+
+def chase_kernel(offsets, lengths, e_ref, m_ref, fh_ref, fl_ref, o_ref, kh_ref, kl_ref):
+    blocks = m_ref.shape[0]
     tiles, rows = e_ref.shape[0], e_ref.shape[1]
-    for s in range(tiles // 8):
-        o_ref[s * 18 : s * 18 + 8] = e_ref[s * 8 : s * 8 + 8]
-    row = lax.broadcasted_iota(jnp.int32, (extent, width), 0)
-
-    def prepare(group, carry):
-        masked = []
-        for u in range(TOGETHER):
-            b = group * TOGETHER + u
-            masked.append(split(jnp.where(row < lengths[b], m_ref[b], 0.0)))
-        grams = [dot3(m, m, TN) for m in masked]
-        factors = [split(f) for f in inverse_of_half(grams)]
-        lefts = [split(dot3(m, f, NT)) for m, f in zip(masked, factors)]
-        for u in range(TOGETHER):
-            high, low = split(dot3(lefts[u], masked[u], NT))
-            b = group * TOGETHER + u
-            kh_ref[b] = high
-            kl_ref[b] = low
+    o_ref[...] = e_ref[...]
+
+    def group_of(group, carry):
+        at = [group * TOGETHER + u for u in range(TOGETHER)]
+        masked = [masked_block(lengths, m_ref, b) for b in at]
+        lefts = [split(dot3(m, (fh_ref[b], fl_ref[b]), NT)) for m, b in zip(masked, at)]
+        for left, m, b in zip(lefts, masked, at):
+            kh_ref[b], kl_ref[b] = split(dot3(left, m, NT))
         return carry
 
-    lax.fori_loop(0, blocks // TOGETHER, prepare, 0)
+    lax.fori_loop(0, blocks // TOGETHER, group_of, 0)
     lane = lax.broadcasted_iota(jnp.int32, (rows, 128), 1)
 
     def step(b, carry):
         offset = offsets[b]
         tile = jnp.minimum(offset // 128, tiles - 3)
         shift = offset - tile * 128
-        at = [place(tile + k) for k in range(3)]
-        v0, v1, v2 = [o_ref[k] for k in at]
+        v0, v1, v2 = o_ref[tile], o_ref[tile + 1], o_ref[tile + 2]
         left = (128 - shift) & 127
         r0 = pltpu.roll(v0, left, 1)
         r1 = pltpu.roll(v1, left, 1)
@@ -121,28 +125,20 @@
         q0 = pltpu.roll(change[:, :128], right, 1)
         q1 = pltpu.roll(change[:, 128:], right, 1)
         after = lane >= shift
-        o_ref[at[0]] = v0 - jnp.where(after, q0, 0.0)
-        o_ref[at[1]] = v1 - jnp.where(after, q1, q0)
-        o_ref[at[2]] = v2 - jnp.where(after, 0.0, q1)
+        o_ref[tile] = v0 - jnp.where(after, q0, 0.0)
+        o_ref[tile + 1] = v1 - jnp.where(after, q1, q0)
+        o_ref[tile + 2] = v2 - jnp.where(after, 0.0, q1)
         return carry
 
     lax.fori_loop(0, blocks, step, 0)
 
 
-def join_kernel(e_ref, g_ref, o_ref, share_ref, sems):
-    chips = o_ref.shape[0] // 18
-    share = g_ref[0:10]
-    for s in range(1, chips):
-        share = share + g_ref[s * 10 : s * 10 + 10]
-    share_ref[...] = share
-    copies = [
-        pltpu.make_async_copy(share_ref, o_ref.at[pl.ds(s * 18 + 8, 10)], sems.at[s])
-        for s in range(chips)
-    ]
-    for copy in copies:
-        copy.start()
-    for copy in copies:
-        copy.wait()
+def share_kernel(g_ref, o_ref):
+    sums = [g_ref[k] for k in range(4)]
+    for s in range(4, g_ref.shape[0]):
+        sums[s % 4] = sums[s % 4] + g_ref[s]
+    total = (sums[0] + sums[1]) + (sums[2] + sums[3])
+    o_ref[...] = jnp.broadcast_to(total[None], o_ref.shape)
 
 
 def vmem():
@@ -161,32 +157,44 @@
     return pl.BlockSpec(memory_space=pltpu.HBM)
 
 
-def chase(tiles, reflectors, offsets, lengths):
+def invert(reflectors, lengths):
     blocks, extent, width = reflectors.shape
+    shape = jax.ShapeDtypeStruct((blocks, width, width), BF16)
+    return pl.pallas_call(
+        invert_kernel,
+        out_shape=[shape, shape],
+        in_specs=[smem(), vmem()],
+        out_specs=[vmem()] * 2,
+        compiler_params=params(),
+        cost_estimate=pl.CostEstimate(flops=10 * 10**9, bytes_accessed=5 << 20, transcendentals=0),
+        name="invert",
+    )(lengths, reflectors)
+
+
+def chase(tiles, reflectors, offsets, lengths, fh, fl):
+    blocks, extent, width = reflectors.shape
     return pl.pallas_call(
         chase_kernel,
-        out_shape=jax.ShapeDtypeStruct((64 * 18, 4, 128), F32),
-        in_specs=[smem(), smem(), vmem(), vmem()],
+        out_shape=jax.ShapeDtypeStruct(tiles.shape, F32),
+        in_specs=[smem(), smem()] + [vmem()] * 4,
         out_specs=vmem(),
         scratch_shapes=[pltpu.VMEM((blocks, extent, extent), BF16)] * 2,
         compiler_params=params(),
-        cost_estimate=pl.CostEstimate(flops=20 * 10**9, bytes_accessed=6 << 20, transcendentals=0),
+        cost_estimate=pl.CostEstimate(flops=10 * 10**9, bytes_accessed=7 << 20, transcendentals=0),
         name="chase",
-    )(offsets, lengths, tiles, reflectors)
-
-
-def join(chased, parts):
-    return pl.pallas_call(
-        join_kernel,
-        out_shape=jax.ShapeDtypeStruct(chased.shape, F32),
-        in_specs=[hbm(), vmem()],
-        out_specs=hbm(),
-        scratch_shapes=[pltpu.VMEM((10, 4, 128), F32), pltpu.SemaphoreType.DMA((64,))],
-        input_output_aliases={0: 0},
+    )(offsets, lengths, tiles, reflectors, fh, fl)
+
+
+def share(parts):
+    return pl.pallas_call(
+        share_kernel,
+        out_shape=jax.ShapeDtypeStruct(parts.shape, F32),
+        in_specs=[vmem()],
+        out_specs=vmem(),
         compiler_params=params(),
         cost_estimate=pl.CostEstimate(flops=10**6, bytes_accessed=3 << 20, transcendentals=0),
-        name="join",
-    )(chased, parts)
+        name="share",
+    )(parts)
 
 
 WIDE = 256
@@ -196,30 +204,29 @@
 UPPER = [(i, j) for i in range(4) for j in range(i + 1, 4)]
 
 
-def gram_kernel(core, own_ref, other_ref, g_ref):
+def gram_kernel(core, v_ref, *refs):
     c = core[0]
+    g_ref = refs[-1]
     order = (2 * c, 1 - c, 2 + c, 3 - 2 * c)
-    blocks = [None] * len(LOCAL)
-    for ref in (own_ref, other_ref):
-        halves = [split(ref[:, pl.ds(pl.multiple_of(o * WIDE, WIDE), WIDE)]) for o in order]
-        for at, (i, j) in enumerate(LOCAL):
-            block = dot3(halves[i], halves[j], TN)
-            blocks[at] = block if blocks[at] is None else blocks[at] + block
-    for at, block in enumerate(blocks):
+    halves = [split(v_ref[:, pl.ds(pl.multiple_of(o * WIDE, WIDE), WIDE)]) for o in order]
+    for at, (i, j) in enumerate(LOCAL):
+        block = dot3(halves[i], halves[j], TN)
         for h in range(2):
-            g_ref[pl.ds((at * 2 + h) * WIDE, WIDE), :] = block[:, h * 128 : (h + 1) * 128]
-
-
-def gram(core, own, other):
+            rows = pl.ds((at * 2 + h) * WIDE, WIDE)
+            part = block[:, h * 128 : (h + 1) * 128]
+            g_ref[rows, :] = part + refs[0][rows, :] if len(refs) == 2 else part
+
+
+def gram(core, panels, *before):
     return pl.pallas_call(
         gram_kernel,
         out_shape=jax.ShapeDtypeStruct((len(LOCAL) * 2 * WIDE, 128), F32),
-        in_specs=[smem(), vmem(), vmem()],
-        out_specs=vmem(),
-        compiler_params=params(),
-        cost_estimate=pl.CostEstimate(flops=2 * 10**9, bytes_accessed=5 << 20, transcendentals=0),
+        in_specs=[smem(), vmem()] + [vmem()] * len(before),
+        out_specs=vmem(),
+        compiler_params=params(),
+        cost_estimate=pl.CostEstimate(flops=10**9, bytes_accessed=4 << 20, transcendentals=0),
         name="gram",
-    )(core, own, other)
+    )(core, panels, *before)
 
 
 def factor_kernel(core, own_ref, other_ref, th_ref, tl_ref, sh_ref, sl_ref):
@@ -280,26 +287,41 @@
     return jnp.concatenate([ref[pl.ds(j * 4 + r, 64, stride=stride), :] for r in range(4)], axis=0)
 
 
-def project_kernel(core, e_ref, own_ref, other_ref, p_ref):
+def project_kernel(core, e_ref, own_hbm, other_hbm, p_ref, v_ref, sems):
     c = core[0]
-    total = [jnp.zeros((256, WIDE), F32) for _ in range(4)]
-    for v_ref, first in ((own_ref, 4 * c), (other_ref, 4 - 4 * c)):
-        left = split(jnp.concatenate([rows_of(e_ref, first + k) for k in range(4)], axis=1))
-        for n in range(4):
-            total[n] += dot3(left, split(v_ref[:, n * WIDE : (n + 1) * WIDE]))
-    for n in range(8):
-        block = total[n // 2][:, (n % 2) * 128 : (n % 2) * 128 + 128]
-        for r in range(4):
-            p_ref[pl.ds(n * 4 + r, 64, stride=32), :] = block[r * 64 : (r + 1) * 64]
+    copies = []
+    for n in range(4):
+        columns = pl.ds(n * WIDE, WIDE)
+        for side, ref in enumerate((own_hbm, other_hbm)):
+            copy = pltpu.make_async_copy(ref.at[:, columns], v_ref.at[side, :, columns], sems.at[side, n])
+            copy.start()
+            copies.append(copy)
+    lefts = [
+        split(jnp.concatenate([rows_of(e_ref, first + k) for k in range(4)], axis=1))
+        for first in (4 * c, 4 - 4 * c)
+    ]
+    for n in range(4):
+        columns = pl.ds(n * WIDE, WIDE)
+        total = None
+        for side in range(2):
+            copies[2 * n + side].wait()
+            part = dot3(lefts[side], split(v_ref[side, :, columns]))
+            total = part if total is None else total + part
+        for h in range(2):
+            for r in range(4):
+                p_ref[pl.ds((2 * n + h) * 4 + r, 64, stride=32), :] = total[
+                    r * 64 : (r + 1) * 64, h * 128 : (h + 1) * 128
+                ]
 
 
 def project(core, e, own, other):
     return pl.pallas_call(
         project_kernel,
         out_shape=jax.ShapeDtypeStruct((2048, 128), F32),
-        in_specs=[smem(), vmem(), vmem(), vmem()],
-        out_specs=vmem(),
-        compiler_params=params(),
+        in_specs=[smem(), vmem(), hbm(), hbm()],
+        out_specs=vmem(),
+        scratch_shapes=[pltpu.VMEM((2,) + own.shape, F32), pltpu.SemaphoreType.DMA((2, 4))],
+        compiler_params=pltpu.CompilerParams(vmem_limit_bytes=LARGE),
         cost_estimate=pl.CostEstimate(flops=2 * 10**9, bytes_accessed=6 << 20, transcendentals=0),
         name="project",
     )(core, e, own, other)
@@ -345,7 +367,7 @@
         out_specs=vmem(),
         scratch_shapes=[pltpu.VMEM((n, WIDE, WIDE), BF16) for n in (4, 4, 6, 6)]
         + [pltpu.SemaphoreType.DMA((4,))],
-        compiler_params=params(),
+        compiler_params=pltpu.CompilerParams(vmem_limit_bytes=LARGE),
         cost_estimate=pl.CostEstimate(flops=10**9, bytes_accessed=4 << 20, transcendentals=0),
         name="solve",
     )(p, *factors)
@@ -388,16 +410,19 @@
 def body(eigvecs, reflectors, offsets, lengths, panels):
     core = lax.axis_index("c").astype(jnp.int32).reshape(1)
     other = swap_cores(panels)
-    parts = to_chips(gram(core, panels, other).reshape(64, 40, 128))
+    parts = to_chips(gram(core, other, gram(core, panels)).reshape(64, 40, 128))
+    factors = invert(reflectors, lengths)
+    copies = share(parts)
+    copies, factors = lax.optimization_barrier((copies, factors))
+    half = to_chips(copies).reshape(2560, 128)
     tiles = eigvecs.reshape(4, 512, 128).transpose(1, 0, 2)
-    chased = chase(tiles, reflectors, offsets, lengths)
-    sent = join(chased, parts.reshape(640, 4, 128))
-    mine = to_chips(sent.reshape(64, 72, 128))
-    half = mine[:, 32:].reshape(2560, 128)
-    factors = factor(core, half, swap_cores(half))
-    mine = mine.reshape(4608, 128)
+    chased = chase(tiles, reflectors, offsets, lengths, *factors)
+    chased, half = lax.optimization_barrier((chased, half))
+    mine = to_chips(chased.reshape(64, 32, 128)).reshape(2048, 128)
+    solvers = factor(core, half, swap_cores(half))
+    mine, solvers = lax.optimization_barrier((mine, solvers))
     projected = to_chips(project(core, mine, panels, other).reshape(64, 32, 128))
-    weights = to_chips(solve(projected, factors)).reshape(2048, 128)
+    weights = to_chips(solve(projected, solvers)).reshape(2048, 128)
     result = to_chips(update(core, mine, weights, panels, other).reshape(64, 32, 128))
     return result.reshape(64, 8, 4, 128).transpose(2, 0, 1, 3).reshape(4, 65536)
 

time: 184 us -> 182 us (0.989)
  blocking collectives: 87.2 us -> 68.1 us
  Pallas kernels: 45.2 us -> 54.1 us
  waiting for transfers between devices: 13.2 us -> 21.9 us
  local copies, waits for them, and re-layouts: 18.1 us -> 12.6 us
  starting transfers between devices: 18.9 us -> 23.9 us
    all_to_all x3, blocking collectives: 87.2 us -> 68.1 us  [to_chips(): return lax.all_to_all(a, CHIPS, split_axis=0, concat_axis=0, tiled=True)]
    all_to_all x2 -> x3, waiting for transfers between devices: 8.87 us -> 20.4 us  [to_chips(): return lax.all_to_all(a, CHIPS, split_axis=0, concat_axis=0, tiled=True)]
    pallas_call x1, Pallas kernels: 2.43 us -> 8 us  [project(): pl.pallas_call(project_kernel, out_shape=jax.ShapeDtypeStruct((2048, 128)...]
    all_to_all x2 -> x3, starting transfers between devices: 18.9 us -> 23.9 us  [to_chips(): return lax.all_to_all(a, CHIPS, split_axis=0, concat_axis=0, tiled=True)]
    unnamed x41 -> x35, local copies, waits for them, and re-layouts: 16.9 us -> 12.5 us
    pallas_call x1, Pallas kernels: 1.55 us -> 5.32 us  [solve(): pl.pallas_call(solve_kernel, out_shape=jax.ShapeDtypeStruct(p.shape, F32)...]
    ppermute x2, waiting for transfers between devices: 4.37 us -> 1.49 us  [swap_cores(): return lax.ppermute(a, 'c', [(0, 1), (1, 0)])]
    pallas_call x2 -> x3, Pallas kernels: 28.7 us -> 27.9 us  [the longest x1 13.4 us: invert(): pl.pallas_call(invert_kernel, out_shape=[shape, shape], in_specs=[smem(),...]
  transfers between devices with their start and end apart: 4 -> 5, of which waited for: 2 -> 4; matrix products, arithmetic and copies ran while one was open for 0% -> 0% of each run, Pallas kernels for 18% -> 19%
where the time goes in v3:
time: 182 us; the launch traced here: 181 us
  blocking collectives  68.1 us (37%)
  Pallas kernels  54.1 us (30%)
  starting transfers between devices  23.9 us (13%)
  waiting for transfers between devices  21.9 us (12%)
  local copies, waits for them, and re-layouts  12.6 us (7%)
    all_to_all x3, blocking collectives, to_chips(): return lax.all_to_all(a, CHIPS, split_axis=0, concat_axis=0, tiled=True)  68.1 us
    all_to_all x3, starting transfers between devices, to_chips(): return lax.all_to_all(a, CHIPS, split_axis=0, concat_axis=0, tiled=True)  23.9 us
    all_to_all x3, waiting for transfers between devices, to_chips(): return lax.all_to_all(a, CHIPS, split_axis=0, concat_axis=0, tiled=True)  20.4 us
    pallas_call x1, Pallas kernels, invert(): pl.pallas_call(invert_kernel, out_shape=[shape, shape], in_specs=[smem(),...  13.4 us
    pallas_call x1, Pallas kernels, chase(): pl.pallas_call(chase_kernel, out_shape=jax.ShapeDtypeStruct(tiles.shape,...  13.2 us
    unnamed x35, local copies, waits for them, and re-layouts  12.5 us
    pallas_call x1, Pallas kernels, project(): pl.pallas_call(project_kernel, out_shape=jax.ShapeDtypeStruct((2048, 128)...  8 us
    pallas_call x1, Pallas kernels, factor(): pl.pallas_call(factor_kernel, out_shape=[jax.ShapeDtypeStruct(s, BF16) fo...  5.54 us
  transfers between devices with their start and end apart: 5, of which 4 were waited for; matrix products, arithmetic and copies ran while one was open for 0% of the time, Pallas kernels for 19%

profile of v3, /device:TPU:0, one launch (start us, length us, event | category | flops | bytes accessed | tf_op | source)
XLA Modules:
  0.0 180.8 jit_solution(1473644711774100924)
XLA Ops:
  0.0 1.6 copy-done.10
  1.6 1.3 gram.2.refs_0_
  2.9 1.5 collective-permute-done.v_ref.other_hbm.other_ref
  4.4 2.4 %gram.3 = f32[2560,128]{1,0:T(8,128)} custom-call(s32[1]{0:T(128)} %bitcast.core, f32[512,1024]{1,0:T(8,128)S(1)} %collective-permute-done.v_ref.other_hbm.other_ref, f32[2560,128]{1,0:T(8,128)S(1)} %gram.2.refs_0_), custom_call_target="tpu_custom_call" | custom-call | flops 1000000000 | bytes 4194304 | tf_op jit(solution)/shard_map/gram/pallas_call | solution.py:221
  6.8 11.6 %all-to-all-start = ((f32[64,40,128]{2,1,0:T(8,128)}), f32[64,40,128]{2,1,0:T(8,128)S(1)}, u32[]{:S(2)}, u32[]{:S(2)}) async-start(f32[64,40,128]{2,1,0:T(8,128)} %bitcast.3), calls=%async_computation | async-start | bytes 2621440 | tf_op jit(solution)/shard_map/all_to_all | solution.py:403
  18.4 0.0 copy-start.8
  18.4 1.9 %copy-done.8 = f32[24,256,128]{2,1,0:T(8,128)S(1)} copy-done((f32[24,256,128]{2,1,0:T(8,128)S(1)}, f32[24,256,128]{2,1,0:T(8,128)}, u32[]{:S(2)}) %copy-start.8) | copy-done | bytes 3145752
  20.3 13.4 %invert.1 = (bf16[24,128,128]{2,1,0:T(8,128)(2,1)S(1)}, bf16[24,128,128]{2,1,0:T(8,128)(2,1)S(1)}) custom-call(s32[24]{0:T(128)S(1)} %copy-done.14, f32[24,256,128]{2,1,0:T(8,128)S(1)} %copy-done.8), custom_call_target="tpu_custom_call" | custom-call | flops 10000000000 | bytes 5242880 | tf_op jit(solution)/shard_map/invert/pallas_call | solution.py:163
  33.8 0.0 copy-start.15
  33.8 6.2 %all-to-all-done.g_ref = f32[64,40,128]{2,1,0:T(8,128)S(1)} async-done(((f32[64,40,128]{2,1,0:T(8,128)}), f32[64,40,128]{2,1,0:T(8,128)S(1)}, u32[]{:S(2)}, u32[]{:S(2)}) %all-to-all-start) | async-done | bytes 1310752 | tf_op jit(solution)/shard_map/all_to_all | solution.py:403
  39.9 1.2 share.1
  41.1 5.9 %all-to-all-start.1 = ((f32[64,40,128]{2,1,0:T(8,128)}), f32[64,40,128]{2,1,0:T(8,128)S(1)}, u32[]{:S(2)}, u32[]{:S(2)}) async-start(f32[64,40,128]{2,1,0:T(8,128)} %share.1), calls=%async_computation.1 | async-start | bytes 2621440 | tf_op jit(solution)/shard_map/all_to_all | solution.py:403
  47.1 1.9 %copy-done.9 = f32[24,256,128]{2,1,0:T(8,128)S(1)} copy-done((f32[24,256,128]{2,1,0:T(8,128)S(1)}, f32[24,256,128]{2,1,0:T(8,128)}, u32[]{:S(2)}) %copy-start.9) | copy-done | bytes 3145752
  49.0 1.1 copy-done.16
  50.1 13.2 %chase.1 = f32[512,4,128]{2,1,0:T(4,128)} custom-call(s32[24]{0:T(128)S(1)} %copy-done.13, s32[24]{0:T(128)S(1)} %copy-done.14, f32[512,4,128]{2,1,0:T(4,128)S(1)} %bitcast.26, f32[24,256,128]{2,1,0:T(8,128)S(1)} %copy-done.9, bf16[24,128,128]{2,1,0:T(8,128)(2,1)S(1)} %get-tuple-element.23.fh_ref, bf16[24,128,128]{2,1,0:T(8,128)(2,1)S(1)} %copy-done.16), custom_call_target="tpu_custom_call" | custom-call | flops 10000000000 | bytes 7340032 | tf_op jit(solution)/shard_map/chase/pallas_call | solution.py:176
  63.4 4.3 %all-to-all-done.1 = f32[64,40,128]{2,1,0:T(8,128)S(1)} async-done(((f32[64,40,128]{2,1,0:T(8,128)}), f32[64,40,128]{2,1,0:T(8,128)S(1)}, u32[]{:S(2)}, u32[]{:S(2)}) %all-to-all-start.1) | async-done | bytes 1310752 | tf_op jit(solution)/shard_map/all_to_all | solution.py:403
  67.6 6.4 %all-to-all-start.2 = ((f32[64,32,128]{2,1,0:T(8,128)}), f32[64,32,128]{2,1,0:T(8,128)S(1)}, u32[]{:S(2)}, u32[]{:S(2)}) async-start(f32[64,32,128]{2,1,0:T(8,128)} %bitcast.5), calls=%async_computation.2 | async-start | bytes 2097152 | tf_op jit(solution)/shard_map/all_to_all | solution.py:403
  74.0 5.5 %factor.1 = (bf16[4,256,256]{2,1,0:T(8,128)(2,1)S(1)}, bf16[4,256,256]{2,1,0:T(8,128)(2,1)S(1)}, bf16[6,256,256]{2,1,0:T(8,128)(2,1)S(1)}, bf16[6,256,256]{2,1,0:T(8,128)(2,1)S(1)}) custom-call(s32[1]{0:T(128)} %bitcast.core, f32[2560,128]{1,0:T(8,128)S(1)} %bitcast.21, f32[2560,128]{1,0:T(8,128)} %collective-permute-done.1.other_ref), custom_call_target="tpu_custom_call" | custom-call | flops 8000000000 | bytes 5242880 | tf_op jit(solution)/shard_map/factor/pallas_call | solution.py:274
  79.5 0.9 copy-done.4
  80.4 0.9 copy-done.5
  81.3 0.8 copy-done.6
  82.1 0.8 copy-done.7
  82.9 10.0 %all-to-all-done.2 = f32[64,32,128]{2,1,0:T(8,128)S(1)} async-done(((f32[64,32,128]{2,1,0:T(8,128)}), f32[64,32,128]{2,1,0:T(8,128)S(1)}, u32[]{:S(2)}, u32[]{:S(2)}) %all-to-all-start.2) | async-done | bytes 1048608 | tf_op jit(solution)/shard_map/all_to_all | solution.py:403
  92.9 1.0 copy-done.2
  93.9 8.0 %project.1 = f32[2048,128]{1,0:T(8,128)} custom-call(s32[1]{0:T(128)} %bitcast.core, f32[2048,128]{1,0:T(8,128)} %bitcast.22, f32[512,1024]{1,0:T(8,128)} %own_ref.1, f32[512,1024]{1,0:T(8,128)} %copy-done), custom_call_target="tpu_custom_call" | custom-call | flops 2000000000 | bytes 6291456 | tf_op jit(solution)/shard_map/project/pallas_call | solution.py:318
  101.9 23.8 %all_to_all.30.p_ref = f32[64,32,128]{2,1,0:T(8,128)} all-to-all(f32[64,32,128]{2,1,0:T(8,128)} %bitcast.29), channel_id=1, replica_groups=mesh['yh'=2,'x'=4,'yl'=2,'z'=4,'c'=2] {'yh','x','yl','z'}, dimensions={0} | all-to-all | bytes 2097152 | tf_op jit(solution)/shard_map/all_to_all | solution.py:403
  125.7 5.3 %solve.1 = f32[64,32,128]{2,1,0:T(8,128)} custom-call(f32[64,32,128]{2,1,0:T(8,128)} %all_to_all.30.p_ref, bf16[4,256,256]{2,1,0:T(8,128)(2,1)} %copy-done.6, bf16[4,256,256]{2,1,0:T(8,128)(2,1)} %copy-done.7, bf16[6,256,256]{2,1,0:T(8,128)(2,1)} %copy-done.4, bf16[6,256,256]{2,1,0:T(8,128)(2,1)} %copy-done.5), custom_call_target="tpu_custom_call" | custom-call | flops 1000000000 | bytes 4194304 | tf_op jit(solution)/shard_map/solve/pallas_call | solution.py:363
  131.1 22.4 %all_to_all.31 = f32[64,32,128]{2,1,0:T(8,128)S(1)} all-to-all(f32[64,32,128]{2,1,0:T(8,128)} %solve.1), channel_id=1, replica_groups=mesh['yh'=2,'x'=4,'yl'=2,'z'=4,'c'=2] {'yh','x','yl','z'}, dimensions={0} | all-to-all | bytes 2097152 | tf_op jit(solution)/shard_map/all_to_all | solution.py:403
  153.5 3.7 %update.1 = f32[2048,128]{1,0:T(8,128)S(1)} custom-call(s32[1]{0:T(128)} %bitcast.core, f32[2048,128]{1,0:T(8,128)S(1)} %bitcast.23, f32[2048,128]{1,0:T(8,128)S(1)} %bitcast.24, f32[512,1024]{1,0:T(8,128)S(1)} %copy-done.11, f32[512,1024]{1,0:T(8,128)S(1)} %copy-done.1), custom_call_target="tpu_custom_call" | custom-call | flops 2000000000 | bytes 7340032 | tf_op jit(solution)/shard_map/update/pallas_call | solution.py:391
  157.1 22.0 %all_to_all.32 = f32[64,32,128]{2,1,0:T(8,128)S(1)} all-to-all(f32[64,32,128]{2,1,0:T(8,128)S(1)} %bitcast.25), channel_id=1, replica_groups=mesh['yh'=2,'x'=4,'yl'=2,'z'=4,'c'=2] {'yh','x','yl','z'}, dimensions={0} | all-to-all | bytes 2097152 | tf_op jit(solution)/shard_map/all_to_all | solution.py:403
  179.1 0.1 copy.11
  179.2 1.6 copy.10
  (26 shorter events, 0.1 us)
Async XLA Ops:
  0.0 4.4 %collective-permute-start = (f32[512,1024]{1,0:T(8,128)}, f32[512,1024]{1,0:T(8,128)S(1)}, u32[]{:S(2)}, u32[]{:S(2)}) collective-permute-start(f32[512,1024]{1,0:T(8,128)} %own_ref.1), channel_id=1, source_target_pairs={{0,1},{1,0},{2,3},{3,2},{4,5},{5,4},{6,7},{7,6},{8,9},{9,8},{10,11... | collective-permute-start | bytes 6291464 | tf_op jit(solution)/shard_map/ppermute | solution.py:407
  0.0 1.6 copy-start.10
  4.4 2.4 %copy-start = (f32[512,1024]{1,0:T(8,128)}, f32[512,1024]{1,0:T(8,128)S(1)}, u32[]{:S(2)}) copy-start(f32[512,1024]{1,0:T(8,128)S(1)} %collective-permute-done.v_ref.other_hbm.other_ref) | copy-start | bytes 6291460
  6.8 11.6 %copy-start.14 = (s32[24]{0:T(128)S(1)}, s32[24]{0:T(128)}, u32[]{:S(2)}) copy-start(s32[24]{0:T(128)} %lengths.3) | copy-start | bytes 292
  6.8 33.2 %all-to-all-start = ((f32[64,40,128]{2,1,0:T(8,128)}), f32[64,40,128]{2,1,0:T(8,128)S(1)}, u32[]{:S(2)}, u32[]{:S(2)}) async-start(f32[64,40,128]{2,1,0:T(8,128)} %bitcast.3), calls=%async_computation | async-start | bytes 2621440 | tf_op jit(solution)/shard_map/all_to_all | solution.py:403
  18.4 1.9 %copy-start.8 = (f32[24,256,128]{2,1,0:T(8,128)S(1)}, f32[24,256,128]{2,1,0:T(8,128)}, u32[]{:S(2)}) copy-start(f32[24,256,128]{2,1,0:T(8,128)} %m_ref.3) | copy-start | bytes 9437188
  33.8 7.4 %copy-start.15 = (bf16[24,128,128]{2,1,0:T(8,128)(2,1)}, bf16[24,128,128]{2,1,0:T(8,128)(2,1)S(1)}, u32[]{:S(2)}) copy-start(bf16[24,128,128]{2,1,0:T(8,128)(2,1)S(1)} %get-tuple-element.24.fl_ref) | copy-start | bytes 2359300
  41.1 6.0 %copy-start.12 = (f32[4,65536]{1,0:T(4,128)S(1)}, f32[4,65536]{1,0:T(4,128)}, u32[]{:S(2)}) copy-start(f32[4,65536]{1,0:T(4,128)} %param.5) | copy-start | bytes 3145732
  41.1 6.0 %copy-start.13 = (s32[24]{0:T(128)S(1)}, s32[24]{0:T(128)}, u32[]{:S(2)}) copy-start(s32[24]{0:T(128)} %offsets.1) | copy-start | bytes 292
  41.1 26.5 %all-to-all-start.1 = ((f32[64,40,128]{2,1,0:T(8,128)}), f32[64,40,128]{2,1,0:T(8,128)S(1)}, u32[]{:S(2)}, u32[]{:S(2)}) async-start(f32[64,40,128]{2,1,0:T(8,128)} %share.1), calls=%async_computation.1 | async-start | bytes 2621440 | tf_op jit(solution)/shard_map/all_to_all | solution.py:403
  47.1 1.9 %copy-start.9 = (f32[24,256,128]{2,1,0:T(8,128)S(1)}, f32[24,256,128]{2,1,0:T(8,128)}, u32[]{:S(2)}) copy-start(f32[24,256,128]{2,1,0:T(8,128)} %m_ref.3) | copy-start | bytes 9437188
  49.0 1.1 copy-start.16
  67.6 6.4 %collective-permute-start.1 = (f32[2560,128]{1,0:T(8,128)S(1)}, f32[2560,128]{1,0:T(8,128)}, u32[]{:S(2)}, u32[]{:S(2)}) collective-permute-start(f32[2560,128]{1,0:T(8,128)S(1)} %bitcast.20), channel_id=1, source_target_pairs={{0,1},{1,0},{2,3},{3,2},{4,5},{5,4},{6,7},{7,6},{8,9},{9,8},{10,11... | collective-permute-start | bytes 3932168 | tf_op jit(solution)/shard_map/ppermute | solution.py:407
  67.6 25.3 %all-to-all-start.2 = ((f32[64,32,128]{2,1,0:T(8,128)}), f32[64,32,128]{2,1,0:T(8,128)S(1)}, u32[]{:S(2)}, u32[]{:S(2)}) async-start(f32[64,32,128]{2,1,0:T(8,128)} %bitcast.5), calls=%async_computation.2 | async-start | bytes 2097152 | tf_op jit(solution)/shard_map/all_to_all | solution.py:403
  79.5 0.9 copy-start.4
  80.4 0.9 copy-start.5
  81.3 0.8 copy-start.6
  82.1 0.8 copy-start.7
  92.9 1.0 copy-start.2
  125.7 27.7 %copy-start.3 = (f32[64,32,128]{2,1,0:T(8,128)S(1)}, f32[64,32,128]{2,1,0:T(8,128)}, u32[]{:S(2)}) copy-start(f32[64,32,128]{2,1,0:T(8,128)} %copy-done.2) | copy-start | bytes 3145732
  125.7 27.7 %copy-start.11 = (f32[512,1024]{1,0:T(8,128)S(1)}, f32[512,1024]{1,0:T(8,128)}, u32[]{:S(2)}) copy-start(f32[512,1024]{1,0:T(8,128)} %own_ref.1) | copy-start | bytes 6291460
  131.1 22.4 %copy-start.1 = (f32[512,1024]{1,0:T(8,128)S(1)}, f32[512,1024]{1,0:T(8,128)}, u32[]{:S(2)}) copy-start(f32[512,1024]{1,0:T(8,128)} %copy-done) | copy-start | bytes 6291460

commit v4 on v3

--- a/solution.py
+++ b/solution.py
@@ -10,7 +10,6 @@
 AXES = ("yh", "x", "yl", "z", "c")
 CHIPS = ("yh", "x", "yl", "z")
 VMEM_LIMIT = 20 * 1024 * 1024
-LARGE = 58 * 1024 * 1024
 
 NN = (((1,), (0,)), ((), ()))
 NT = (((1,), (1,)), ((), ()))
@@ -32,9 +31,18 @@
     return dg(ah, bh, dims) + (dg(ah, bl, dims) + dg(al, bh, dims))
 
 
-def dot3_stacked(a, b):
-    (ah, al), (bh, bl) = a, b
-    return dg(jnp.concatenate([ah, ah, al], axis=1), jnp.concatenate([bh, bl, bh], axis=0))
+def dot4(a, b):
+    n = b[0].shape[1]
+    right = jnp.concatenate(b, axis=1)
+    both = dg(jnp.concatenate(a, axis=1), jnp.concatenate([right, right], axis=0))
+    return both[:, :n] + both[:, n:]
+
+
+def dot4_nt(a, b):
+    n = b[0].shape[0]
+    right = jnp.concatenate(b, axis=0)
+    both = dg(jnp.concatenate(a, axis=1), jnp.concatenate([right, right], axis=1), NT)
+    return both[:, :n] + both[:, n:]
 
 
 def iotas(n):
@@ -64,25 +72,31 @@
         corner = ((row // (2 * size)) == (col // (2 * size))) & ((row & size) == 0) & ((col & size) != 0)
         halves = [split(x) for x in inverses]
         corners = [split(jnp.where(corner, nil, 0.0)) for nil in strict]
-        middles = [split(dot3_stacked(x, m)) for x, m in zip(halves, corners)]
-        inverses = [x - dot3_stacked(y, h) for x, y, h in zip(inverses, middles, halves)]
+        middles = [split(dot4(x, m)) for x, m in zip(halves, corners)]
+        inverses = [x - dot4(y, h) for x, y, h in zip(inverses, middles, halves)]
         size *= 2
     return [x * s for x, s in zip(inverses, scale)]
 
 
-TOGETHER = 4
+TOGETHER = 8
 
 
 def masked_block(lengths, m_ref, b):
     row = lax.broadcasted_iota(jnp.int32, m_ref.shape[1:], 0)
     return split(jnp.where(row < lengths[b], m_ref[b], 0.0))
+
+
+def gram_of(m):
+    width = m[0].shape[1]
+    both = dg(m[0], jnp.concatenate(m, axis=1), TN)
+    return both[:, :width] + both[:, width:] + dg(m[1], m[0], TN)
 
 
 def invert_kernel(lengths, m_ref, fh_ref, fl_ref):
     def group_of(group, carry):
         blocks = [group * TOGETHER + u for u in range(TOGETHER)]
         masked = [masked_block(lengths, m_ref, b) for b in blocks]
-        grams = [dot3(m, m, TN) for m in masked]
+        grams = [gram_of(m) for m in masked]
         for b, f in zip(blocks, inverse_of_half(grams)):
             fh_ref[b], fl_ref[b] = split(f)
         return carry
@@ -98,9 +112,9 @@
     def group_of(group, carry):
         at = [group * TOGETHER + u for u in range(TOGETHER)]
         masked = [masked_block(lengths, m_ref, b) for b in at]
-        lefts = [split(dot3(m, (fh_ref[b], fl_ref[b]), NT)) for m, b in zip(masked, at)]
+        lefts = [split(dot4_nt(m, (fh_ref[b], fl_ref[b]))) for m, b in zip(masked, at)]
         for left, m, b in zip(lefts, masked, at):
-            kh_ref[b], kl_ref[b] = split(dot3(left, m, NT))
+            kh_ref[b], kl_ref[b] = split(dot4_nt(left, m))
         return carry
 
     lax.fori_loop(0, blocks // TOGETHER, group_of, 0)
@@ -256,7 +270,7 @@
     inverses = inverse_of_half(small[:4]) + inverse_of_half(small[4:])
     for p, d in enumerate(diagonals):
         a, c = inverses[2 * p], inverses[2 * p + 1]
-        corner = -dot3_stacked(split(dot3_stacked(split(a), split(d[:128, 128:]))), split(c))
+        corner = -dot4(split(dot4(split(a), split(d[:128, 128:]))), split(c))
         whole = jnp.concatenate(
             [
                 jnp.concatenate([a.T, jnp.zeros((128, 128), F32)], axis=1),
@@ -287,26 +301,14 @@
     return jnp.concatenate([ref[pl.ds(j * 4 + r, 64, stride=stride), :] for r in range(4)], axis=0)
 
 
-def project_kernel(core, e_ref, own_hbm, other_hbm, p_ref, v_ref, sems):
+def project_kernel(core, e_ref, own_ref, other_ref, p_ref):
     c = core[0]
-    copies = []
-    for n in range(4):
-        columns = pl.ds(n * WIDE, WIDE)
-        for side, ref in enumerate((own_hbm, other_hbm)):
-            copy = pltpu.make_async_copy(ref.at[:, columns], v_ref.at[side, :, columns], sems.at[side, n])
-            copy.start()
-            copies.append(copy)
-    lefts = [
-        split(jnp.concatenate([rows_of(e_ref, first + k) for k in range(4)], axis=1))
-        for first in (4 * c, 4 - 4 * c)
+    sides = [
+        (split(jnp.concatenate([rows_of(e_ref, first + k) for k in range(4)], axis=1)), v_ref)
+        for v_ref, first in ((own_ref, 4 * c), (other_ref, 4 - 4 * c))
     ]
     for n in range(4):
-        columns = pl.ds(n * WIDE, WIDE)
-        total = None
-        for side in range(2):
-            copies[2 * n + side].wait()
-            part = dot3(lefts[side], split(v_ref[side, :, columns]))
-            total = part if total is None else total + part
+        total = sum(dot3(left, split(v_ref[:, n * WIDE : (n + 1) * WIDE])) for left, v_ref in sides)
         for h in range(2):
             for r in range(4):
                 p_ref[pl.ds((2 * n + h) * 4 + r, 64, stride=32), :] = total[
@@ -318,23 +320,19 @@
     return pl.pallas_call(
         project_kernel,
         out_shape=jax.ShapeDtypeStruct((2048, 128), F32),
-        in_specs=[smem(), vmem(), hbm(), hbm()],
-        out_specs=vmem(),
-        scratch_shapes=[pltpu.VMEM((2,) + own.shape, F32), pltpu.SemaphoreType.DMA((2, 4))],
-        compiler_params=pltpu.CompilerParams(vmem_limit_bytes=LARGE),
+        in_specs=[smem(), vmem(), vmem(), vmem()],
+        out_specs=vmem(),
+        compiler_params=params(),
         cost_estimate=pl.CostEstimate(flops=2 * 10**9, bytes_accessed=6 << 20, transcendentals=0),
         name="project",
     )(core, e, own, other)
 
 
-def solve_kernel(p_ref, th_hbm, tl_hbm, sh_hbm, sl_hbm, w_ref, th_ref, tl_ref, sh_ref, sl_ref, sems):
-    pairs = ((th_hbm, th_ref), (tl_hbm, tl_ref), (sh_hbm, sh_ref), (sl_hbm, sl_ref))
-    copies = [pltpu.make_async_copy(a, b, sems.at[i]) for i, (a, b) in enumerate(pairs)]
-    for copy in copies:
-        copy.start()
-    total = p_ref[0]
-    for s in range(1, p_ref.shape[0]):
-        total = total + p_ref[s]
+def solve_kernel(p_ref, th_ref, tl_ref, sh_ref, sl_ref, w_ref):
+    sums = [p_ref[k] for k in range(4)]
+    for s in range(4, p_ref.shape[0]):
+        sums[s % 4] = sums[s % 4] + p_ref[s]
+    total = (sums[0] + sums[1]) + (sums[2] + sums[3])
     rest = [
         jnp.concatenate([total[8 * p : 8 * p + 4], total[8 * p + 4 : 8 * p + 8]], axis=1)
         for p in range(4)
@@ -346,8 +344,6 @@
         product = dg(both, bh) + dg(both, bl)
         return product[:4] + product[4:]
 
-    for copy in copies:
-        copy.wait()
     pieces = [None] * 4
     for q in range(3, -1, -1):
         solved = times(rest[q], th_ref[q], tl_ref[q])
@@ -363,11 +359,9 @@
     return pl.pallas_call(
         solve_kernel,
         out_shape=jax.ShapeDtypeStruct(p.shape, F32),
-        in_specs=[vmem()] + [hbm()] * 4,
-        out_specs=vmem(),
-        scratch_shapes=[pltpu.VMEM((n, WIDE, WIDE), BF16) for n in (4, 4, 6, 6)]
-        + [pltpu.SemaphoreType.DMA((4,))],
-        compiler_params=pltpu.CompilerParams(vmem_limit_bytes=LARGE),
+        in_specs=[vmem()] * 5,
+        out_specs=vmem(),
+        compiler_params=params(),
         cost_estimate=pl.CostEstimate(flops=10**9, bytes_accessed=4 << 20, transcendentals=0),
         name="solve",
     )(p, *factors)

time: 182 us -> 176 us (0.967)
  Pallas kernels: 54.1 us -> 39 us
  local copies, waits for them, and re-layouts: 12.6 us -> 18.3 us
  waiting for transfers between devices: 21.9 us -> 25.2 us
    unnamed x35 -> x43, local copies, waits for them, and re-layouts: 12.5 us -> 18.3 us
    pallas_call x1, Pallas kernels: 13.4 us -> 8 us  [invert(): pl.pallas_call(invert_kernel, out_shape=[shape, shape], in_specs=[smem(),...]
    pallas_call x1, Pallas kernels: 5.32 us -> 1.27 us  [solve(): pl.pallas_call(solve_kernel, out_shape=jax.ShapeDtypeStruct(p.shape, F32)...]
    pallas_call x1, Pallas kernels: 8 us -> 4.27 us  [project(): pl.pallas_call(project_kernel, out_shape=jax.ShapeDtypeStruct((2048, 128)...]
    all_to_all x3, waiting for transfers between devices: 20.4 us -> 23.8 us  [to_chips(): return lax.all_to_all(a, CHIPS, split_axis=0, concat_axis=0, tiled=True)]
    pallas_call x1, Pallas kernels: 13.2 us -> 10.6 us  [chase(): pl.pallas_call(chase_kernel, out_shape=jax.ShapeDtypeStruct(tiles.shape,...]
  transfers between devices with their start and end apart: 5 -> 5, of which waited for: 4 -> 4; matrix products, arithmetic and copies ran while one was open for 0% -> 0% of each run, Pallas kernels for 19% -> 14%
where the time goes in v4:
time: 176 us
  blocking collectives  67.9 us (39%)
  Pallas kernels  39 us (22%)
  waiting for transfers between devices  25.2 us (14%)
  starting transfers between devices  24.9 us (14%)
  local copies, waits for them, and re-layouts  18.3 us (10%)
    all_to_all x3, blocking collectives, to_chips(): return lax.all_to_all(a, CHIPS, split_axis=0, concat_axis=0, tiled=True)  67.9 us
    all_to_all x3, starting transfers between devices, to_chips(): return lax.all_to_all(a, CHIPS, split_axis=0, concat_axis=0, tiled=True)  24.9 us
    all_to_all x3, waiting for transfers between devices, to_chips(): return lax.all_to_all(a, CHIPS, split_axis=0, concat_axis=0, tiled=True)  23.8 us
    unnamed x43, local copies, waits for them, and re-layouts  18.3 us
    pallas_call x1, Pallas kernels, chase(): pl.pallas_call(chase_kernel, out_shape=jax.ShapeDtypeStruct(tiles.shape,...  10.6 us
    pallas_call x1, Pallas kernels, invert(): pl.pallas_call(invert_kernel, out_shape=[shape, shape], in_specs=[smem(),...  8 us
    pallas_call x1, Pallas kernels, update(): pl.pallas_call(update_kernel, out_shape=jax.ShapeDtypeStruct((2048, 128),...  5 us
    pallas_call x1, Pallas kernels, factor(): pl.pallas_call(factor_kernel, out_shape=[jax.ShapeDtypeStruct(s, BF16) fo...  4.96 us
  transfers between devices with their start and end apart: 5, of which 4 were waited for; matrix products, arithmetic and copies ran while one was open for 0% of the time, Pallas kernels for 14%

profile of v4, /device:TPU:0, one launch (start us, length us, event | category | flops | bytes accessed | tf_op | source)
XLA Modules:
  0.0 175.6 jit_solution(15588491622577523255)
XLA Ops:
  0.0 1.6 copy-done.11
  1.6 1.3 gram.2.refs_0_
  2.9 1.5 collective-permute-done.v_ref.other_ref
  4.4 2.4 %gram.3 = f32[2560,128]{1,0:T(8,128)} custom-call(s32[1]{0:T(128)} %bitcast.core, f32[512,1024]{1,0:T(8,128)S(1)} %collective-permute-done.v_ref.other_ref, f32[2560,128]{1,0:T(8,128)S(1)} %gram.2.refs_0_), custom_call_target="tpu_custom_call" | custom-call | flops 1000000000 | bytes 4194304 | tf_op jit(solution)/shard_map/gram/pallas_call | solution.py:235
  6.8 11.6 %all-to-all-start = ((f32[64,40,128]{2,1,0:T(8,128)}), f32[64,40,128]{2,1,0:T(8,128)S(1)}, u32[]{:S(2)}, u32[]{:S(2)}) async-start(f32[64,40,128]{2,1,0:T(8,128)} %bitcast.3), calls=%async_computation | async-start | bytes 2621440 | tf_op jit(solution)/shard_map/all_to_all | solution.py:397
  18.4 1.9 %copy-done.9 = f32[24,256,128]{2,1,0:T(8,128)S(1)} copy-done((f32[24,256,128]{2,1,0:T(8,128)S(1)}, f32[24,256,128]{2,1,0:T(8,128)}, u32[]{:S(2)}) %copy-start.9) | copy-done | bytes 3145752
  20.3 8.0 %invert.1 = (bf16[24,128,128]{2,1,0:T(8,128)(2,1)S(1)}, bf16[24,128,128]{2,1,0:T(8,128)(2,1)S(1)}) custom-call(s32[24]{0:T(128)S(1)} %copy-done.16, f32[24,256,128]{2,1,0:T(8,128)S(1)} %copy-done.9), custom_call_target="tpu_custom_call" | custom-call | flops 10000000000 | bytes 5242880 | tf_op jit(solution)/shard_map/invert/pallas_call | solution.py:177
  28.3 0.9 copy-done.17
  29.2 0.9 copy-done.19
  30.1 9.9 %all-to-all-done.g_ref = f32[64,40,128]{2,1,0:T(8,128)S(1)} async-done(((f32[64,40,128]{2,1,0:T(8,128)}), f32[64,40,128]{2,1,0:T(8,128)S(1)}, u32[]{:S(2)}, u32[]{:S(2)}) %all-to-all-start) | async-done | bytes 1310752 | tf_op jit(solution)/shard_map/all_to_all | solution.py:397
  39.9 1.2 share.1
  41.1 5.9 %all-to-all-start.1 = ((f32[64,40,128]{2,1,0:T(8,128)}), f32[64,40,128]{2,1,0:T(8,128)S(1)}, u32[]{:S(2)}, u32[]{:S(2)}) async-start(f32[64,40,128]{2,1,0:T(8,128)} %share.1), calls=%async_computation.1 | async-start | bytes 2621440 | tf_op jit(solution)/shard_map/all_to_all | solution.py:397
  47.1 1.9 %copy-done.10 = f32[24,256,128]{2,1,0:T(8,128)S(1)} copy-done((f32[24,256,128]{2,1,0:T(8,128)S(1)}, f32[24,256,128]{2,1,0:T(8,128)}, u32[]{:S(2)}) %copy-start.10) | copy-done | bytes 3145752
  49.0 1.2 copy-done.14
  50.2 1.1 copy-done.18
  51.4 1.1 copy-done.20
  52.5 10.6 %chase.1 = f32[512,4,128]{2,1,0:T(4,128)S(1)} custom-call(s32[24]{0:T(128)S(1)} %copy-done.15, s32[24]{0:T(128)S(1)} %copy-done.16, f32[512,4,128]{2,1,0:T(4,128)S(1)} %bitcast.26, f32[24,256,128]{2,1,0:T(8,128)S(1)} %copy-done.10, bf16[24,128,128]{2,1,0:T(8,128)(2,1)S(1)} %copy-done.18, bf16[24,128,128]{2,1,0:T(8,128)(2,1)S(1)} %copy-done.20), custom_call_target="tpu_custom_call" | custom-call | flops 10000000000 | bytes 7340032 | tf_op jit(solution)/shard_map/chase/pallas_call | solution.py:190
  63.1 1.0 copy-done
  64.1 3.5 %all-to-all-done.1 = f32[64,40,128]{2,1,0:T(8,128)S(1)} async-done(((f32[64,40,128]{2,1,0:T(8,128)}), f32[64,40,128]{2,1,0:T(8,128)S(1)}, u32[]{:S(2)}, u32[]{:S(2)}) %all-to-all-start.1) | async-done | bytes 1310752 | tf_op jit(solution)/shard_map/all_to_all | solution.py:397
  67.6 7.3 %all-to-all-start.2 = ((f32[64,32,128]{2,1,0:T(8,128)}), f32[64,32,128]{2,1,0:T(8,128)}, u32[]{:S(2)}, u32[]{:S(2)}) async-start(f32[64,32,128]{2,1,0:T(8,128)} %bitcast.22), calls=%async_computation.2 | async-start | bytes 2097152 | tf_op jit(solution)/shard_map/all_to_all | solution.py:397
  75.0 5.0 %factor.1 = (bf16[4,256,256]{2,1,0:T(8,128)(2,1)S(1)}, bf16[4,256,256]{2,1,0:T(8,128)(2,1)S(1)}, bf16[6,256,256]{2,1,0:T(8,128)(2,1)S(1)}, bf16[6,256,256]{2,1,0:T(8,128)(2,1)S(1)}) custom-call(s32[1]{0:T(128)} %bitcast.core, f32[2560,128]{1,0:T(8,128)S(1)} %bitcast.21, f32[2560,128]{1,0:T(8,128)} %collective-permute-done.1.other_ref), custom_call_target="tpu_custom_call" | custom-call | flops 8000000000 | bytes 5242880 | tf_op jit(solution)/shard_map/factor/pallas_call | solution.py:288
  79.9 0.9 copy-done.1
  80.8 0.9 copy-done.3
  83.4 10.4 %all-to-all-done.2 = f32[64,32,128]{2,1,0:T(8,128)} async-done(((f32[64,32,128]{2,1,0:T(8,128)}), f32[64,32,128]{2,1,0:T(8,128)}, u32[]{:S(2)}, u32[]{:S(2)}) %all-to-all-start.2) | async-done | bytes 1048608 | tf_op jit(solution)/shard_map/all_to_all | solution.py:397
  93.8 1.6 copy-done.12
  95.4 4.3 %project.1 = f32[2048,128]{1,0:T(8,128)S(1)} custom-call(s32[1]{0:T(128)} %bitcast.core, f32[2048,128]{1,0:T(8,128)} %bitcast.6.e_ref, f32[512,1024]{1,0:T(8,128)S(1)} %copy-done.12, f32[512,1024]{1,0:T(8,128)S(1)} %collective-permute-done.v_ref.other_ref), custom_call_target="tpu_custom_call" | custom-call | flops 2000000000 | bytes 6291456 | tf_op jit(solution)/shard_map/project/pallas_call | solution.py:320
  99.7 23.6 %all_to_all.30.p_ref = f32[64,32,128]{2,1,0:T(8,128)S(1)} all-to-all(f32[64,32,128]{2,1,0:T(8,128)S(1)} %bitcast.25), channel_id=1, replica_groups=mesh['yh'=2,'x'=4,'yl'=2,'z'=4,'c'=2] {'yh','x','yl','z'}, dimensions={0} | all-to-all | bytes 2097152 | tf_op jit(solution)/shard_map/all_to_all | solution.py:397
  123.3 1.3 solve.1
  124.6 22.2 %all_to_all.31 = f32[64,32,128]{2,1,0:T(8,128)S(1)} all-to-all(f32[64,32,128]{2,1,0:T(8,128)S(1)} %solve.1), channel_id=1, replica_groups=mesh['yh'=2,'x'=4,'yl'=2,'z'=4,'c'=2] {'yh','x','yl','z'}, dimensions={0} | all-to-all | bytes 2097152 | tf_op jit(solution)/shard_map/all_to_all | solution.py:397
  146.8 5.0 %update.1 = f32[2048,128]{1,0:T(8,128)S(1)} custom-call(s32[1]{0:T(128)} %bitcast.core, f32[2048,128]{1,0:T(8,128)} %bitcast.6.e_ref, f32[2048,128]{1,0:T(8,128)S(1)} %bitcast.23, f32[512,1024]{1,0:T(8,128)S(1)} %copy-done.13, f32[512,1024]{1,0:T(8,128)S(1)} %collective-permute-done.v_ref.other_ref), custom_call_target="tpu_custom_call" | custom-call | flops 2000000000 | bytes 7340032 | tf_op jit(solution)/shard_map/update/pallas_call | solution.py:385
  151.8 22.0 %all_to_all.32 = f32[64,32,128]{2,1,0:T(8,128)S(1)} all-to-all(f32[64,32,128]{2,1,0:T(8,128)S(1)} %bitcast.24), channel_id=1, replica_groups=mesh['yh'=2,'x'=4,'yl'=2,'z'=4,'c'=2] {'yh','x','yl','z'}, dimensions={0} | all-to-all | bytes 2097152 | tf_op jit(solution)/shard_map/all_to_all | solution.py:397
  173.9 1.6 copy.10
  (34 shorter events, 1.8 us)
Async XLA Ops:
  0.0 4.4 %collective-permute-start = (f32[512,1024]{1,0:T(8,128)}, f32[512,1024]{1,0:T(8,128)S(1)}, u32[]{:S(2)}, u32[]{:S(2)}) collective-permute-start(f32[512,1024]{1,0:T(8,128)} %own_ref.3), channel_id=1, source_target_pairs={{0,1},{1,0},{2,3},{3,2},{4,5},{5,4},{6,7},{7,6},{8,9},{9,8},{10,11... | collective-permute-start | bytes 6291464 | tf_op jit(solution)/shard_map/ppermute | solution.py:401
  0.0 1.6 copy-start.11
  6.8 11.6 %copy-start.16 = (s32[24]{0:T(128)S(1)}, s32[24]{0:T(128)}, u32[]{:S(2)}) copy-start(s32[24]{0:T(128)} %lengths.3) | copy-start | bytes 292
  6.8 33.2 %all-to-all-start = ((f32[64,40,128]{2,1,0:T(8,128)}), f32[64,40,128]{2,1,0:T(8,128)S(1)}, u32[]{:S(2)}, u32[]{:S(2)}) async-start(f32[64,40,128]{2,1,0:T(8,128)} %bitcast.3), calls=%async_computation | async-start | bytes 2621440 | tf_op jit(solution)/shard_map/all_to_all | solution.py:397
  18.4 1.9 %copy-start.9 = (f32[24,256,128]{2,1,0:T(8,128)S(1)}, f32[24,256,128]{2,1,0:T(8,128)}, u32[]{:S(2)}) copy-start(f32[24,256,128]{2,1,0:T(8,128)} %m_ref.3) | copy-start | bytes 9437188
  28.3 0.9 copy-start.17
  29.2 0.9 copy-start.19
  41.1 6.0 %copy-start.15 = (s32[24]{0:T(128)S(1)}, s32[24]{0:T(128)}, u32[]{:S(2)}) copy-start(s32[24]{0:T(128)} %offsets.1) | copy-start | bytes 292
  41.1 26.5 %all-to-all-start.1 = ((f32[64,40,128]{2,1,0:T(8,128)}), f32[64,40,128]{2,1,0:T(8,128)S(1)}, u32[]{:S(2)}, u32[]{:S(2)}) async-start(f32[64,40,128]{2,1,0:T(8,128)} %share.1), calls=%async_computation.1 | async-start | bytes 2621440 | tf_op jit(solution)/shard_map/all_to_all | solution.py:397
  47.1 1.9 %copy-start.10 = (f32[24,256,128]{2,1,0:T(8,128)S(1)}, f32[24,256,128]{2,1,0:T(8,128)}, u32[]{:S(2)}) copy-start(f32[24,256,128]{2,1,0:T(8,128)} %m_ref.3) | copy-start | bytes 9437188
  49.0 1.2 copy-start.14
  50.2 1.1 copy-start.18
  51.4 1.1 copy-start.20
  63.1 1.0 copy-start
  67.6 7.4 %collective-permute-start.1 = (f32[2560,128]{1,0:T(8,128)S(1)}, f32[2560,128]{1,0:T(8,128)}, u32[]{:S(2)}, u32[]{:S(2)}) collective-permute-start(f32[2560,128]{1,0:T(8,128)S(1)} %bitcast.20), channel_id=1, source_target_pairs={{0,1},{1,0},{2,3},{3,2},{4,5},{5,4},{6,7},{7,6},{8,9},{9,8},{10,11... | collective-permute-start | bytes 3932168 | tf_op jit(solution)/shard_map/ppermute | solution.py:401
  67.6 26.2 %all-to-all-start.2 = ((f32[64,32,128]{2,1,0:T(8,128)}), f32[64,32,128]{2,1,0:T(8,128)}, u32[]{:S(2)}, u32[]{:S(2)}) async-start(f32[64,32,128]{2,1,0:T(8,128)} %bitcast.22), calls=%async_computation.2 | async-start | bytes 2097152 | tf_op jit(solution)/shard_map/all_to_all | solution.py:397
  79.9 0.9 copy-start.1
  80.8 0.9 copy-start.3
  81.7 0.8 copy-start.5
  82.5 0.8 copy-start.7
  93.8 1.6 copy-start.12
  95.4 28.0 %copy-start.8 = (bf16[4,256,256]{2,1,0:T(8,128)(2,1)S(1)}, bf16[4,256,256]{2,1,0:T(8,128)(2,1)}, u32[]{:S(2)}) copy-start(bf16[4,256,256]{2,1,0:T(8,128)(2,1)} %copy-done.7) | copy-start | bytes 1572868
  99.6 23.7 %copy-start.2 = (bf16[6,256,256]{2,1,0:T(8,128)(2,1)S(1)}, bf16[6,256,256]{2,1,0:T(8,128)(2,1)}, u32[]{:S(2)}) copy-start(bf16[6,256,256]{2,1,0:T(8,128)(2,1)} %copy-done.1) | copy-start | bytes 2359300
  99.6 23.7 %copy-start.4 = (bf16[6,256,256]{2,1,0:T(8,128)(2,1)S(1)}, bf16[6,256,256]{2,1,0:T(8,128)(2,1)}, u32[]{:S(2)}) copy-start(bf16[6,256,256]{2,1,0:T(8,128)(2,1)} %copy-done.3) | copy-start | bytes 2359300
  99.7 23.7 %copy-start.6 = (bf16[4,256,256]{2,1,0:T(8,128)(2,1)S(1)}, bf16[4,256,256]{2,1,0:T(8,128)(2,1)}, u32[]{:S(2)}) copy-start(bf16[4,256,256]{2,1,0:T(8,128)(2,1)} %copy-done.5) | copy-start | bytes 1572868
  124.6 22.2 %copy-start.13 = (f32[512,1024]{1,0:T(8,128)S(1)}, f32[512,1024]{1,0:T(8,128)}, u32[]{:S(2)}) copy-start(f32[512,1024]{1,0:T(8,128)} %own_ref.3) | copy-start | bytes 6291460

commit v5 on v4

--- a/solution.py
+++ b/solution.py
@@ -92,19 +92,7 @@
     return both[:, :width] + both[:, width:] + dg(m[1], m[0], TN)
 
 
-def invert_kernel(lengths, m_ref, fh_ref, fl_ref):
-    def group_of(group, carry):
-        blocks = [group * TOGETHER + u for u in range(TOGETHER)]
-        masked = [masked_block(lengths, m_ref, b) for b in blocks]
-        grams = [gram_of(m) for m in masked]
-        for b, f in zip(blocks, inverse_of_half(grams)):
-            fh_ref[b], fl_ref[b] = split(f)
-        return carry
-
-    lax.fori_loop(0, m_ref.shape[0] // TOGETHER, group_of, 0)
-
-
-def chase_kernel(offsets, lengths, e_ref, m_ref, fh_ref, fl_ref, o_ref, kh_ref, kl_ref):
+def chase_kernel(offsets, lengths, e_ref, m_ref, o_ref, kh_ref, kl_ref):
     blocks = m_ref.shape[0]
     tiles, rows = e_ref.shape[0], e_ref.shape[1]
     o_ref[...] = e_ref[...]
@@ -112,7 +100,8 @@
     def group_of(group, carry):
         at = [group * TOGETHER + u for u in range(TOGETHER)]
         masked = [masked_block(lengths, m_ref, b) for b in at]
-        lefts = [split(dot4_nt(m, (fh_ref[b], fl_ref[b]))) for m, b in zip(masked, at)]
+        factors = [split(f) for f in inverse_of_half([gram_of(m) for m in masked])]
+        lefts = [split(dot4_nt(m, f)) for m, f in zip(masked, factors)]
         for left, m, b in zip(lefts, masked, at):
             kh_ref[b], kl_ref[b] = split(dot4_nt(left, m))
         return carry
@@ -171,38 +160,24 @@
     return pl.BlockSpec(memory_space=pltpu.HBM)
 
 
-def invert(reflectors, lengths):
-    blocks, extent, width = reflectors.shape
-    shape = jax.ShapeDtypeStruct((blocks, width, width), BF16)
-    return pl.pallas_call(
-        invert_kernel,
-        out_shape=[shape, shape],
-        in_specs=[smem(), vmem()],
-        out_specs=[vmem()] * 2,
-        compiler_params=params(),
-        cost_estimate=pl.CostEstimate(flops=10 * 10**9, bytes_accessed=5 << 20, transcendentals=0),
-        name="invert",
-    )(lengths, reflectors)
-
-
-def chase(tiles, reflectors, offsets, lengths, fh, fl):
+def chase(tiles, reflectors, offsets, lengths):
     blocks, extent, width = reflectors.shape
     return pl.pallas_call(
         chase_kernel,
         out_shape=jax.ShapeDtypeStruct(tiles.shape, F32),
-        in_specs=[smem(), smem()] + [vmem()] * 4,
+        in_specs=[smem(), smem()] + [vmem()] * 2,
         out_specs=vmem(),
         scratch_shapes=[pltpu.VMEM((blocks, extent, extent), BF16)] * 2,
         compiler_params=params(),
-        cost_estimate=pl.CostEstimate(flops=10 * 10**9, bytes_accessed=7 << 20, transcendentals=0),
+        cost_estimate=pl.CostEstimate(flops=20 * 10**9, bytes_accessed=7 << 20, transcendentals=0),
         name="chase",
-    )(offsets, lengths, tiles, reflectors, fh, fl)
+    )(offsets, lengths, tiles, reflectors)
 
 
 def share(parts):
     return pl.pallas_call(
         share_kernel,
-        out_shape=jax.ShapeDtypeStruct(parts.shape, F32),
+        out_shape=jax.ShapeDtypeStruct((8,) + parts.shape[1:], F32),
         in_specs=[vmem()],
         out_specs=vmem(),
         compiler_params=params(),
@@ -215,7 +190,6 @@
 ORDER = ((0, 1, 2, 3), (2, 0, 3, 1))
 LOCAL = ((0, 1), (1, 2), (2, 3), (1, 1), (2, 2))
 MADE = [(ORDER[c][i], ORDER[c][j]) for c in range(2) for (i, j) in LOCAL]
-UPPER = [(i, j) for i in range(4) for j in range(i + 1, 4)]
 
 
 def gram_kernel(core, v_ref, *refs):
@@ -243,57 +217,81 @@
     )(core, panels, *before)
 
 
-def factor_kernel(core, own_ref, other_ref, th_ref, tl_ref, sh_ref, sl_ref):
-    first = core[0] == 0
-
-    def block(c, at):
-        halves = []
-        for h in range(2):
-            rows = pl.ds((at * 2 + h) * WIDE, WIDE)
-            mine, theirs = own_ref[rows, :], other_ref[rows, :]
-            halves.append(jnp.where(first, mine, theirs) if c == 0 else jnp.where(first, theirs, mine))
-        return jnp.concatenate(halves, axis=1)
-
-    diagonals = [None] * 4
+def rows_between(ref, half, start, stop):
+    pieces = []
+    while start < stop:
+        group, within = divmod(start, 160)
+        count = min(160 - within, stop - start)
+        pieces.append(ref[pl.ds(group * 320 + half * 160 + within, count), :])
+        start += count
+    return jnp.concatenate(pieces, axis=0)
+
+
+def gram_block(ref, at):
+    half, local = divmod(at, len(LOCAL))
+    return jnp.concatenate(
+        [
+            rows_between(ref, half, (2 * local + h) * WIDE, (2 * local + h + 1) * WIDE)
+            for h in range(2)
+        ],
+        axis=1,
+    )
+
+
+def solve_kernel(g_ref, p_ref, w_ref):
+    diagonals, others = [None] * 4, {}
     for at, (i, j) in enumerate(MADE):
-        value = block(at // len(LOCAL), at % len(LOCAL))
+        value = gram_block(g_ref, at)
         if i == j:
             diagonals[i] = value
         else:
-            high, low = split(value.T if i < j else value)
-            slot = UPPER.index((min(i, j), max(i, j)))
-            sh_ref[slot] = high
-            sl_ref[slot] = low
+            others[min(i, j), max(i, j)] = split(value.T if i < j else value)
     small = []
     for d in diagonals:
         small.extend([d[:128, :128], d[128:, 128:]])
-    inverses = inverse_of_half(small[:4]) + inverse_of_half(small[4:])
+    inverses = inverse_of_half(small)
+    transposed = []
     for p, d in enumerate(diagonals):
         a, c = inverses[2 * p], inverses[2 * p + 1]
         corner = -dot4(split(dot4(split(a), split(d[:128, 128:]))), split(c))
-        whole = jnp.concatenate(
-            [
-                jnp.concatenate([a.T, jnp.zeros((128, 128), F32)], axis=1),
-                jnp.concatenate([corner.T, c.T], axis=1),
-            ],
-            axis=0,
-        )
-        high, low = split(whole)
-        th_ref[p] = high
-        tl_ref[p] = low
-
-
-def factor(core, own, other):
-    shapes = [(4, WIDE, WIDE)] * 2 + [(6, WIDE, WIDE)] * 2
-    return pl.pallas_call(
-        factor_kernel,
-        out_shape=[jax.ShapeDtypeStruct(s, BF16) for s in shapes],
-        in_specs=[smem(), vmem(), vmem()],
-        out_specs=[vmem()] * 4,
-        compiler_params=params(),
-        cost_estimate=pl.CostEstimate(flops=8 * 10**9, bytes_accessed=5 << 20, transcendentals=0),
-        name="factor",
-    )(core, own, other)
+        top = jnp.concatenate([a.T, jnp.zeros((128, 128), F32)], axis=1)
+        transposed.append(split(jnp.concatenate([top, jnp.concatenate([corner.T, c.T], axis=1)], axis=0)))
+
+    sums = [p_ref[k] for k in range(4)]
+    for s in range(4, p_ref.shape[0]):
+        sums[s % 4] = sums[s % 4] + p_ref[s]
+    total = (sums[0] + sums[1]) + (sums[2] + sums[3])
+    rest = [
+        jnp.concatenate([total[8 * p : 8 * p + 4], total[8 * p + 4 : 8 * p + 8]], axis=1)
+        for p in range(4)
+    ]
+
+    def times(a, b):
+        high = a.astype(BF16).astype(F32)
+        both = jnp.concatenate([high, a - high], axis=0).astype(BF16)
+        product = dg(both, b[0]) + dg(both, b[1])
+        return product[:4] + product[4:]
+
+    pieces = [None] * 4
+    for q in range(3, -1, -1):
+        solved = times(rest[q], transposed[q])
+        pieces[q] = jnp.concatenate([solved[:, :128], solved[:, 128:]], axis=0)
+        for p in range(q):
+            rest[p] = rest[p] - times(solved, others[p, q])
+    result = jnp.concatenate(pieces, axis=0)
+    w_ref[...] = jnp.broadcast_to(result[None], w_ref.shape)
+
+
+def solve(gathered, p):
+    return pl.pallas_call(
+        solve_kernel,
+        out_shape=jax.ShapeDtypeStruct(p.shape, F32),
+        in_specs=[vmem()] * 2,
+        out_specs=vmem(),
+        compiler_params=params(),
+        cost_estimate=pl.CostEstimate(flops=4 * 10**9, bytes_accessed=5 << 20, transcendentals=0),
+        name="solve",
+    )(gathered, p)
 
 
 def rows_of(ref, j):
@@ -328,45 +326,6 @@
     )(core, e, own, other)
 
 
-def solve_kernel(p_ref, th_ref, tl_ref, sh_ref, sl_ref, w_ref):
-    sums = [p_ref[k] for k in range(4)]
-    for s in range(4, p_ref.shape[0]):
-        sums[s % 4] = sums[s % 4] + p_ref[s]
-    total = (sums[0] + sums[1]) + (sums[2] + sums[3])
-    rest = [
-        jnp.concatenate([total[8 * p : 8 * p + 4], total[8 * p + 4 : 8 * p + 8]], axis=1)
-        for p in range(4)
-    ]
-
-    def times(a, bh, bl):
-        high = a.astype(BF16).astype(F32)
-        both = jnp.concatenate([high, a - high], axis=0).astype(BF16)
-        product = dg(both, bh) + dg(both, bl)
-        return product[:4] + product[4:]
-
-    pieces = [None] * 4
-    for q in range(3, -1, -1):
-        solved = times(rest[q], th_ref[q], tl_ref[q])
-        pieces[q] = jnp.concatenate([solved[:, :128], solved[:, 128:]], axis=0)
-        for p in range(q):
-            at = UPPER.index((p, q))
-            rest[p] = rest[p] - times(solved, sh_ref[at], sl_ref[at])
-    result = jnp.concatenate(pieces, axis=0)
-    w_ref[...] = jnp.broadcast_to(result[None], w_ref.shape)
-
-
-def solve(p, factors):
-    return pl.pallas_call(
-        solve_kernel,
-        out_shape=jax.ShapeDtypeStruct(p.shape, F32),
-        in_specs=[vmem()] * 5,
-        out_specs=vmem(),
-        compiler_params=params(),
-        cost_estimate=pl.CostEstimate(flops=10**9, bytes_accessed=4 << 20, transcendentals=0),
-        name="solve",
-    )(p, *factors)
-
-
 def update_kernel(core, e_ref, w_ref, own_ref, other_ref, o_ref):
     c = core[0]
     left = split(jnp.concatenate([rows_of(w_ref, n) for n in range(8)], axis=1))
@@ -404,19 +363,17 @@
 def body(eigvecs, reflectors, offsets, lengths, panels):
     core = lax.axis_index("c").astype(jnp.int32).reshape(1)
     other = swap_cores(panels)
-    parts = to_chips(gram(core, other, gram(core, panels)).reshape(64, 40, 128))
-    factors = invert(reflectors, lengths)
-    copies = share(parts)
-    copies, factors = lax.optimization_barrier((copies, factors))
-    half = to_chips(copies).reshape(2560, 128)
+    parts = gram(core, other, gram(core, panels)).reshape(64, 40, 128)
+    parts = lax.all_to_all(parts, ("x", "z", "yh", "yl"), split_axis=0, concat_axis=0, tiled=True)
     tiles = eigvecs.reshape(4, 512, 128).transpose(1, 0, 2)
-    chased = chase(tiles, reflectors, offsets, lengths, *factors)
-    chased, half = lax.optimization_barrier((chased, half))
+    chased = chase(tiles, reflectors, offsets, lengths)
+    parts, chased = lax.optimization_barrier((parts, chased))
+    shares = lax.all_to_all(share(parts), ("c", "yh", "yl"), split_axis=0, concat_axis=0, tiled=True)
+    shares, chased = lax.optimization_barrier((shares, chased))
+    gathered = lax.all_gather(shares.reshape(320, 128), ("x", "z"), axis=0, tiled=True)
     mine = to_chips(chased.reshape(64, 32, 128)).reshape(2048, 128)
-    solvers = factor(core, half, swap_cores(half))
-    mine, solvers = lax.optimization_barrier((mine, solvers))
     projected = to_chips(project(core, mine, panels, other).reshape(64, 32, 128))
-    weights = to_chips(solve(projected, solvers)).reshape(2048, 128)
+    weights = to_chips(solve(gathered, projected)).reshape(2048, 128)
     result = to_chips(update(core, mine, weights, panels, other).reshape(64, 32, 128))
     return result.reshape(64, 8, 4, 128).transpose(2, 0, 1, 3).reshape(4, 65536)
 

time: 176 us -> 187 us (1.062)
  blocking collectives: 67.9 us -> 115 us
  waiting for transfers between devices: 25.2 us -> 4.77 us
  between operations: 0.19 us -> 13.5 us
  starting transfers between devices: 24.9 us -> 11.7 us
  local copies, waits for them, and re-layouts: 18.3 us -> 10.4 us
  Pallas kernels: 39 us -> 31.3 us
    all_to_all x3 -> x4, blocking collectives: 67.9 us -> 105 us  [to_chips(): return lax.all_to_all(a, CHIPS, split_axis=0, concat_axis=0, tiled=True)]
    all_to_all x3 -> x1, waiting for transfers between devices: 23.8 us -> 0.28 us  [body(): lax.all_to_all(parts, ('x', 'z', 'yh', 'yl'), split_axis=0, concat_axis=0...]
    pallas_call x3 -> x1, Pallas kernels: 14.2 us -> 0.07 us  [share(): pl.pallas_call(share_kernel, out_shape=jax.ShapeDtypeStruct((8,) + parts....]
    all_to_all x3 -> x1, starting transfers between devices: 24.9 us -> 11.6 us  [body(): lax.all_to_all(parts, ('x', 'z', 'yh', 'yl'), split_axis=0, concat_axis=0...]
    all_to_all x0 -> x1, blocking collectives: none -> 9.84 us  [body(): lax.all_to_all(share(parts), ('c', 'yh', 'yl'), split_axis=0, concat_axis...]
    unnamed x43 -> x21, local copies, waits for them, and re-layouts: 18.3 us -> 10.3 us
    pallas_call x1, Pallas kernels: 10.6 us -> 17.3 us  [chase(): pl.pallas_call(chase_kernel, out_shape=jax.ShapeDtypeStruct(tiles.shape,...]
    all_gather x0 -> x1, waiting for transfers between devices: none -> 2.99 us  [body(): lax.all_gather(shares.reshape(320, 128), ('x', 'z'), axis=0, tiled=True)]
  transfers between devices with their start and end apart: 5 -> 3, of which waited for: 4 -> 3; matrix products, arithmetic and copies ran while one was open for 0% -> 0% of each run, Pallas kernels for 14% -> 12%
where the time goes in v5:
time: 187 us; the launch traced here: 186 us
  blocking collectives  115 us (61%)
  Pallas kernels  31.3 us (17%)
  between operations  13.5 us (7%)
  starting transfers between devices  11.7 us (6%)
  local copies, waits for them, and re-layouts  10.4 us (6%)
  waiting for transfers between devices  4.77 us (3%)
    all_to_all x4, blocking collectives, to_chips(): return lax.all_to_all(a, CHIPS, split_axis=0, concat_axis=0, tiled=True)  105 us
    pallas_call x1, Pallas kernels, chase(): pl.pallas_call(chase_kernel, out_shape=jax.ShapeDtypeStruct(tiles.shape,...  17.3 us
    all_to_all x1, starting transfers between devices, body(): lax.all_to_all(parts, ('x', 'z', 'yh', 'yl'), split_axis=0, concat_axis=0...  11.6 us
    unnamed x21, local copies, waits for them, and re-layouts  10.3 us
    all_to_all x1, blocking collectives, body(): lax.all_to_all(share(parts), ('c', 'yh', 'yl'), split_axis=0, concat_axis...  9.84 us
  transfers between devices with their start and end apart: 3, of which 3 were waited for; matrix products, arithmetic and copies ran while one was open for 0% of the time, Pallas kernels for 12%

profile of v5, /device:TPU:0, one launch (start us, length us, event | category | flops | bytes accessed | tf_op | source)
XLA Modules:
  0.0 186.2 jit_solution(10688823764570605263)
XLA Ops:
  6.5 0.0 collective-permute-start
  6.5 1.6 copy-done.4
  8.1 1.3 gram.2.refs_0_
  9.4 1.5 collective-permute-done.v_ref.other_ref
  10.9 2.4 %gram.3 = f32[2560,128]{1,0:T(8,128)} custom-call(s32[1]{0:T(128)} %bitcast.core, f32[512,1024]{1,0:T(8,128)S(1)} %collective-permute-done.v_ref.other_ref, f32[2560,128]{1,0:T(8,128)S(1)} %gram.2.refs_0_), custom_call_target="tpu_custom_call" | custom-call | flops 1000000000 | bytes 4194304 | tf_op jit(solution)/shard_map/gram/pallas_call | solution.py:209
  13.3 11.6 %all-to-all-start = ((f32[64,40,128]{2,1,0:T(8,128)}), f32[64,40,128]{2,1,0:T(8,128)S(1)}, u32[]{:S(2)}, u32[]{:S(2)}) async-start(f32[64,40,128]{2,1,0:T(8,128)} %bitcast.1), calls=%async_computation | async-start | bytes 2621440 | tf_op jit(solution)/shard_map/all_to_all | solution.py:367
  24.9 0.0 all-gather.2.cloned.1.call-start
  25.0 0.0 copy-done.8
  25.0 0.0 copy-start.2
  25.0 1.9 %copy-done.2 = f32[24,256,128]{2,1,0:T(8,128)S(1)} copy-done((f32[24,256,128]{2,1,0:T(8,128)S(1)}, f32[24,256,128]{2,1,0:T(8,128)}, u32[]{:S(2)}) %copy-start.2) | copy-done | bytes 3145752
  26.9 1.2 copy-done.7
  28.1 17.3 %chase.1 = f32[512,4,128]{2,1,0:T(4,128)S(1)} custom-call(s32[24]{0:T(128)S(1)} %copy-done.8, s32[24]{0:T(128)S(1)} %copy-done.9, f32[512,4,128]{2,1,0:T(4,128)S(1)} %bitcast.26, f32[24,256,128]{2,1,0:T(8,128)S(1)} %copy-done.2), custom_call_target="tpu_custom_call" | custom-call | flops 20000000000 | bytes 7340032 | tf_op jit(solution)/shard_map/chase/pallas_call | solution.py:165
  45.4 1.0 copy-done
  46.4 0.3 all-to-all-done.g_ref
  46.7 0.1 share.1
  46.7 9.8 %all_to_all.30 = f32[8,40,128]{2,1,0:T(8,128)} all-to-all(f32[8,40,128]{2,1,0:T(8,128)S(1)} %share.1), channel_id=1, replica_groups=mesh['yh'=2,'x'=4,'yl'=2,'z'=4,'c'=2] {'c','yh','yl'}, dimensions={0} | all-to-all | bytes 327680 | tf_op jit(solution)/shard_map/all_to_all | solution.py:371
  56.6 0.0 all-gather.2.cloned.1.call-update
  56.6 0.0 copy-start.5
  56.6 28.8 %all_to_all.31 = f32[64,32,128]{2,1,0:T(8,128)S(1)} all-to-all(f32[64,32,128]{2,1,0:T(8,128)} %bitcast.20), channel_id=1, replica_groups=mesh['yh'=2,'x'=4,'yl'=2,'z'=4,'c'=2] {'yh','x','yl','z'}, dimensions={0} | all-to-all | bytes 2097152 | tf_op jit(solution)/shard_map/all_to_all | solution.py:356
  85.4 0.0 copy-done.5
  85.4 3.0 %project.1 = f32[2048,128]{1,0:T(8,128)S(1)} custom-call(s32[1]{0:T(128)} %bitcast.core, f32[2048,128]{1,0:T(8,128)S(1)} %bitcast.21, f32[512,1024]{1,0:T(8,128)S(1)} %copy-done.5, f32[512,1024]{1,0:T(8,128)S(1)} %collective-permute-done.v_ref.other_ref), custom_call_target="tpu_custom_call" | custom-call | flops 2000000000 | bytes 6291456 | tf_op jit(solution)/shard_map/project/pallas_call | solution.py:318
  88.4 28.5 %all_to_all.32.p_ref = f32[64,32,128]{2,1,0:T(8,128)} all-to-all(f32[64,32,128]{2,1,0:T(8,128)S(1)} %bitcast.25), channel_id=1, replica_groups=mesh['yh'=2,'x'=4,'yl'=2,'z'=4,'c'=2] {'yh','x','yl','z'}, dimensions={0} | all-to-all | bytes 2097152 | tf_op jit(solution)/shard_map/all_to_all | solution.py:356
  116.9 3.0 %all-gather.2.cloned.1.call-done.g_ref = f32[5120,128]{1,0:T(8,128)} async-done(((f32[320,128]{1,0:T(8,128)}), f32[5120,128]{1,0:T(8,128)}) %all-gather.2.cloned.1.call-update) | async-done | bytes 2621456 | tf_op jit(solution)/shard_map/all_gather | solution.py:373
  119.9 1.2 copy-done.1
  121.1 1.7 copy-done.3
  122.9 3.6 %solve.1 = f32[64,32,128]{2,1,0:T(8,128)S(1)} custom-call(f32[5120,128]{1,0:T(8,128)S(1)} %copy-done.3, f32[64,32,128]{2,1,0:T(8,128)S(1)} %copy-done.1), custom_call_target="tpu_custom_call" | custom-call | flops 4000000000 | bytes 5242880 | tf_op jit(solution)/shard_map/solve/pallas_call | solution.py:286
  126.5 0.0 copy-start.6
  126.5 24.9 %all_to_all.33 = f32[64,32,128]{2,1,0:T(8,128)S(1)} all-to-all(f32[64,32,128]{2,1,0:T(8,128)S(1)} %solve.1), channel_id=1, replica_groups=mesh['yh'=2,'x'=4,'yl'=2,'z'=4,'c'=2] {'yh','x','yl','z'}, dimensions={0} | all-to-all | bytes 2097152 | tf_op jit(solution)/shard_map/all_to_all | solution.py:356
  151.4 3.7 %update.1 = f32[2048,128]{1,0:T(8,128)S(1)} custom-call(s32[1]{0:T(128)} %bitcast.core, f32[2048,128]{1,0:T(8,128)S(1)} %bitcast.22, f32[2048,128]{1,0:T(8,128)S(1)} %bitcast.23, f32[512,1024]{1,0:T(8,128)S(1)} %copy-done.6, f32[512,1024]{1,0:T(8,128)S(1)} %collective-permute-done.v_ref.other_ref), custom_call_target="tpu_custom_call" | custom-call | flops 2000000000 | bytes 7340032 | tf_op jit(solution)/shard_map/update/pallas_call | solution.py:344
  155.1 22.6 %all_to_all.34 = f32[64,32,128]{2,1,0:T(8,128)S(1)} all-to-all(f32[64,32,128]{2,1,0:T(8,128)S(1)} %bitcast.24), channel_id=1, replica_groups=mesh['yh'=2,'x'=4,'yl'=2,'z'=4,'c'=2] {'yh','x','yl','z'}, dimensions={0} | all-to-all | bytes 2097152 | tf_op jit(solution)/shard_map/all_to_all | solution.py:356
  177.6 0.1 copy.11
  177.7 1.6 copy.10
  (9 shorter events, 0.0 us)
Async XLA Ops:
  6.5 4.4 %collective-permute-start = (f32[512,1024]{1,0:T(8,128)}, f32[512,1024]{1,0:T(8,128)S(1)}, u32[]{:S(2)}, u32[]{:S(2)}) collective-permute-start(f32[512,1024]{1,0:T(8,128)} %own_ref.3), channel_id=1, source_target_pairs={{0,1},{1,0},{2,3},{3,2},{4,5},{5,4},{6,7},{7,6},{8,9},{9,8},{10,11... | collective-permute-start | bytes 6291464 | tf_op jit(solution)/shard_map/ppermute | solution.py:360
  6.5 1.6 copy-start.4
  13.3 11.7 %copy-start.8 = (s32[24]{0:T(128)S(1)}, s32[24]{0:T(128)}, u32[]{:S(2)}) copy-start(s32[24]{0:T(128)} %offsets.1) | copy-start | bytes 292
  13.3 11.7 %copy-start.9 = (s32[24]{0:T(128)S(1)}, s32[24]{0:T(128)}, u32[]{:S(2)}) copy-start(s32[24]{0:T(128)} %lengths.1) | copy-start | bytes 292
  13.3 33.4 %all-to-all-start = ((f32[64,40,128]{2,1,0:T(8,128)}), f32[64,40,128]{2,1,0:T(8,128)S(1)}, u32[]{:S(2)}, u32[]{:S(2)}) async-start(f32[64,40,128]{2,1,0:T(8,128)} %bitcast.1), calls=%async_computation | async-start | bytes 2621440 | tf_op jit(solution)/shard_map/all_to_all | solution.py:367
  24.9 95.0 %all-gather.2.cloned.1.call-start = ((), (), s32[]{:S(2)}) async-start(), calls=%async_computation.6 | async-start | bytes 2785280 | tf_op jit(solution)/shard_map/all_gather | solution.py:373
  25.0 1.9 %copy-start.2 = (f32[24,256,128]{2,1,0:T(8,128)S(1)}, f32[24,256,128]{2,1,0:T(8,128)}, u32[]{:S(2)}) copy-start(f32[24,256,128]{2,1,0:T(8,128)} %m_ref.1) | copy-start | bytes 9437188
  26.9 1.2 copy-start.7
  45.4 1.0 copy-start
  56.6 28.8 %copy-start.5 = (f32[512,1024]{1,0:T(8,128)S(1)}, f32[512,1024]{1,0:T(8,128)}, u32[]{:S(2)}) copy-start(f32[512,1024]{1,0:T(8,128)} %own_ref.3) | copy-start | bytes 6291460
  119.9 1.2 copy-start.1
  121.1 1.7 copy-start.3
  126.5 24.9 %copy-start.6 = (f32[512,1024]{1,0:T(8,128)S(1)}, f32[512,1024]{1,0:T(8,128)}, u32[]{:S(2)}) copy-start(f32[512,1024]{1,0:T(8,128)} %own_ref.3) | copy-start | bytes 6291460
Sparse Core Ops, SparseCore 0:
  56.7 63.1 all-gather.1

commit v6 on v5

--- a/solution.py
+++ b/solution.py
@@ -136,12 +136,14 @@
     lax.fori_loop(0, blocks, step, 0)
 
 
-def share_kernel(g_ref, o_ref):
+def share_kernel(e_ref, g_ref, o_ref):
     sums = [g_ref[k] for k in range(4)]
     for s in range(4, g_ref.shape[0]):
         sums[s % 4] = sums[s % 4] + g_ref[s]
     total = (sums[0] + sums[1]) + (sums[2] + sums[3])
-    o_ref[...] = jnp.broadcast_to(total[None], o_ref.shape)
+    for s in range(g_ref.shape[0]):
+        o_ref[s, :32, :] = e_ref[s]
+        o_ref[s, 32:, :] = total
 
 
 def vmem():
@@ -174,16 +176,16 @@
     )(offsets, lengths, tiles, reflectors)
 
 
-def share(parts):
+def share(chased, parts):
     return pl.pallas_call(
         share_kernel,
-        out_shape=jax.ShapeDtypeStruct((8,) + parts.shape[1:], F32),
-        in_specs=[vmem()],
-        out_specs=vmem(),
-        compiler_params=params(),
-        cost_estimate=pl.CostEstimate(flops=10**6, bytes_accessed=3 << 20, transcendentals=0),
+        out_shape=jax.ShapeDtypeStruct((64, 72, 128), F32),
+        in_specs=[vmem()] * 2,
+        out_specs=vmem(),
+        compiler_params=params(),
+        cost_estimate=pl.CostEstimate(flops=10**6, bytes_accessed=5 << 20, transcendentals=0),
         name="share",
-    )(parts)
+    )(chased, parts)
 
 
 WIDE = 256
@@ -217,31 +219,28 @@
     )(core, panels, *before)
 
 
-def rows_between(ref, half, start, stop):
+def gram_rows(ref, start, stop):
     pieces = []
     while start < stop:
-        group, within = divmod(start, 160)
-        count = min(160 - within, stop - start)
-        pieces.append(ref[pl.ds(group * 320 + half * 160 + within, count), :])
+        chip, within = divmod(start, 40)
+        count = min(40 - within, stop - start)
+        pieces.append(ref[pl.ds(chip * 72 + 32 + within, count), :])
         start += count
     return jnp.concatenate(pieces, axis=0)
 
 
-def gram_block(ref, at):
-    half, local = divmod(at, len(LOCAL))
+def gram_block(ref, local):
     return jnp.concatenate(
-        [
-            rows_between(ref, half, (2 * local + h) * WIDE, (2 * local + h + 1) * WIDE)
-            for h in range(2)
-        ],
-        axis=1,
+        [gram_rows(ref, (2 * local + h) * WIDE, (2 * local + h + 1) * WIDE) for h in range(2)], axis=1
     )
 
 
-def solve_kernel(g_ref, p_ref, w_ref):
+def solve_kernel(core, own_ref, other_ref, p_ref, w_ref):
     diagonals, others = [None] * 4, {}
-    for at, (i, j) in enumerate(MADE):
-        value = gram_block(g_ref, at)
+    first = core[0] == 0
+    pairs = [(gram_block(own_ref, k), gram_block(other_ref, k)) for k in range(len(LOCAL))]
+    values = [jnp.where(first, a, b) for a, b in pairs] + [jnp.where(first, b, a) for a, b in pairs]
+    for value, (i, j) in zip(values, MADE):
         if i == j:
             diagonals[i] = value
         else:
@@ -282,16 +281,16 @@
     w_ref[...] = jnp.broadcast_to(result[None], w_ref.shape)
 
 
-def solve(gathered, p):
+def solve(core, own, other, p):
     return pl.pallas_call(
         solve_kernel,
         out_shape=jax.ShapeDtypeStruct(p.shape, F32),
-        in_specs=[vmem()] * 2,
+        in_specs=[smem()] + [vmem()] * 3,
         out_specs=vmem(),
         compiler_params=params(),
         cost_estimate=pl.CostEstimate(flops=4 * 10**9, bytes_accessed=5 << 20, transcendentals=0),
         name="solve",
-    )(gathered, p)
+    )(core, own, other, p)
 
 
 def rows_of(ref, j):
@@ -363,17 +362,13 @@
 def body(eigvecs, reflectors, offsets, lengths, panels):
     core = lax.axis_index("c").astype(jnp.int32).reshape(1)
     other = swap_cores(panels)
-    parts = gram(core, other, gram(core, panels)).reshape(64, 40, 128)
-    parts = lax.all_to_all(parts, ("x", "z", "yh", "yl"), split_axis=0, concat_axis=0, tiled=True)
+    parts = to_chips(gram(core, other, gram(core, panels)).reshape(64, 40, 128))
     tiles = eigvecs.reshape(4, 512, 128).transpose(1, 0, 2)
     chased = chase(tiles, reflectors, offsets, lengths)
-    parts, chased = lax.optimization_barrier((parts, chased))
-    shares = lax.all_to_all(share(parts), ("c", "yh", "yl"), split_axis=0, concat_axis=0, tiled=True)
-    shares, chased = lax.optimization_barrier((shares, chased))
-    gathered = lax.all_gather(shares.reshape(320, 128), ("x", "z"), axis=0, tiled=True)
-    mine = to_chips(chased.reshape(64, 32, 128)).reshape(2048, 128)
+    mine = to_chips(share(chased.reshape(64, 32, 128), parts)).reshape(4608, 128)
+    theirs = swap_cores(mine)
     projected = to_chips(project(core, mine, panels, other).reshape(64, 32, 128))
-    weights = to_chips(solve(gathered, projected)).reshape(2048, 128)
+    weights = to_chips(solve(core, mine, theirs, projected)).reshape(2048, 128)
     result = to_chips(update(core, mine, weights, panels, other).reshape(64, 32, 128))
     return result.reshape(64, 8, 4, 128).transpose(2, 0, 1, 3).reshape(4, 65536)
 

time: 187 us -> 167 us (0.89)
  between operations: 13.5 us -> 0.11 us
  waiting for transfers between devices: 4.77 us -> 1.59 us
  Pallas kernels: 31.3 us -> 29.4 us
    all_to_all x1 -> x0, blocking collectives: 9.84 us -> none  [body(): lax.all_to_all(share(parts), ('c', 'yh', 'yl'), split_axis=0, concat_axis...]
    all_to_all x4, blocking collectives: 105 us -> 114 us  [to_chips(): return lax.all_to_all(a, CHIPS, split_axis=0, concat_axis=0, tiled=True)]
    all_gather x1 -> x0, waiting for transfers between devices: 2.99 us -> none  [body(): lax.all_gather(shares.reshape(320, 128), ('x', 'z'), axis=0, tiled=True)]
    unnamed x21 -> x19, local copies, waits for them, and re-layouts: 10.3 us -> 9.65 us
  transfers between devices with their start and end apart: 3 -> 3, of which waited for: 3 -> 2; matrix products, arithmetic and copies ran while one was open for 0% -> 0% of each run, Pallas kernels for 12% -> 13%
where the time goes in v6:
time: 167 us
  blocking collectives  114 us (68%)
  Pallas kernels  29.4 us (18%)
  starting transfers between devices  11.6 us (7%)
  local copies, waits for them, and re-layouts  9.71 us (6%)
    all_to_all x4, blocking collectives, to_chips(): return lax.all_to_all(a, CHIPS, split_axis=0, concat_axis=0, tiled=True)  114 us
    pallas_call x1, Pallas kernels, chase(): pl.pallas_call(chase_kernel, out_shape=jax.ShapeDtypeStruct(tiles.shape,...  17.3 us
    all_to_all x1, starting transfers between devices, to_chips(): return lax.all_to_all(a, CHIPS, split_axis=0, concat_axis=0, tiled=True)  11.6 us
    unnamed x19, local copies, waits for them, and re-layouts  9.65 us
    pallas_call x1, Pallas kernels, solve(): pl.pallas_call(solve_kernel, out_shape=jax.ShapeDtypeStruct(p.shape, F32)...  3.68 us
  transfers between devices with their start and end apart: 3, of which 2 were waited for; matrix products, arithmetic and copies ran while one was open for 0% of the time, Pallas kernels for 13%

profile of v6, /device:TPU:0, one launch (start us, length us, event | category | flops | bytes accessed | tf_op | source)
XLA Modules:
  0.0 166.5 jit_solution(6350935001892727951)
XLA Ops:
  0.0 0.0 collective-permute-start
  0.0 0.0 copy-start
  0.0 1.6 copy-done
  1.6 1.3 gram.2.refs_0_
  2.9 1.5 collective-permute-done.v_ref.other_ref
  4.4 1.3 gram.3
  5.7 0.0 copy-start.2
  5.7 1.1 copy-done.2
  6.8 11.6 %all-to-all-start = ((f32[64,40,128]{2,1,0:T(8,128)}), f32[64,40,128]{2,1,0:T(8,128)S(1)}, u32[]{:S(2)}, u32[]{:S(2)}) async-start(f32[64,40,128]{2,1,0:T(8,128)} %bitcast.23), calls=%async_computation | async-start | bytes 2621440 | tf_op jit(solution)/shard_map/all_to_all | solution.py:355
  18.4 0.0 copy-done.7
  18.4 0.0 copy-done.8
  18.4 0.0 copy-start.5
  18.4 1.9 %copy-done.5 = f32[24,256,128]{2,1,0:T(8,128)S(1)} copy-done((f32[24,256,128]{2,1,0:T(8,128)S(1)}, f32[24,256,128]{2,1,0:T(8,128)}, u32[]{:S(2)}) %copy-start.5) | copy-done | bytes 3145752
  20.3 1.2 copy-done.6
  21.6 17.3 %chase.1 = f32[512,4,128]{2,1,0:T(4,128)S(1)} custom-call(s32[24]{0:T(128)S(1)} %copy-done.7, s32[24]{0:T(128)S(1)} %copy-done.8, f32[512,4,128]{2,1,0:T(4,128)S(1)} %bitcast.28, f32[24,256,128]{2,1,0:T(8,128)S(1)} %copy-done.5), custom_call_target="tpu_custom_call" | custom-call | flops 20000000000 | bytes 7340032 | tf_op jit(solution)/shard_map/chase/pallas_call | solution.py:167
  38.9 1.0 copy-done.3
  39.8 0.1 all-to-all-done.g_ref
  39.9 1.2 copy-done.4
  41.2 0.2 share.1
  41.3 0.0 copy-start.1
  41.4 42.7 %all_to_all.25 = f32[64,72,128]{2,1,0:T(8,128)S(1)} all-to-all(f32[64,72,128]{2,1,0:T(8,128)S(1)} %share.1), channel_id=1, replica_groups=mesh['yh'=2,'x'=4,'yl'=2,'z'=4,'c'=2] {'yh','x','yl','z'}, dimensions={0} | all-to-all | bytes 4718592 | tf_op jit(solution)/shard_map/all_to_all | solution.py:355
  84.1 0.0 collective-permute-start.1
  84.1 0.0 copy-done.1
  84.1 2.4 %project.1 = f32[2048,128]{1,0:T(8,128)S(1)} custom-call(s32[1]{0:T(128)} %bitcast.core, f32[4608,128]{1,0:T(8,128)S(1)} %bitcast.20, f32[512,1024]{1,0:T(8,128)S(1)} %copy-done.1, f32[512,1024]{1,0:T(8,128)S(1)} %collective-permute-done.v_ref.other_ref), custom_call_target="tpu_custom_call" | custom-call | flops 2000000000 | bytes 6291456 | tf_op jit(solution)/shard_map/project/pallas_call | solution.py:317
  86.5 25.8 %all_to_all.26.p_ref = f32[64,32,128]{2,1,0:T(8,128)S(1)} all-to-all(f32[64,32,128]{2,1,0:T(8,128)S(1)} %bitcast.26), channel_id=1, replica_groups=mesh['yh'=2,'x'=4,'yl'=2,'z'=4,'c'=2] {'yh','x','yl','z'}, dimensions={0} | all-to-all | bytes 2097152 | tf_op jit(solution)/shard_map/all_to_all | solution.py:355
  112.4 0.0 collective-permute-done.1.other_ref
  112.4 3.7 %solve.1 = f32[64,32,128]{2,1,0:T(8,128)S(1)} custom-call(s32[1]{0:T(128)} %bitcast.core, f32[4608,128]{1,0:T(8,128)S(1)} %bitcast.21, f32[4608,128]{1,0:T(8,128)S(1)} %collective-permute-done.1.other_ref, f32[64,32,128]{2,1,0:T(8,128)S(1)} %all_to_all.26.p_ref), custom_call_target="tpu_custom_call" | custom-call | flops 4000000000 | bytes 5242880 | tf_op jit(solution)/shard_map/solve/pallas_call | solution.py:285
  116.1 23.5 %all_to_all.27 = f32[64,32,128]{2,1,0:T(8,128)S(1)} all-to-all(f32[64,32,128]{2,1,0:T(8,128)S(1)} %solve.1), channel_id=1, replica_groups=mesh['yh'=2,'x'=4,'yl'=2,'z'=4,'c'=2] {'yh','x','yl','z'}, dimensions={0} | all-to-all | bytes 2097152 | tf_op jit(solution)/shard_map/all_to_all | solution.py:355
  139.5 3.2 %update.1 = f32[2048,128]{1,0:T(8,128)S(1)} custom-call(s32[1]{0:T(128)} %bitcast.core, f32[4608,128]{1,0:T(8,128)S(1)} %bitcast.22, f32[2048,128]{1,0:T(8,128)S(1)} %bitcast.24, f32[512,1024]{1,0:T(8,128)S(1)} %copy-done.1, f32[512,1024]{1,0:T(8,128)S(1)} %collective-permute-done.v_ref.other_ref), custom_call_target="tpu_custom_call" | custom-call | flops 2000000000 | bytes 7340032 | tf_op jit(solution)/shard_map/update/pallas_call | solution.py:343
  142.8 22.0 %all_to_all.28 = f32[64,32,128]{2,1,0:T(8,128)S(1)} all-to-all(f32[64,32,128]{2,1,0:T(8,128)S(1)} %bitcast.25), channel_id=1, replica_groups=mesh['yh'=2,'x'=4,'yl'=2,'z'=4,'c'=2] {'yh','x','yl','z'}, dimensions={0} | all-to-all | bytes 2097152 | tf_op jit(solution)/shard_map/all_to_all | solution.py:355
  164.8 0.1 copy.11
  164.9 1.6 copy.10
  (5 shorter events, 0.0 us)
Async XLA Ops:
  0.0 4.4 %collective-permute-start = (f32[512,1024]{1,0:T(8,128)}, f32[512,1024]{1,0:T(8,128)S(1)}, u32[]{:S(2)}, u32[]{:S(2)}) collective-permute-start(f32[512,1024]{1,0:T(8,128)} %own_ref.3), channel_id=1, source_target_pairs={{0,1},{1,0},{2,3},{3,2},{4,5},{5,4},{6,7},{7,6},{8,9},{9,8},{10,11... | collective-permute-start | bytes 6291464 | tf_op jit(solution)/shard_map/ppermute | solution.py:359
  0.0 1.6 copy-start
  5.7 1.1 copy-start.2
  6.8 11.6 %copy-start.7 = (s32[24]{0:T(128)S(1)}, s32[24]{0:T(128)}, u32[]{:S(2)}) copy-start(s32[24]{0:T(128)} %offsets.1) | copy-start | bytes 292
  6.8 11.7 %copy-start.8 = (s32[24]{0:T(128)S(1)}, s32[24]{0:T(128)}, u32[]{:S(2)}) copy-start(s32[24]{0:T(128)} %lengths.1) | copy-start | bytes 292
  6.8 33.2 %all-to-all-start = ((f32[64,40,128]{2,1,0:T(8,128)}), f32[64,40,128]{2,1,0:T(8,128)S(1)}, u32[]{:S(2)}, u32[]{:S(2)}) async-start(f32[64,40,128]{2,1,0:T(8,128)} %bitcast.23), calls=%async_computation | async-start | bytes 2621440 | tf_op jit(solution)/shard_map/all_to_all | solution.py:355
  18.4 1.9 %copy-start.5 = (f32[24,256,128]{2,1,0:T(8,128)S(1)}, f32[24,256,128]{2,1,0:T(8,128)}, u32[]{:S(2)}) copy-start(f32[24,256,128]{2,1,0:T(8,128)} %m_ref.1) | copy-start | bytes 9437188
  20.3 1.2 copy-start.6
  38.9 1.0 copy-start.3
  39.9 1.2 copy-start.4
  41.3 42.8 %copy-start.1 = (f32[512,1024]{1,0:T(8,128)S(1)}, f32[512,1024]{1,0:T(8,128)}, u32[]{:S(2)}) copy-start(f32[512,1024]{1,0:T(8,128)} %own_ref.3) | copy-start | bytes 6291460
  84.1 28.3 %collective-permute-start.1 = (f32[4608,128]{1,0:T(8,128)S(1)}, f32[4608,128]{1,0:T(8,128)S(1)}, u32[]{:S(2)}, u32[]{:S(2)}) collective-permute-start(f32[4608,128]{1,0:T(8,128)S(1)} %bitcast.19), channel_id=1, source_target_pairs={{0,1},{1,0},{2,3},{3,2},{4,5},{5,4},{6,7},{7,6},{8,9},{9,8},{10,11... | collective-permute-start | bytes 7077896 | tf_op jit(solution)/shard_map/ppermute | solution.py:359

commit v7 on v6

--- a/solution.py
+++ b/solution.py
@@ -10,6 +10,7 @@
 AXES = ("yh", "x", "yl", "z", "c")
 CHIPS = ("yh", "x", "yl", "z")
 VMEM_LIMIT = 20 * 1024 * 1024
+LARGE = 58 * 1024 * 1024
 
 NN = (((1,), (0,)), ((), ()))
 NT = (((1,), (1,)), ((), ()))
@@ -53,6 +54,15 @@
 
 
 def inverse_of_half(grams):
+    stages = inverse_stages(grams)
+    while True:
+        try:
+            next(stages)
+        except StopIteration as end:
+            return end.value
+
+
+def inverse_stages(grams):
     n = grams[0].shape[0]
     row, col = iotas(n)
     eye = (row == col).astype(F32)
@@ -73,17 +83,15 @@
         halves = [split(x) for x in inverses]
         corners = [split(jnp.where(corner, nil, 0.0)) for nil in strict]
         middles = [split(dot4(x, m)) for x, m in zip(halves, corners)]
+        yield
         inverses = [x - dot4(y, h) for x, y, h in zip(inverses, middles, halves)]
         size *= 2
+        yield
     return [x * s for x, s in zip(inverses, scale)]
 
 
 TOGETHER = 8
-
-
-def masked_block(lengths, m_ref, b):
-    row = lax.broadcasted_iota(jnp.int32, m_ref.shape[1:], 0)
-    return split(jnp.where(row < lengths[b], m_ref[b], 0.0))
+EVERY = 2
 
 
 def gram_of(m):
@@ -92,28 +100,40 @@
     return both[:, :width] + both[:, width:] + dg(m[1], m[0], TN)
 
 
-def chase_kernel(offsets, lengths, e_ref, m_ref, o_ref, kh_ref, kl_ref):
-    blocks = m_ref.shape[0]
+def chase_kernel(offsets, lengths, e_hbm, m_hbm, o_hbm, e_ref, m_ref, kh_ref, kl_ref, sems):
+    blocks, extent, width = m_ref.shape
     tiles, rows = e_ref.shape[0], e_ref.shape[1]
-    o_ref[...] = e_ref[...]
-
-    def group_of(group, carry):
+    groups = blocks // TOGETHER
+    loads = [
+        pltpu.make_async_copy(
+            m_hbm.at[pl.ds(g * TOGETHER, TOGETHER)], m_ref.at[pl.ds(g * TOGETHER, TOGETHER)], sems.at[g]
+        )
+        for g in range(groups)
+    ]
+    load_e = pltpu.make_async_copy(e_hbm, e_ref, sems.at[groups])
+    loads[0].start()
+    load_e.start()
+    for load in loads[1:]:
+        load.start()
+    row = lax.broadcasted_iota(jnp.int32, (extent, width), 0)
+    lane = lax.broadcasted_iota(jnp.int32, (rows, 128), 1)
+
+    def prepare(group):
         at = [group * TOGETHER + u for u in range(TOGETHER)]
-        masked = [masked_block(lengths, m_ref, b) for b in at]
-        factors = [split(f) for f in inverse_of_half([gram_of(m) for m in masked])]
-        lefts = [split(dot4_nt(m, f)) for m, f in zip(masked, factors)]
+        masked = [split(jnp.where(row < lengths[b], m_ref[b], 0.0)) for b in at]
+        grams = [gram_of(m) for m in masked]
+        yield
+        inverses = yield from inverse_stages(grams)
+        lefts = [split(dot4_nt(m, split(f))) for m, f in zip(masked, inverses)]
+        yield
         for left, m, b in zip(lefts, masked, at):
             kh_ref[b], kl_ref[b] = split(dot4_nt(left, m))
-        return carry
-
-    lax.fori_loop(0, blocks // TOGETHER, group_of, 0)
-    lane = lax.broadcasted_iota(jnp.int32, (rows, 128), 1)
-
-    def step(b, carry):
+
+    def step(b):
         offset = offsets[b]
         tile = jnp.minimum(offset // 128, tiles - 3)
         shift = offset - tile * 128
-        v0, v1, v2 = o_ref[tile], o_ref[tile + 1], o_ref[tile + 2]
+        v0, v1, v2 = e_ref[tile], e_ref[tile + 1], e_ref[tile + 2]
         left = (128 - shift) & 127
         r0 = pltpu.roll(v0, left, 1)
         r1 = pltpu.roll(v1, left, 1)
@@ -128,22 +148,40 @@
         q0 = pltpu.roll(change[:, :128], right, 1)
         q1 = pltpu.roll(change[:, 128:], right, 1)
         after = lane >= shift
-        o_ref[tile] = v0 - jnp.where(after, q0, 0.0)
-        o_ref[tile + 1] = v1 - jnp.where(after, q1, q0)
-        o_ref[tile + 2] = v2 - jnp.where(after, 0.0, q1)
-        return carry
-
-    lax.fori_loop(0, blocks, step, 0)
-
-
-def share_kernel(e_ref, g_ref, o_ref):
+        e_ref[tile] = v0 - jnp.where(after, q0, 0.0)
+        e_ref[tile + 1] = v1 - jnp.where(after, q1, q0)
+        e_ref[tile + 2] = v2 - jnp.where(after, 0.0, q1)
+
+    loads[0].wait()
+    for stage in prepare(0):
+        pass
+    load_e.wait()
+    for load in loads[1:]:
+        load.wait()
+    for group in range(1, groups):
+        waiting = list(range((group - 1) * TOGETHER, group * TOGETHER))
+        for at, stage in enumerate(prepare(group)):
+            if waiting and at % EVERY == 0:
+                step(waiting.pop(0))
+        for b in waiting:
+            step(b)
+    for u in range(TOGETHER):
+        step((groups - 1) * TOGETHER + u)
+    store = pltpu.make_async_copy(e_ref, o_hbm, sems.at[groups + 1])
+    store.start()
+    store.wait()
+
+
+def share_kernel(e_hbm, g_ref, o_ref, sem):
+    copy = pltpu.make_async_copy(e_hbm, o_ref.at[:, pl.ds(0, 32), :], sem)
+    copy.start()
     sums = [g_ref[k] for k in range(4)]
     for s in range(4, g_ref.shape[0]):
         sums[s % 4] = sums[s % 4] + g_ref[s]
     total = (sums[0] + sums[1]) + (sums[2] + sums[3])
     for s in range(g_ref.shape[0]):
-        o_ref[s, :32, :] = e_ref[s]
         o_ref[s, 32:, :] = total
+    copy.wait()
 
 
 def vmem():
@@ -167,10 +205,12 @@
     return pl.pallas_call(
         chase_kernel,
         out_shape=jax.ShapeDtypeStruct(tiles.shape, F32),
-        in_specs=[smem(), smem()] + [vmem()] * 2,
-        out_specs=vmem(),
-        scratch_shapes=[pltpu.VMEM((blocks, extent, extent), BF16)] * 2,
-        compiler_params=params(),
+        in_specs=[smem(), smem()] + [hbm()] * 2,
+        out_specs=hbm(),
+        scratch_shapes=[pltpu.VMEM(tiles.shape, F32), pltpu.VMEM(reflectors.shape, F32)]
+        + [pltpu.VMEM((blocks, extent, extent), BF16)] * 2
+        + [pltpu.SemaphoreType.DMA((blocks // TOGETHER + 2,))],
+        compiler_params=pltpu.CompilerParams(vmem_limit_bytes=LARGE),
         cost_estimate=pl.CostEstimate(flops=20 * 10**9, bytes_accessed=7 << 20, transcendentals=0),
         name="chase",
     )(offsets, lengths, tiles, reflectors)
@@ -180,8 +220,9 @@
     return pl.pallas_call(
         share_kernel,
         out_shape=jax.ShapeDtypeStruct((64, 72, 128), F32),
-        in_specs=[vmem()] * 2,
+        in_specs=[hbm(), vmem()],
         out_specs=vmem(),
+        scratch_shapes=[pltpu.SemaphoreType.DMA],
         compiler_params=params(),
         cost_estimate=pl.CostEstimate(flops=10**6, bytes_accessed=5 << 20, transcendentals=0),
         name="share",
@@ -219,20 +260,9 @@
     )(core, panels, *before)
 
 
-def gram_rows(ref, start, stop):
-    pieces = []
-    while start < stop:
-        chip, within = divmod(start, 40)
-        count = min(40 - within, stop - start)
-        pieces.append(ref[pl.ds(chip * 72 + 32 + within, count), :])
-        start += count
-    return jnp.concatenate(pieces, axis=0)
-
-
 def gram_block(ref, local):
-    return jnp.concatenate(
-        [gram_rows(ref, (2 * local + h) * WIDE, (2 * local + h + 1) * WIDE) for h in range(2)], axis=1
-    )
+    first = 2 * local * WIDE
+    return jnp.concatenate([ref[pl.ds(first + h * WIDE, WIDE), :] for h in range(2)], axis=1)
 
 
 def solve_kernel(core, own_ref, other_ref, p_ref, w_ref):
@@ -298,7 +328,9 @@
     return jnp.concatenate([ref[pl.ds(j * 4 + r, 64, stride=stride), :] for r in range(4)], axis=0)
 
 
-def project_kernel(core, e_ref, own_ref, other_ref, p_ref):
+def project_kernel(core, e_ref, own_ref, other_ref, p_ref, half_ref):
+    for s in range(64):
+        half_ref[s * 40 : (s + 1) * 40, :] = e_ref[s * 72 + 32 : (s + 1) * 72, :]
     c = core[0]
     sides = [
         (split(jnp.concatenate([rows_of(e_ref, first + k) for k in range(4)], axis=1)), v_ref)
@@ -316,9 +348,9 @@
 def project(core, e, own, other):
     return pl.pallas_call(
         project_kernel,
-        out_shape=jax.ShapeDtypeStruct((2048, 128), F32),
+        out_shape=[jax.ShapeDtypeStruct((rows, 128), F32) for rows in (2048, 2560)],
         in_specs=[smem(), vmem(), vmem(), vmem()],
-        out_specs=vmem(),
+        out_specs=[vmem()] * 2,
         compiler_params=params(),
         cost_estimate=pl.CostEstimate(flops=2 * 10**9, bytes_accessed=6 << 20, transcendentals=0),
         name="project",
@@ -351,6 +383,13 @@
     )(core, e, w, own, other)
 
 
+def finish_kernel(t_ref, o_ref):
+    count = o_ref.shape[1] // 128
+    first = pl.program_id(0) * count
+    for t in range(count):
+        o_ref[:, t * 128 : (t + 1) * 128] = t_ref[first + t]
+
+
 def to_chips(a):
     return lax.all_to_all(a, CHIPS, split_axis=0, concat_axis=0, tiled=True)
 
@@ -366,11 +405,20 @@
     tiles = eigvecs.reshape(4, 512, 128).transpose(1, 0, 2)
     chased = chase(tiles, reflectors, offsets, lengths)
     mine = to_chips(share(chased.reshape(64, 32, 128), parts)).reshape(4608, 128)
-    theirs = swap_cores(mine)
-    projected = to_chips(project(core, mine, panels, other).reshape(64, 32, 128))
-    weights = to_chips(solve(core, mine, theirs, projected)).reshape(2048, 128)
+    projected, half = project(core, mine, panels, other)
+    projected = to_chips(projected.reshape(64, 32, 128))
+    weights = to_chips(solve(core, half, swap_cores(half), projected)).reshape(2048, 128)
     result = to_chips(update(core, mine, weights, panels, other).reshape(64, 32, 128))
-    return result.reshape(64, 8, 4, 128).transpose(2, 0, 1, 3).reshape(4, 65536)
+    return pl.pallas_call(
+        finish_kernel,
+        out_shape=jax.ShapeDtypeStruct((4, 65536), F32),
+        grid=(4,),
+        in_specs=[vmem()],
+        out_specs=pl.BlockSpec((4, 16384), lambda i: (0, i)),
+        compiler_params=params(),
+        cost_estimate=pl.CostEstimate(flops=0, bytes_accessed=2 << 20, transcendentals=0),
+        name="finish",
+    )(result.reshape(512, 4, 128))
 
 
 def solution(mesh):

time: 167 us -> 161 us (0.964)
  blocking collectives: 114 us -> 108 us
  local copies, waits for them, and re-layouts: 9.71 us -> 3.88 us
  waiting for transfers between devices: 1.59 us -> 7.1 us
    all_to_all x4, blocking collectives: 114 us -> 108 us  [to_chips(): return lax.all_to_all(a, CHIPS, split_axis=0, concat_axis=0, tiled=True)]
    unnamed x19 -> x8, local copies, waits for them, and re-layouts: 9.65 us -> 3.88 us
    all_to_all x1, waiting for transfers between devices: 0.1 us -> 5.61 us  [to_chips(): return lax.all_to_all(a, CHIPS, split_axis=0, concat_axis=0, tiled=True)]
    pallas_call x1 -> x2, Pallas kernels: 2.43 us -> 4.07 us  [the longest x1 2.55 us: project(): pl.pallas_call(project_kernel, out_shape=[jax.ShapeDtypeStruct((rows, 128...]
  transfers between devices with their start and end apart: 3 -> 3, of which waited for: 2 -> 2; matrix products, arithmetic and copies ran while one was open for 0% -> 0% of each run, Pallas kernels for 13% -> 11%
where the time goes in v7:
time: 161 us
  blocking collectives  108 us (67%)
  Pallas kernels  29.6 us (18%)
  starting transfers between devices  11.8 us (7%)
  waiting for transfers between devices  7.1 us (4%)
  local copies, waits for them, and re-layouts  3.88 us (2%)
    all_to_all x4, blocking collectives, to_chips(): return lax.all_to_all(a, CHIPS, split_axis=0, concat_axis=0, tiled=True)  108 us
    pallas_call x1, Pallas kernels, chase(): pl.pallas_call(chase_kernel, out_shape=jax.ShapeDtypeStruct(tiles.shape,...  15.7 us
    all_to_all x1, starting transfers between devices, to_chips(): return lax.all_to_all(a, CHIPS, split_axis=0, concat_axis=0, tiled=True)  11.7 us
    all_to_all x1, waiting for transfers between devices, to_chips(): return lax.all_to_all(a, CHIPS, split_axis=0, concat_axis=0, tiled=True)  5.61 us
    unnamed x8, local copies, waits for them, and re-layouts  3.88 us
    pallas_call x1, Pallas kernels, solve(): pl.pallas_call(solve_kernel, out_shape=jax.ShapeDtypeStruct(p.shape, F32)...  3.67 us
    pallas_call x1, Pallas kernels, update(): pl.pallas_call(update_kernel, out_shape=jax.ShapeDtypeStruct((2048, 128),...  3.32 us
  transfers between devices with their start and end apart: 3, of which 2 were waited for; matrix products, arithmetic and copies ran while one was open for 0% of the time, Pallas kernels for 11%

profile of v7, /device:TPU:0, one launch (start us, length us, event | category | flops | bytes accessed | tf_op | source)
XLA Modules:
  0.0 160.7 jit_solution(15728256524857176412)
XLA Ops:
  0.0 0.0 collective-permute-start
  0.0 0.0 copy-start.1
  0.0 1.6 copy-done.1
  1.6 1.3 gram.2.refs_0_
  2.9 1.5 collective-permute-done.v_ref.other_ref
  4.4 1.3 gram.3
  5.7 0.0 copy-start
  5.7 1.1 copy-done
  6.8 11.7 %all-to-all-start = ((f32[64,40,128]{2,1,0:T(8,128)}), f32[64,40,128]{2,1,0:T(8,128)S(1)}, u32[]{:S(2)}, u32[]{:S(2)}) async-start(f32[64,40,128]{2,1,0:T(8,128)} %bitcast.13), calls=%async_computation | async-start | bytes 2621440 | tf_op jit(solution)/shard_map/all_to_all | solution.py:394
  18.4 15.7 %chase.1 = f32[512,4,128]{2,1,0:T(4,128)} custom-call(s32[24]{0:T(128)} %offsets.1, s32[24]{0:T(128)} %lengths.1, f32[512,4,128]{2,1,0:T(4,128)} %bitcast.19, f32[24,256,128]{2,1,0:T(8,128)} %m_hbm.1), custom_call_target="tpu_custom_call" | custom-call | flops 20000000000 | bytes 7340032 | tf_op jit(solution)/shard_map/chase/pallas_call | solution.py:205
  34.2 5.6 %all-to-all-done.g_ref = f32[64,40,128]{2,1,0:T(8,128)S(1)} async-done(((f32[64,40,128]{2,1,0:T(8,128)}), f32[64,40,128]{2,1,0:T(8,128)S(1)}, u32[]{:S(2)}, u32[]{:S(2)}) %all-to-all-start) | async-done | bytes 1310752 | tf_op jit(solution)/shard_map/all_to_all | solution.py:394
  39.8 0.0 copy-start.3
  39.8 1.2 copy-done.3
  41.0 0.3 share.1
  41.3 0.0 copy-start.2
  41.3 37.8 %all_to_all.25 = f32[64,72,128]{2,1,0:T(8,128)S(1)} all-to-all(f32[64,72,128]{2,1,0:T(8,128)S(1)} %share.1), channel_id=1, replica_groups=mesh['yh'=2,'x'=4,'yl'=2,'z'=4,'c'=2] {'yh','x','yl','z'}, dimensions={0} | all-to-all | bytes 4718592 | tf_op jit(solution)/shard_map/all_to_all | solution.py:394
  79.1 0.0 copy-done.2
  79.1 2.5 %project.1 = (f32[2048,128]{1,0:T(8,128)S(1)}, f32[2560,128]{1,0:T(8,128)S(1)}) custom-call(s32[1]{0:T(128)} %bitcast.core, f32[4608,128]{1,0:T(8,128)S(1)} %bitcast.11, f32[512,1024]{1,0:T(8,128)S(1)} %copy-done.2, f32[512,1024]{1,0:T(8,128)S(1)} %collective-permute-done.v_ref.other_ref), custom_call_target="tpu_custom_call" | custom-call | flops 2000000000 | bytes 6291456 | tf_op jit(solution)/shard_map/project/pallas_call | solution.py:349
  81.7 0.1 collective-permute-start.1
  81.8 24.9 %all_to_all.26.p_ref = f32[64,32,128]{2,1,0:T(8,128)S(1)} all-to-all(f32[64,32,128]{2,1,0:T(8,128)S(1)} %bitcast.17), channel_id=1, replica_groups=mesh['yh'=2,'x'=4,'yl'=2,'z'=4,'c'=2] {'yh','x','yl','z'}, dimensions={0} | all-to-all | bytes 2097152 | tf_op jit(solution)/shard_map/all_to_all | solution.py:394
  106.7 0.0 collective-permute-done.1.other_ref
  106.7 3.7 %solve.1 = f32[64,32,128]{2,1,0:T(8,128)S(1)} custom-call(s32[1]{0:T(128)} %bitcast.core, f32[2560,128]{1,0:T(8,128)S(1)} %get-tuple-element.7.own_ref, f32[2560,128]{1,0:T(8,128)S(1)} %collective-permute-done.1.other_ref, f32[64,32,128]{2,1,0:T(8,128)S(1)} %all_to_all.26.p_ref), custom_call_target="tpu_custom_call" | custom-call | flops 4000000000 | bytes 5242880 | tf_op jit(solution)/shard_map/solve/pallas_call | solution.py:315
  110.4 23.4 %all_to_all.27 = f32[64,32,128]{2,1,0:T(8,128)S(1)} all-to-all(f32[64,32,128]{2,1,0:T(8,128)S(1)} %solve.1), channel_id=1, replica_groups=mesh['yh'=2,'x'=4,'yl'=2,'z'=4,'c'=2] {'yh','x','yl','z'}, dimensions={0} | all-to-all | bytes 2097152 | tf_op jit(solution)/shard_map/all_to_all | solution.py:394
  133.8 3.3 %update.1 = f32[2048,128]{1,0:T(8,128)S(1)} custom-call(s32[1]{0:T(128)} %bitcast.core, f32[4608,128]{1,0:T(8,128)S(1)} %bitcast.12, f32[2048,128]{1,0:T(8,128)S(1)} %bitcast.14, f32[512,1024]{1,0:T(8,128)S(1)} %copy-done.2, f32[512,1024]{1,0:T(8,128)S(1)} %collective-permute-done.v_ref.other_ref), custom_call_target="tpu_custom_call" | custom-call | flops 2000000000 | bytes 7340032 | tf_op jit(solution)/shard_map/update/pallas_call | solution.py:375
  137.1 22.0 %all_to_all.28 = f32[64,32,128]{2,1,0:T(8,128)S(1)} all-to-all(f32[64,32,128]{2,1,0:T(8,128)S(1)} %bitcast.15), channel_id=1, replica_groups=mesh['yh'=2,'x'=4,'yl'=2,'z'=4,'c'=2] {'yh','x','yl','z'}, dimensions={0} | all-to-all | bytes 2097152 | tf_op jit(solution)/shard_map/all_to_all | solution.py:394
  159.1 1.5 finish.1
Async XLA Ops:
  0.0 4.4 %collective-permute-start = (f32[512,1024]{1,0:T(8,128)}, f32[512,1024]{1,0:T(8,128)S(1)}, u32[]{:S(2)}, u32[]{:S(2)}) collective-permute-start(f32[512,1024]{1,0:T(8,128)} %own_ref.3), channel_id=1, source_target_pairs={{0,1},{1,0},{2,3},{3,2},{4,5},{5,4},{6,7},{7,6},{8,9},{9,8},{10,11... | collective-permute-start | bytes 6291464 | tf_op jit(solution)/shard_map/ppermute | solution.py:398
  0.0 1.6 copy-start.1
  5.7 1.1 copy-start
  6.8 33.0 %all-to-all-start = ((f32[64,40,128]{2,1,0:T(8,128)}), f32[64,40,128]{2,1,0:T(8,128)S(1)}, u32[]{:S(2)}, u32[]{:S(2)}) async-start(f32[64,40,128]{2,1,0:T(8,128)} %bitcast.13), calls=%async_computation | async-start | bytes 2621440 | tf_op jit(solution)/shard_map/all_to_all | solution.py:394
  39.8 1.2 copy-start.3
  41.3 37.8 %copy-start.2 = (f32[512,1024]{1,0:T(8,128)S(1)}, f32[512,1024]{1,0:T(8,128)}, u32[]{:S(2)}) copy-start(f32[512,1024]{1,0:T(8,128)} %own_ref.3) | copy-start | bytes 6291460
  81.7 25.0 %collective-permute-start.1 = (f32[2560,128]{1,0:T(8,128)S(1)}, f32[2560,128]{1,0:T(8,128)S(1)}, u32[]{:S(2)}, u32[]{:S(2)}) collective-permute-start(f32[2560,128]{1,0:T(8,128)S(1)} %get-tuple-element.7.own_ref), channel_id=1, source_target_pairs={{0,1},{1,0},{2,3},{3,2},{4,5},{5,4},{6,7},{7,6},{8,9},{9,8},{10,11... | collective-permute-start | bytes 3932168 | tf_op jit(solution)/shard_map/ppermute | solution.py:398

commit v8 on v7

--- a/solution.py
+++ b/solution.py
@@ -173,14 +173,15 @@
 
 
 def share_kernel(e_hbm, g_ref, o_ref, sem):
-    copy = pltpu.make_async_copy(e_hbm, o_ref.at[:, pl.ds(0, 32), :], sem)
+    copy = pltpu.make_async_copy(e_hbm, o_ref.at[:, pl.ds(0, 8)], sem)
     copy.start()
+    chips, count = g_ref.shape[0], g_ref.shape[1]
     sums = [g_ref[k] for k in range(4)]
-    for s in range(4, g_ref.shape[0]):
+    for s in range(4, chips):
         sums[s % 4] = sums[s % 4] + g_ref[s]
     total = (sums[0] + sums[1]) + (sums[2] + sums[3])
-    for s in range(g_ref.shape[0]):
-        o_ref[s, 32:, :] = total
+    for s in range(chips):
+        o_ref[s, 8:] = total
     copy.wait()
 
 
@@ -219,7 +220,7 @@
 def share(chased, parts):
     return pl.pallas_call(
         share_kernel,
-        out_shape=jax.ShapeDtypeStruct((64, 72, 128), F32),
+        out_shape=jax.ShapeDtypeStruct((64, 8 + SHARE // 4, 4, 128), F32),
         in_specs=[hbm(), vmem()],
         out_specs=vmem(),
         scratch_shapes=[pltpu.SemaphoreType.DMA],
@@ -233,6 +234,9 @@
 ORDER = ((0, 1, 2, 3), (2, 0, 3, 1))
 LOCAL = ((0, 1), (1, 2), (2, 3), (1, 1), (2, 2))
 MADE = [(ORDER[c][i], ORDER[c][j]) for c in range(2) for (i, j) in LOCAL]
+SENT = [(WIDE // 2 if i == j else WIDE, WIDE) for (i, j) in LOCAL]
+STARTS = [sum(map(sum, SENT[:at])) for at in range(len(LOCAL) + 1)]
+SHARE = STARTS[-1] // 64
 
 
 def gram_kernel(core, v_ref, *refs):
@@ -242,16 +246,18 @@
     halves = [split(v_ref[:, pl.ds(pl.multiple_of(o * WIDE, WIDE), WIDE)]) for o in order]
     for at, (i, j) in enumerate(LOCAL):
         block = dot3(halves[i], halves[j], TN)
-        for h in range(2):
-            rows = pl.ds((at * 2 + h) * WIDE, WIDE)
-            part = block[:, h * 128 : (h + 1) * 128]
+        start = STARTS[at]
+        for h, count in enumerate(SENT[at]):
+            rows = pl.ds(start, count)
+            part = block[:count, h * 128 : (h + 1) * 128]
             g_ref[rows, :] = part + refs[0][rows, :] if len(refs) == 2 else part
+            start += count
 
 
 def gram(core, panels, *before):
     return pl.pallas_call(
         gram_kernel,
-        out_shape=jax.ShapeDtypeStruct((len(LOCAL) * 2 * WIDE, 128), F32),
+        out_shape=jax.ShapeDtypeStruct((STARTS[-1], 128), F32),
         in_specs=[smem(), vmem()] + [vmem()] * len(before),
         out_specs=vmem(),
         compiler_params=params(),
@@ -261,8 +267,12 @@
 
 
 def gram_block(ref, local):
-    first = 2 * local * WIDE
-    return jnp.concatenate([ref[pl.ds(first + h * WIDE, WIDE), :] for h in range(2)], axis=1)
+    left, right = SENT[local]
+    start = STARTS[local]
+    first = ref[pl.ds(start, left), :]
+    if left < right:
+        first = jnp.concatenate([first, jnp.zeros((right - left, 128), F32)], axis=0)
+    return jnp.concatenate([first, ref[pl.ds(start + left, right), :]], axis=1)
 
 
 def solve_kernel(core, own_ref, other_ref, p_ref, w_ref):
@@ -329,8 +339,9 @@
 
 
 def project_kernel(core, e_ref, own_ref, other_ref, p_ref, half_ref):
+    stride = 32 + SHARE
     for s in range(64):
-        half_ref[s * 40 : (s + 1) * 40, :] = e_ref[s * 72 + 32 : (s + 1) * 72, :]
+        half_ref[s * SHARE : (s + 1) * SHARE, :] = e_ref[s * stride + 32 : (s + 1) * stride, :]
     c = core[0]
     sides = [
         (split(jnp.concatenate([rows_of(e_ref, first + k) for k in range(4)], axis=1)), v_ref)
@@ -348,7 +359,7 @@
 def project(core, e, own, other):
     return pl.pallas_call(
         project_kernel,
-        out_shape=[jax.ShapeDtypeStruct((rows, 128), F32) for rows in (2048, 2560)],
+        out_shape=[jax.ShapeDtypeStruct((rows, 128), F32) for rows in (2048, STARTS[-1])],
         in_specs=[smem(), vmem(), vmem(), vmem()],
         out_specs=[vmem()] * 2,
         compiler_params=params(),
@@ -401,10 +412,10 @@
 def body(eigvecs, reflectors, offsets, lengths, panels):
     core = lax.axis_index("c").astype(jnp.int32).reshape(1)
     other = swap_cores(panels)
-    parts = to_chips(gram(core, other, gram(core, panels)).reshape(64, 40, 128))
+    parts = to_chips(gram(core, other, gram(core, panels)).reshape(64, SHARE // 4, 4, 128))
     tiles = eigvecs.reshape(4, 512, 128).transpose(1, 0, 2)
     chased = chase(tiles, reflectors, offsets, lengths)
-    mine = to_chips(share(chased.reshape(64, 32, 128), parts)).reshape(4608, 128)
+    mine = to_chips(share(chased.reshape(64, 8, 4, 128), parts)).reshape(64 * (32 + SHARE), 128)
     projected, half = project(core, mine, panels, other)
     projected = to_chips(projected.reshape(64, 32, 128))
     weights = to_chips(solve(core, half, swap_cores(half), projected)).reshape(2048, 128)

time: 161 us -> 160 us (level)
    unnamed x8 -> x6, local copies, waits for them, and re-layouts: 3.88 us -> 2.82 us
where the time goes in v8:
time: 160 us; the launch traced here: 159 us
  blocking collectives  108 us (68%)
  Pallas kernels  30.5 us (19%)
  starting transfers between devices  11.8 us (7%)
  waiting for transfers between devices  5.74 us (4%)
  local copies, waits for them, and re-layouts  2.82 us (2%)
    all_to_all x4, blocking collectives, to_chips(): return lax.all_to_all(a, CHIPS, split_axis=0, concat_axis=0, tiled=True)  108 us
    pallas_call x1, Pallas kernels, chase(): pl.pallas_call(chase_kernel, out_shape=jax.ShapeDtypeStruct(tiles.shape,...  15.7 us
    all_to_all x1, starting transfers between devices, to_chips(): return lax.all_to_all(a, CHIPS, split_axis=0, concat_axis=0, tiled=True)  11.7 us
    all_to_all x1, waiting for transfers between devices, to_chips(): return lax.all_to_all(a, CHIPS, split_axis=0, concat_axis=0, tiled=True)  4.27 us
    pallas_call x1, Pallas kernels, solve(): pl.pallas_call(solve_kernel, out_shape=jax.ShapeDtypeStruct(p.shape, F32)...  3.67 us
    pallas_call x2, Pallas kernels, gram(): pl.pallas_call(gram_kernel, out_shape=jax.ShapeDtypeStruct((STARTS[-1], 1...  3.64 us
  transfers between devices with their start and end apart: 3, of which 2 were waited for; matrix products, arithmetic and copies ran while one was open for 0% of the time, Pallas kernels for 11%

profile of v8, /device:TPU:0, one launch (start us, length us, event | category | flops | bytes accessed | tf_op | source)
XLA Modules:
  0.0 159.4 jit_solution(9527580177701766918)
XLA Ops:
  0.0 0.0 collective-permute-start
  0.0 0.0 copy-start
  0.0 1.6 copy-done
  1.6 1.3 gram.2.refs_0_
  2.9 1.5 collective-permute-done.v_ref.other_ref
  4.4 2.3 %gram.3 = f32[2304,128]{1,0:T(8,128)} custom-call(s32[1]{0:T(128)} %bitcast.core, f32[512,1024]{1,0:T(8,128)S(1)} %collective-permute-done.v_ref.other_ref, f32[2304,128]{1,0:T(8,128)S(1)} %gram.2.refs_0_), custom_call_target="tpu_custom_call" | custom-call | flops 1000000000 | bytes 4194304 | tf_op jit(solution)/shard_map/gram/pallas_call | solution.py:258
  6.7 11.7 %all-to-all-start = ((f32[64,9,4,128]{3,2,1,0:T(4,128)}), f32[64,9,4,128]{3,2,1,0:T(4,128)S(1)}, u32[]{:S(2)}, u32[]{:S(2)}) async-start(f32[64,9,4,128]{3,2,1,0:T(4,128)} %bitcast.4), calls=%async_computation | async-start | bytes 2359296 | tf_op jit(solution)/shard_map/all_to_all | solution.py:405
  18.4 15.7 %chase.1 = f32[512,4,128]{2,1,0:T(4,128)} custom-call(s32[24]{0:T(128)} %offsets.1, s32[24]{0:T(128)} %lengths.1, f32[512,4,128]{2,1,0:T(4,128)} %bitcast.18, f32[24,256,128]{2,1,0:T(8,128)} %m_hbm.1), custom_call_target="tpu_custom_call" | custom-call | flops 20000000000 | bytes 7340032 | tf_op jit(solution)/shard_map/chase/pallas_call | solution.py:206
  34.1 4.3 %all-to-all-done.g_ref = f32[64,9,4,128]{3,2,1,0:T(4,128)S(1)} async-done(((f32[64,9,4,128]{3,2,1,0:T(4,128)}), f32[64,9,4,128]{3,2,1,0:T(4,128)S(1)}, u32[]{:S(2)}, u32[]{:S(2)}) %all-to-all-start) | async-done | bytes 1179680 | tf_op jit(solution)/shard_map/all_to_all | solution.py:405
  38.4 0.0 copy-start.2
  38.4 1.2 copy-done.2
  39.6 0.4 share.1
  40.0 0.0 copy-start.1
  40.0 37.3 %all_to_all.25 = f32[64,17,4,128]{3,2,1,0:T(4,128)S(1)} all-to-all(f32[64,17,4,128]{3,2,1,0:T(4,128)S(1)} %share.1), channel_id=1, replica_groups=mesh['yh'=2,'x'=4,'yl'=2,'z'=4,'c'=2] {'yh','x','yl','z'}, dimensions={0} | all-to-all | bytes 4456448 | tf_op jit(solution)/shard_map/all_to_all | solution.py:405
  77.3 0.0 copy-done.1
  77.3 2.5 %project.1 = (f32[2048,128]{1,0:T(8,128)S(1)}, f32[2304,128]{1,0:T(8,128)S(1)}) custom-call(s32[1]{0:T(128)} %bitcast.core, f32[4352,128]{1,0:T(8,128)S(1)} %bitcast.11, f32[512,1024]{1,0:T(8,128)S(1)} %copy-done.1, f32[512,1024]{1,0:T(8,128)S(1)} %collective-permute-done.v_ref.other_ref), custom_call_target="tpu_custom_call" | custom-call | flops 2000000000 | bytes 6291456 | tf_op jit(solution)/shard_map/project/pallas_call | solution.py:360
  79.8 0.1 collective-permute-start.1
  79.9 25.8 %all_to_all.26.p_ref = f32[64,32,128]{2,1,0:T(8,128)S(1)} all-to-all(f32[64,32,128]{2,1,0:T(8,128)S(1)} %bitcast.17), channel_id=1, replica_groups=mesh['yh'=2,'x'=4,'yl'=2,'z'=4,'c'=2] {'yh','x','yl','z'}, dimensions={0} | all-to-all | bytes 2097152 | tf_op jit(solution)/shard_map/all_to_all | solution.py:405
  105.7 0.0 collective-permute-done.1.other_ref
  105.7 3.7 %solve.1 = f32[64,32,128]{2,1,0:T(8,128)S(1)} custom-call(s32[1]{0:T(128)} %bitcast.core, f32[2304,128]{1,0:T(8,128)S(1)} %get-tuple-element.7.own_ref, f32[2304,128]{1,0:T(8,128)S(1)} %collective-permute-done.1.other_ref, f32[64,32,128]{2,1,0:T(8,128)S(1)} %all_to_all.26.p_ref), custom_call_target="tpu_custom_call" | custom-call | flops 4000000000 | bytes 5242880 | tf_op jit(solution)/shard_map/solve/pallas_call | solution.py:325
  109.4 23.4 %all_to_all.27 = f32[64,32,128]{2,1,0:T(8,128)S(1)} all-to-all(f32[64,32,128]{2,1,0:T(8,128)S(1)} %solve.1), channel_id=1, replica_groups=mesh['yh'=2,'x'=4,'yl'=2,'z'=4,'c'=2] {'yh','x','yl','z'}, dimensions={0} | all-to-all | bytes 2097152 | tf_op jit(solution)/shard_map/all_to_all | solution.py:405
  132.8 3.1 %update.1 = f32[2048,128]{1,0:T(8,128)S(1)} custom-call(s32[1]{0:T(128)} %bitcast.core, f32[4352,128]{1,0:T(8,128)S(1)} %bitcast.12, f32[2048,128]{1,0:T(8,128)S(1)} %bitcast.13, f32[512,1024]{1,0:T(8,128)S(1)} %copy-done.1, f32[512,1024]{1,0:T(8,128)S(1)} %collective-permute-done.v_ref.other_ref), custom_call_target="tpu_custom_call" | custom-call | flops 2000000000 | bytes 7340032 | tf_op jit(solution)/shard_map/update/pallas_call | solution.py:386
  135.9 22.0 %all_to_all.28 = f32[64,32,128]{2,1,0:T(8,128)S(1)} all-to-all(f32[64,32,128]{2,1,0:T(8,128)S(1)} %bitcast.14), channel_id=1, replica_groups=mesh['yh'=2,'x'=4,'yl'=2,'z'=4,'c'=2] {'yh','x','yl','z'}, dimensions={0} | all-to-all | bytes 2097152 | tf_op jit(solution)/shard_map/all_to_all | solution.py:405
  157.9 1.5 finish.1
Async XLA Ops:
  0.0 4.4 %collective-permute-start = (f32[512,1024]{1,0:T(8,128)}, f32[512,1024]{1,0:T(8,128)S(1)}, u32[]{:S(2)}, u32[]{:S(2)}) collective-permute-start(f32[512,1024]{1,0:T(8,128)} %own_ref.3), channel_id=1, source_target_pairs={{0,1},{1,0},{2,3},{3,2},{4,5},{5,4},{6,7},{7,6},{8,9},{9,8},{10,11... | collective-permute-start | bytes 6291464 | tf_op jit(solution)/shard_map/ppermute | solution.py:409
  0.0 1.6 copy-start
  6.7 31.7 %all-to-all-start = ((f32[64,9,4,128]{3,2,1,0:T(4,128)}), f32[64,9,4,128]{3,2,1,0:T(4,128)S(1)}, u32[]{:S(2)}, u32[]{:S(2)}) async-start(f32[64,9,4,128]{3,2,1,0:T(4,128)} %bitcast.4), calls=%async_computation | async-start | bytes 2359296 | tf_op jit(solution)/shard_map/all_to_all | solution.py:405
  38.4 1.2 copy-start.2
  40.0 37.3 %copy-start.1 = (f32[512,1024]{1,0:T(8,128)S(1)}, f32[512,1024]{1,0:T(8,128)}, u32[]{:S(2)}) copy-start(f32[512,1024]{1,0:T(8,128)} %own_ref.3) | copy-start | bytes 6291460
  79.8 25.9 %collective-permute-start.1 = (f32[2304,128]{1,0:T(8,128)S(1)}, f32[2304,128]{1,0:T(8,128)S(1)}, u32[]{:S(2)}, u32[]{:S(2)}) collective-permute-start(f32[2304,128]{1,0:T(8,128)S(1)} %get-tuple-element.7.own_ref), channel_id=1, source_target_pairs={{0,1},{1,0},{2,3},{3,2},{4,5},{5,4},{6,7},{7,6},{8,9},{9,8},{10,11... | collective-permute-start | bytes 3538952 | tf_op jit(solution)/shard_map/ppermute | solution.py:409

commit v9 on v8

--- a/solution.py
+++ b/solution.py
@@ -224,7 +224,7 @@
         in_specs=[hbm(), vmem()],
         out_specs=vmem(),
         scratch_shapes=[pltpu.SemaphoreType.DMA],
-        compiler_params=params(),
+        compiler_params=pltpu.CompilerParams(vmem_limit_bytes=20 * 1024 * 1024),
         cost_estimate=pl.CostEstimate(flops=10**6, bytes_accessed=5 << 20, transcendentals=0),
         name="share",
     )(chased, parts)
@@ -239,31 +239,59 @@
 SHARE = STARTS[-1] // 64
 
 
-def gram_kernel(core, v_ref, *refs):
+def gram_blocks(core, v_ref):
     c = core[0]
-    g_ref = refs[-1]
     order = (2 * c, 1 - c, 2 + c, 3 - 2 * c)
     halves = [split(v_ref[:, pl.ds(pl.multiple_of(o * WIDE, WIDE), WIDE)]) for o in order]
     for at, (i, j) in enumerate(LOCAL):
         block = dot3(halves[i], halves[j], TN)
         start = STARTS[at]
         for h, count in enumerate(SENT[at]):
-            rows = pl.ds(start, count)
-            part = block[:count, h * 128 : (h + 1) * 128]
-            g_ref[rows, :] = part + refs[0][rows, :] if len(refs) == 2 else part
+            yield pl.ds(start, count), block[:count, h * 128 : (h + 1) * 128]
             start += count
 
 
-def gram(core, panels, *before):
+def gram_kernel(core, v_ref, g_ref):
+    for rows, part in gram_blocks(core, v_ref):
+        g_ref[rows, :] = part
+
+
+def gram_more_kernel(core, v_ref, before_ref, g_hbm, g_ref, sems):
+    copies = []
+    for rows, part in gram_blocks(core, v_ref):
+        g_ref[rows, :] = before_ref[rows, :] + part
+        copies.append(pltpu.make_async_copy(g_ref.at[rows], g_hbm.at[rows], sems.at[len(copies)]))
+        copies[-1].start()
+    for copy in copies:
+        copy.wait()
+
+
+def gram(core, panels):
     return pl.pallas_call(
         gram_kernel,
         out_shape=jax.ShapeDtypeStruct((STARTS[-1], 128), F32),
-        in_specs=[smem(), vmem()] + [vmem()] * len(before),
-        out_specs=vmem(),
+        in_specs=[smem(), vmem()],
+        out_specs=vmem(),
+        compiler_params=params(),
+        cost_estimate=pl.CostEstimate(flops=10**9, bytes_accessed=3 << 20, transcendentals=0),
+        name="gram",
+    )(core, panels)
+
+
+def gram_more(core, panels, before):
+    return pl.pallas_call(
+        gram_more_kernel,
+        out_shape=jax.ShapeDtypeStruct((STARTS[-1], 128), F32),
+        in_specs=[smem(), vmem(), vmem()],
+        out_specs=hbm(),
+        scratch_shapes=[
+            pltpu.VMEM((STARTS[-1], 128), F32),
+            pltpu.SemaphoreType.DMA((2 * len(LOCAL),)),
+        ],
         compiler_params=params(),
         cost_estimate=pl.CostEstimate(flops=10**9, bytes_accessed=4 << 20, transcendentals=0),
-        name="gram",
-    )(core, panels, *before)
+        name="gram_more",
+    )(core, panels, before)
 
 
 def gram_block(ref, local):
@@ -338,10 +366,25 @@
     return jnp.concatenate([ref[pl.ds(j * 4 + r, 64, stride=stride), :] for r in range(4)], axis=0)
 
 
-def project_kernel(core, e_ref, own_ref, other_ref, p_ref, half_ref):
+def compact_kernel(e_ref, half_ref):
     stride = 32 + SHARE
     for s in range(64):
         half_ref[s * SHARE : (s + 1) * SHARE, :] = e_ref[s * stride + 32 : (s + 1) * stride, :]
+
+
+def compact(e):
+    return pl.pallas_call(
+        compact_kernel,
+        out_shape=jax.ShapeDtypeStruct((STARTS[-1], 128), F32),
+        in_specs=[vmem()],
+        out_specs=vmem(),
+        compiler_params=params(),
+        cost_estimate=pl.CostEstimate(flops=0, bytes_accessed=2 << 20, transcendentals=0),
+        name="compact",
+    )(e)
+
+
+def project_kernel(core, e_ref, own_ref, other_ref, p_ref):
     c = core[0]
     sides = [
         (split(jnp.concatenate([rows_of(e_ref, first + k) for k in range(4)], axis=1)), v_ref)
@@ -359,9 +402,9 @@
 def project(core, e, own, other):
     return pl.pallas_call(
         project_kernel,
-        out_shape=[jax.ShapeDtypeStruct((rows, 128), F32) for rows in (2048, STARTS[-1])],
+        out_shape=jax.ShapeDtypeStruct((2048, 128), F32),
         in_specs=[smem(), vmem(), vmem(), vmem()],
-        out_specs=[vmem()] * 2,
+        out_specs=vmem(),
         compiler_params=params(),
         cost_estimate=pl.CostEstimate(flops=2 * 10**9, bytes_accessed=6 << 20, transcendentals=0),
         name="project",
@@ -412,20 +455,21 @@
 def body(eigvecs, reflectors, offsets, lengths, panels):
     core = lax.axis_index("c").astype(jnp.int32).reshape(1)
     other = swap_cores(panels)
-    parts = to_chips(gram(core, other, gram(core, panels)).reshape(64, SHARE // 4, 4, 128))
+    parts = to_chips(gram_more(core, other, gram(core, panels)).reshape(64, SHARE // 4, 4, 128))
     tiles = eigvecs.reshape(4, 512, 128).transpose(1, 0, 2)
     chased = chase(tiles, reflectors, offsets, lengths)
     mine = to_chips(share(chased.reshape(64, 8, 4, 128), parts)).reshape(64 * (32 + SHARE), 128)
-    projected, half = project(core, mine, panels, other)
-    projected = to_chips(projected.reshape(64, 32, 128))
-    weights = to_chips(solve(core, half, swap_cores(half), projected)).reshape(2048, 128)
+    half = compact(mine)
+    theirs = swap_cores(half)
+    projected = to_chips(project(core, mine, panels, other).reshape(64, 32, 128))
+    weights = to_chips(solve(core, half, theirs, projected)).reshape(2048, 128)
     result = to_chips(update(core, mine, weights, panels, other).reshape(64, 32, 128))
     return pl.pallas_call(
         finish_kernel,
         out_shape=jax.ShapeDtypeStruct((4, 65536), F32),
-        grid=(4,),
+        grid=(2,),
         in_specs=[vmem()],
-        out_specs=pl.BlockSpec((4, 16384), lambda i: (0, i)),
+        out_specs=pl.BlockSpec((4, 32768), lambda i: (0, i)),
         compiler_params=params(),
         cost_estimate=pl.CostEstimate(flops=0, bytes_accessed=2 << 20, transcendentals=0),
         name="finish",

time: 160 us -> 158 us (0.988)
  blocking collectives: 108 us -> 106 us
    all_to_all x4, blocking collectives: 108 us -> 106 us  [to_chips(): return lax.all_to_all(a, CHIPS, split_axis=0, concat_axis=0, tiled=True)]
    pallas_call x2 -> x1, Pallas kernels: 3.64 us -> 1.3 us  [gram(): pl.pallas_call(gram_kernel, out_shape=jax.ShapeDtypeStruct((STARTS[-1], 1...]
    pallas_call x1 -> x3, Pallas kernels: 2.5 us -> 4.62 us  [the longest x1 2.4 us: project(): pl.pallas_call(project_kernel, out_shape=jax.ShapeDtypeStruct((2048, 128)...]
  transfers between devices with their start and end apart: 3 -> 3, of which waited for: 2 -> 2; matrix products, arithmetic and copies ran while one was open for 0% -> 0% of each run, Pallas kernels for 11% -> 12%
where the time goes in v9:
time: 158 us; the launch traced here: 157 us
  blocking collectives  106 us (67%)
  Pallas kernels  29.8 us (19%)
  starting transfers between devices  11.8 us (7%)
  waiting for transfers between devices  5.74 us (4%)
  local copies, waits for them, and re-layouts  4.22 us (3%)
    all_to_all x4, blocking collectives, to_chips(): return lax.all_to_all(a, CHIPS, split_axis=0, concat_axis=0, tiled=True)  106 us
    pallas_call x1, Pallas kernels, chase(): pl.pallas_call(chase_kernel, out_shape=jax.ShapeDtypeStruct(tiles.shape,...  15.7 us
    all_to_all x1, starting transfers between devices, to_chips(): return lax.all_to_all(a, CHIPS, split_axis=0, concat_axis=0, tiled=True)  11.7 us
    all_to_all x1, waiting for transfers between devices, to_chips(): return lax.all_to_all(a, CHIPS, split_axis=0, concat_axis=0, tiled=True)  4.27 us
    unnamed x6, local copies, waits for them, and re-layouts  4.22 us
    pallas_call x1, Pallas kernels, solve(): pl.pallas_call(solve_kernel, out_shape=jax.ShapeDtypeStruct(p.shape, F32)...  3.67 us
  transfers between devices with their start and end apart: 3, of which 2 were waited for; matrix products, arithmetic and copies ran while one was open for 0% of the time, Pallas kernels for 12%

profile of v9, /device:TPU:0, one launch (start us, length us, event | category | flops | bytes accessed | tf_op | source)
XLA Modules:
  0.0 157.2 jit_solution(11420582955228679225)
XLA Ops:
  0.0 0.0 collective-permute-start
  0.0 0.0 copy-start
  0.0 1.6 %copy-done = f32[512,1024]{1,0:T(8,128)S(1)} copy-done((f32[512,1024]{1,0:T(8,128)S(1)}, f32[512,1024]{1,0:T(8,128)}, u32[]{:S(2)}) %copy-start) | copy-done | bytes 2097176
  1.6 1.3 gram.1.before_ref
  2.9 1.5 collective-permute-done.v_ref.other_ref
  4.4 2.1 %gram_more.1 = f32[2304,128]{1,0:T(8,128)} custom-call(s32[1]{0:T(128)} %bitcast.core, f32[512,1024]{1,0:T(8,128)S(1)} %collective-permute-done.v_ref.other_ref, f32[2304,128]{1,0:T(8,128)S(1)} %gram.1.before_ref), custom_call_target="tpu_custom_call" | custom-call | flops 1000000000 | bytes 4194304 | tf_op jit(solution)/shard_map/gram_more/pallas_call | solution.py:282
  6.5 11.7 %all-to-all-start = ((f32[64,9,4,128]{3,2,1,0:T(4,128)}), f32[64,9,4,128]{3,2,1,0:T(4,128)S(1)}, u32[]{:S(2)}, u32[]{:S(2)}) async-start(f32[64,9,4,128]{3,2,1,0:T(4,128)} %bitcast.4), calls=%async_computation | async-start | bytes 2359296 | tf_op jit(solution)/shard_map/all_to_all | solution.py:448
  18.2 15.7 %chase.1 = f32[512,4,128]{2,1,0:T(4,128)} custom-call(s32[24]{0:T(128)} %offsets.1, s32[24]{0:T(128)} %lengths.1, f32[512,4,128]{2,1,0:T(4,128)} %bitcast.19, f32[24,256,128]{2,1,0:T(8,128)} %m_hbm.1), custom_call_target="tpu_custom_call" | custom-call | flops 20000000000 | bytes 7340032 | tf_op jit(solution)/shard_map/chase/pallas_call | solution.py:206
  33.9 4.3 %all-to-all-done.g_ref = f32[64,9,4,128]{3,2,1,0:T(4,128)S(1)} async-done(((f32[64,9,4,128]{3,2,1,0:T(4,128)}), f32[64,9,4,128]{3,2,1,0:T(4,128)S(1)}, u32[]{:S(2)}, u32[]{:S(2)}) %all-to-all-start) | async-done | bytes 1179680 | tf_op jit(solution)/shard_map/all_to_all | solution.py:448
  38.2 0.0 copy-start.2
  38.2 1.2 copy-done.2
  39.4 0.4 share.1
  39.8 37.2 %all_to_all.25 = f32[64,17,4,128]{3,2,1,0:T(4,128)S(1)} all-to-all(f32[64,17,4,128]{3,2,1,0:T(4,128)S(1)} %share.1), channel_id=1, replica_groups=mesh['yh'=2,'x'=4,'yl'=2,'z'=4,'c'=2] {'yh','x','yl','z'}, dimensions={0} | all-to-all | bytes 4456448 | tf_op jit(solution)/shard_map/all_to_all | solution.py:448
  77.0 0.0 copy-start.1
  77.0 0.1 compact.1.own_ref
  77.1 0.1 collective-permute-start.1
  77.2 1.4 copy-done.1
  78.6 2.4 %project.1 = f32[2048,128]{1,0:T(8,128)S(1)} custom-call(s32[1]{0:T(128)} %bitcast.core, f32[4352,128]{1,0:T(8,128)S(1)} %bitcast.12, f32[512,1024]{1,0:T(8,128)S(1)} %copy-done.1, f32[512,1024]{1,0:T(8,128)S(1)} %collective-permute-done.v_ref.other_ref), custom_call_target="tpu_custom_call" | custom-call | flops 2000000000 | bytes 6291456 | tf_op jit(solution)/shard_map/project/pallas_call | solution.py:403
  81.0 24.4 %all_to_all.26.p_ref = f32[64,32,128]{2,1,0:T(8,128)S(1)} all-to-all(f32[64,32,128]{2,1,0:T(8,128)S(1)} %bitcast.17), channel_id=1, replica_groups=mesh['yh'=2,'x'=4,'yl'=2,'z'=4,'c'=2] {'yh','x','yl','z'}, dimensions={0} | all-to-all | bytes 2097152 | tf_op jit(solution)/shard_map/all_to_all | solution.py:448
  105.4 0.0 collective-permute-done.1.other_ref
  105.4 3.7 %solve.1 = f32[64,32,128]{2,1,0:T(8,128)S(1)} custom-call(s32[1]{0:T(128)} %bitcast.core, f32[2304,128]{1,0:T(8,128)S(1)} %compact.1.own_ref, f32[2304,128]{1,0:T(8,128)S(1)} %collective-permute-done.1.other_ref, f32[64,32,128]{2,1,0:T(8,128)S(1)} %all_to_all.26.p_ref), custom_call_target="tpu_custom_call" | custom-call | flops 4000000000 | bytes 5242880 | tf_op jit(solution)/shard_map/solve/pallas_call | solution.py:353
  109.1 22.0 %all_to_all.27 = f32[64,32,128]{2,1,0:T(8,128)S(1)} all-to-all(f32[64,32,128]{2,1,0:T(8,128)S(1)} %solve.1), channel_id=1, replica_groups=mesh['yh'=2,'x'=4,'yl'=2,'z'=4,'c'=2] {'yh','x','yl','z'}, dimensions={0} | all-to-all | bytes 2097152 | tf_op jit(solution)/shard_map/all_to_all | solution.py:448
  131.1 3.1 %update.1 = f32[2048,128]{1,0:T(8,128)S(1)} custom-call(s32[1]{0:T(128)} %bitcast.core, f32[4352,128]{1,0:T(8,128)S(1)} %bitcast.13, f32[2048,128]{1,0:T(8,128)S(1)} %bitcast.14, f32[512,1024]{1,0:T(8,128)S(1)} %copy-done.1, f32[512,1024]{1,0:T(8,128)S(1)} %collective-permute-done.v_ref.other_ref), custom_call_target="tpu_custom_call" | custom-call | flops 2000000000 | bytes 7340032 | tf_op jit(solution)/shard_map/update/pallas_call | solution.py:429
  134.2 22.0 %all_to_all.28 = f32[64,32,128]{2,1,0:T(8,128)S(1)} all-to-all(f32[64,32,128]{2,1,0:T(8,128)S(1)} %bitcast.15), channel_id=1, replica_groups=mesh['yh'=2,'x'=4,'yl'=2,'z'=4,'c'=2] {'yh','x','yl','z'}, dimensions={0} | all-to-all | bytes 2097152 | tf_op jit(solution)/shard_map/all_to_all | solution.py:448
  156.2 1.0 finish.1
Async XLA Ops:
  0.0 4.4 %collective-permute-start = (f32[512,1024]{1,0:T(8,128)}, f32[512,1024]{1,0:T(8,128)S(1)}, u32[]{:S(2)}, u32[]{:S(2)}) collective-permute-start(f32[512,1024]{1,0:T(8,128)} %own_ref.3), channel_id=1, source_target_pairs={{0,1},{1,0},{2,3},{3,2},{4,5},{5,4},{6,7},{7,6},{8,9},{9,8},{10,11... | collective-permute-start | bytes 6291464 | tf_op jit(solution)/shard_map/ppermute | solution.py:452
  0.0 1.6 %copy-start = (f32[512,1024]{1,0:T(8,128)S(1)}, f32[512,1024]{1,0:T(8,128)}, u32[]{:S(2)}) copy-start(f32[512,1024]{1,0:T(8,128)} %own_ref.3) | copy-start | bytes 6291460
  6.5 31.7 %all-to-all-start = ((f32[64,9,4,128]{3,2,1,0:T(4,128)}), f32[64,9,4,128]{3,2,1,0:T(4,128)S(1)}, u32[]{:S(2)}, u32[]{:S(2)}) async-start(f32[64,9,4,128]{3,2,1,0:T(4,128)} %bitcast.4), calls=%async_computation | async-start | bytes 2359296 | tf_op jit(solution)/shard_map/all_to_all | solution.py:448
  38.2 1.2 copy-start.2
  77.0 1.6 %copy-start.1 = (f32[512,1024]{1,0:T(8,128)S(1)}, f32[512,1024]{1,0:T(8,128)}, u32[]{:S(2)}) copy-start(f32[512,1024]{1,0:T(8,128)} %own_ref.3) | copy-start | bytes 6291460
  77.1 28.3 %collective-permute-start.1 = (f32[2304,128]{1,0:T(8,128)S(1)}, f32[2304,128]{1,0:T(8,128)S(1)}, u32[]{:S(2)}, u32[]{:S(2)}) collective-permute-start(f32[2304,128]{1,0:T(8,128)S(1)} %compact.1.own_ref), channel_id=1, source_target_pairs={{0,1},{1,0},{2,3},{3,2},{4,5},{5,4},{6,7},{7,6},{8,9},{9,8},{10,11... | collective-permute-start | bytes 3538952 | tf_op jit(solution)/shard_map/ppermute | solution.py:452

commit v10 on v9

--- a/solution.py
+++ b/solution.py
@@ -366,22 +366,22 @@
     return jnp.concatenate([ref[pl.ds(j * 4 + r, 64, stride=stride), :] for r in range(4)], axis=0)
 
 
-def compact_kernel(e_ref, half_ref):
+def compact_kernel(e_ref, own_ref, half_ref):
     stride = 32 + SHARE
     for s in range(64):
         half_ref[s * SHARE : (s + 1) * SHARE, :] = e_ref[s * stride + 32 : (s + 1) * stride, :]
 
 
-def compact(e):
+def compact(e, own):
     return pl.pallas_call(
         compact_kernel,
         out_shape=jax.ShapeDtypeStruct((STARTS[-1], 128), F32),
-        in_specs=[vmem()],
-        out_specs=vmem(),
-        compiler_params=params(),
-        cost_estimate=pl.CostEstimate(flops=0, bytes_accessed=2 << 20, transcendentals=0),
+        in_specs=[vmem()] * 2,
+        out_specs=vmem(),
+        compiler_params=params(),
+        cost_estimate=pl.CostEstimate(flops=0, bytes_accessed=6 << 20, transcendentals=0),
         name="compact",
-    )(e)
+    )(e, own)
 
 
 def project_kernel(core, e_ref, own_ref, other_ref, p_ref):
@@ -459,7 +459,7 @@
     tiles = eigvecs.reshape(4, 512, 128).transpose(1, 0, 2)
     chased = chase(tiles, reflectors, offsets, lengths)
     mine = to_chips(share(chased.reshape(64, 8, 4, 128), parts)).reshape(64 * (32 + SHARE), 128)
-    half = compact(mine)
+    half = compact(mine, panels)
     theirs = swap_cores(half)
     projected = to_chips(project(core, mine, panels, other).reshape(64, 32, 128))
     weights = to_chips(solve(core, half, theirs, projected)).reshape(2048, 128)

time: 158 us -> 159 us (level)
  blocking collectives: 106 us -> 109 us
    all_to_all x4, blocking collectives: 106 us -> 109 us  [to_chips(): return lax.all_to_all(a, CHIPS, split_axis=0, concat_axis=0, tiled=True)]
where the time goes in v10:
time: 159 us
  blocking collectives  109 us (69%)
  Pallas kernels  29.8 us (19%)
  starting transfers between devices  11.8 us (7%)
  waiting for transfers between devices  5.74 us (4%)
  local copies, waits for them, and re-layouts  2.82 us (2%)
    all_to_all x4, blocking collectives, to_chips(): return lax.all_to_all(a, CHIPS, split_axis=0, concat_axis=0, tiled=True)  109 us
    pallas_call x1, Pallas kernels, chase(): pl.pallas_call(chase_kernel, out_shape=jax.ShapeDtypeStruct(tiles.shape,...  15.7 us
    all_to_all x1, starting transfers between devices, to_chips(): return lax.all_to_all(a, CHIPS, split_axis=0, concat_axis=0, tiled=True)  11.7 us
    all_to_all x1, waiting for transfers between devices, to_chips(): return lax.all_to_all(a, CHIPS, split_axis=0, concat_axis=0, tiled=True)  4.26 us
    pallas_call x1, Pallas kernels, solve(): pl.pallas_call(solve_kernel, out_shape=jax.ShapeDtypeStruct(p.shape, F32)...  3.67 us
  transfers between devices with their start and end apart: 3, of which 2 were waited for; matrix products, arithmetic and copies ran while one was open for 0% of the time, Pallas kernels for 12%

profile of v10, /device:TPU:0, one launch (start us, length us, event | category | flops | bytes accessed | tf_op | source)
XLA Modules:
  0.0 158.7 jit_solution(13547890011996657019)
XLA Ops:
  0.0 0.0 collective-permute-start
  0.0 0.0 copy-start
  0.0 1.6 %copy-done = f32[512,1024]{1,0:T(8,128)S(1)} copy-done((f32[512,1024]{1,0:T(8,128)S(1)}, f32[512,1024]{1,0:T(8,128)}, u32[]{:S(2)}) %copy-start) | copy-done | bytes 2097176
  1.6 1.3 gram.1.before_ref
  2.9 1.5 collective-permute-done.v_ref.other_ref
  4.4 2.1 %gram_more.1 = f32[2304,128]{1,0:T(8,128)} custom-call(s32[1]{0:T(128)} %bitcast.core, f32[512,1024]{1,0:T(8,128)S(1)} %collective-permute-done.v_ref.other_ref, f32[2304,128]{1,0:T(8,128)S(1)} %gram.1.before_ref), custom_call_target="tpu_custom_call" | custom-call | flops 1000000000 | bytes 4194304 | tf_op jit(solution)/shard_map/gram_more/pallas_call | solution.py:282
  6.5 11.7 %all-to-all-start = ((f32[64,9,4,128]{3,2,1,0:T(4,128)}), f32[64,9,4,128]{3,2,1,0:T(4,128)S(1)}, u32[]{:S(2)}, u32[]{:S(2)}) async-start(f32[64,9,4,128]{3,2,1,0:T(4,128)} %bitcast.4), calls=%async_computation | async-start | bytes 2359296 | tf_op jit(solution)/shard_map/all_to_all | solution.py:448
  18.2 15.7 %chase.1 = f32[512,4,128]{2,1,0:T(4,128)} custom-call(s32[24]{0:T(128)} %offsets.1, s32[24]{0:T(128)} %lengths.1, f32[512,4,128]{2,1,0:T(4,128)} %bitcast.19, f32[24,256,128]{2,1,0:T(8,128)} %m_hbm.1), custom_call_target="tpu_custom_call" | custom-call | flops 20000000000 | bytes 7340032 | tf_op jit(solution)/shard_map/chase/pallas_call | solution.py:206
  34.0 4.3 %all-to-all-done.g_ref = f32[64,9,4,128]{3,2,1,0:T(4,128)S(1)} async-done(((f32[64,9,4,128]{3,2,1,0:T(4,128)}), f32[64,9,4,128]{3,2,1,0:T(4,128)S(1)}, u32[]{:S(2)}, u32[]{:S(2)}) %all-to-all-start) | async-done | bytes 1179680 | tf_op jit(solution)/shard_map/all_to_all | solution.py:448
  38.2 0.0 copy-start.2
  38.2 1.2 copy-done.2
  39.4 0.4 share.1
  39.8 0.0 copy-start.1
  39.8 37.3 %all_to_all.25 = f32[64,17,4,128]{3,2,1,0:T(4,128)S(1)} all-to-all(f32[64,17,4,128]{3,2,1,0:T(4,128)S(1)} %share.1), channel_id=1, replica_groups=mesh['yh'=2,'x'=4,'yl'=2,'z'=4,'c'=2] {'yh','x','yl','z'}, dimensions={0} | all-to-all | bytes 4456448 | tf_op jit(solution)/shard_map/all_to_all | solution.py:448
  77.1 0.0 copy-done.1
  77.1 0.1 compact.1.own_ref
  77.2 0.1 collective-permute-start.1
  77.3 2.4 %project.1 = f32[2048,128]{1,0:T(8,128)S(1)} custom-call(s32[1]{0:T(128)} %bitcast.core, f32[4352,128]{1,0:T(8,128)S(1)} %bitcast.12, f32[512,1024]{1,0:T(8,128)S(1)} %copy-done.1, f32[512,1024]{1,0:T(8,128)S(1)} %collective-permute-done.v_ref.other_ref), custom_call_target="tpu_custom_call" | custom-call | flops 2000000000 | bytes 6291456 | tf_op jit(solution)/shard_map/project/pallas_call | solution.py:403
  79.7 25.8 %all_to_all.26.p_ref = f32[64,32,128]{2,1,0:T(8,128)S(1)} all-to-all(f32[64,32,128]{2,1,0:T(8,128)S(1)} %bitcast.17), channel_id=1, replica_groups=mesh['yh'=2,'x'=4,'yl'=2,'z'=4,'c'=2] {'yh','x','yl','z'}, dimensions={0} | all-to-all | bytes 2097152 | tf_op jit(solution)/shard_map/all_to_all | solution.py:448
  105.5 0.0 collective-permute-done.1.other_ref
  105.5 3.7 %solve.1 = f32[64,32,128]{2,1,0:T(8,128)S(1)} custom-call(s32[1]{0:T(128)} %bitcast.core, f32[2304,128]{1,0:T(8,128)S(1)} %compact.1.own_ref, f32[2304,128]{1,0:T(8,128)S(1)} %collective-permute-done.1.other_ref, f32[64,32,128]{2,1,0:T(8,128)S(1)} %all_to_all.26.p_ref), custom_call_target="tpu_custom_call" | custom-call | flops 4000000000 | bytes 5242880 | tf_op jit(solution)/shard_map/solve/pallas_call | solution.py:353
  109.2 23.4 %all_to_all.27 = f32[64,32,128]{2,1,0:T(8,128)S(1)} all-to-all(f32[64,32,128]{2,1,0:T(8,128)S(1)} %solve.1), channel_id=1, replica_groups=mesh['yh'=2,'x'=4,'yl'=2,'z'=4,'c'=2] {'yh','x','yl','z'}, dimensions={0} | all-to-all | bytes 2097152 | tf_op jit(solution)/shard_map/all_to_all | solution.py:448
  132.6 3.1 %update.1 = f32[2048,128]{1,0:T(8,128)S(1)} custom-call(s32[1]{0:T(128)} %bitcast.core, f32[4352,128]{1,0:T(8,128)S(1)} %bitcast.13, f32[2048,128]{1,0:T(8,128)S(1)} %bitcast.14, f32[512,1024]{1,0:T(8,128)S(1)} %copy-done.1, f32[512,1024]{1,0:T(8,128)S(1)} %collective-permute-done.v_ref.other_ref), custom_call_target="tpu_custom_call" | custom-call | flops 2000000000 | bytes 7340032 | tf_op jit(solution)/shard_map/update/pallas_call | solution.py:429
  135.7 22.0 %all_to_all.28 = f32[64,32,128]{2,1,0:T(8,128)S(1)} all-to-all(f32[64,32,128]{2,1,0:T(8,128)S(1)} %bitcast.15), channel_id=1, replica_groups=mesh['yh'=2,'x'=4,'yl'=2,'z'=4,'c'=2] {'yh','x','yl','z'}, dimensions={0} | all-to-all | bytes 2097152 | tf_op jit(solution)/shard_map/all_to_all | solution.py:448
  157.7 1.0 finish.1
Async XLA Ops:
  0.0 4.4 %collective-permute-start = (f32[512,1024]{1,0:T(8,128)}, f32[512,1024]{1,0:T(8,128)S(1)}, u32[]{:S(2)}, u32[]{:S(2)}) collective-permute-start(f32[512,1024]{1,0:T(8,128)} %own_ref.5), channel_id=1, source_target_pairs={{0,1},{1,0},{2,3},{3,2},{4,5},{5,4},{6,7},{7,6},{8,9},{9,8},{10,11... | collective-permute-start | bytes 6291464 | tf_op jit(solution)/shard_map/ppermute | solution.py:452
  0.0 1.6 %copy-start = (f32[512,1024]{1,0:T(8,128)S(1)}, f32[512,1024]{1,0:T(8,128)}, u32[]{:S(2)}) copy-start(f32[512,1024]{1,0:T(8,128)} %own_ref.5) | copy-start | bytes 6291460
  6.5 31.7 %all-to-all-start = ((f32[64,9,4,128]{3,2,1,0:T(4,128)}), f32[64,9,4,128]{3,2,1,0:T(4,128)S(1)}, u32[]{:S(2)}, u32[]{:S(2)}) async-start(f32[64,9,4,128]{3,2,1,0:T(4,128)} %bitcast.4), calls=%async_computation | async-start | bytes 2359296 | tf_op jit(solution)/shard_map/all_to_all | solution.py:448
  38.2 1.2 copy-start.2
  39.8 37.3 %copy-start.1 = (f32[512,1024]{1,0:T(8,128)S(1)}, f32[512,1024]{1,0:T(8,128)}, u32[]{:S(2)}) copy-start(f32[512,1024]{1,0:T(8,128)} %own_ref.5) | copy-start | bytes 6291460
  77.2 28.3 %collective-permute-start.1 = (f32[2304,128]{1,0:T(8,128)S(1)}, f32[2304,128]{1,0:T(8,128)S(1)}, u32[]{:S(2)}, u32[]{:S(2)}) collective-permute-start(f32[2304,128]{1,0:T(8,128)S(1)} %compact.1.own_ref), channel_id=1, source_target_pairs={{0,1},{1,0},{2,3},{3,2},{4,5},{5,4},{6,7},{7,6},{8,9},{9,8},{10,11... | collective-permute-start | bytes 3538952 | tf_op jit(solution)/shard_map/ppermute | solution.py:452

commit v11 on v10

--- a/solution.py
+++ b/solution.py
@@ -461,7 +461,8 @@
     mine = to_chips(share(chased.reshape(64, 8, 4, 128), parts)).reshape(64 * (32 + SHARE), 128)
     half = compact(mine, panels)
     theirs = swap_cores(half)
-    projected = to_chips(project(core, mine, panels, other).reshape(64, 32, 128))
+    projected, theirs = lax.optimization_barrier((project(core, mine, panels, other), theirs))
+    projected = to_chips(projected.reshape(64, 32, 128))
     weights = to_chips(solve(core, half, theirs, projected)).reshape(2048, 128)
     result = to_chips(update(core, mine, weights, panels, other).reshape(64, 32, 128))
     return pl.pallas_call(

time: 159 us -> 159 us (level)
  transfers between devices with their start and end apart: 3 -> 3, of which waited for: 2 -> 3; matrix products, arithmetic and copies ran while one was open for 0% -> 0% of each run, Pallas kernels for 12% -> 12%
where the time goes in v11:
time: 159 us; the launch traced here: 158 us
  blocking collectives  108 us (68%)
  Pallas kernels  29.8 us (19%)
  starting transfers between devices  11.8 us (7%)
  waiting for transfers between devices  6.16 us (4%)
  local copies, waits for them, and re-layouts  2.82 us (2%)
    all_to_all x4, blocking collectives, to_chips(): return lax.all_to_all(a, CHIPS, split_axis=0, concat_axis=0, tiled=True)  108 us
    pallas_call x1, Pallas kernels, chase(): pl.pallas_call(chase_kernel, out_shape=jax.ShapeDtypeStruct(tiles.shape,...  15.7 us
    all_to_all x1, starting transfers between devices, to_chips(): return lax.all_to_all(a, CHIPS, split_axis=0, concat_axis=0, tiled=True)  11.7 us
    all_to_all x1, waiting for transfers between devices, to_chips(): return lax.all_to_all(a, CHIPS, split_axis=0, concat_axis=0, tiled=True)  4.26 us
    pallas_call x1, Pallas kernels, solve(): pl.pallas_call(solve_kernel, out_shape=jax.ShapeDtypeStruct(p.shape, F32)...  3.67 us
  transfers between devices with their start and end apart: 3, of which 3 were waited for; matrix products, arithmetic and copies ran while one was open for 0% of the time, Pallas kernels for 12%

profile of v11, /device:TPU:0, one launch (start us, length us, event | category | flops | bytes accessed | tf_op | source)
XLA Modules:
  0.0 158.4 jit_solution(17405057700448917755)
XLA Ops:
  0.0 0.0 collective-permute-start
  0.0 0.0 copy-start
  0.0 1.6 %copy-done = f32[512,1024]{1,0:T(8,128)S(1)} copy-done((f32[512,1024]{1,0:T(8,128)S(1)}, f32[512,1024]{1,0:T(8,128)}, u32[]{:S(2)}) %copy-start) | copy-done | bytes 2097176
  1.6 1.3 gram.1.before_ref
  2.9 1.5 collective-permute-done.v_ref.other_ref
  4.4 2.1 %gram_more.1 = f32[2304,128]{1,0:T(8,128)} custom-call(s32[1]{0:T(128)} %bitcast.core, f32[512,1024]{1,0:T(8,128)S(1)} %collective-permute-done.v_ref.other_ref, f32[2304,128]{1,0:T(8,128)S(1)} %gram.1.before_ref), custom_call_target="tpu_custom_call" | custom-call | flops 1000000000 | bytes 4194304 | tf_op jit(solution)/shard_map/gram_more/pallas_call | solution.py:282
  6.5 11.7 %all-to-all-start = ((f32[64,9,4,128]{3,2,1,0:T(4,128)}), f32[64,9,4,128]{3,2,1,0:T(4,128)S(1)}, u32[]{:S(2)}, u32[]{:S(2)}) async-start(f32[64,9,4,128]{3,2,1,0:T(4,128)} %bitcast.4), calls=%async_computation | async-start | bytes 2359296 | tf_op jit(solution)/shard_map/all_to_all | solution.py:448
  18.2 15.7 %chase.1 = f32[512,4,128]{2,1,0:T(4,128)} custom-call(s32[24]{0:T(128)} %offsets.1, s32[24]{0:T(128)} %lengths.1, f32[512,4,128]{2,1,0:T(4,128)} %bitcast.19, f32[24,256,128]{2,1,0:T(8,128)} %m_hbm.1), custom_call_target="tpu_custom_call" | custom-call | flops 20000000000 | bytes 7340032 | tf_op jit(solution)/shard_map/chase/pallas_call | solution.py:206
  34.0 4.3 %all-to-all-done.g_ref = f32[64,9,4,128]{3,2,1,0:T(4,128)S(1)} async-done(((f32[64,9,4,128]{3,2,1,0:T(4,128)}), f32[64,9,4,128]{3,2,1,0:T(4,128)S(1)}, u32[]{:S(2)}, u32[]{:S(2)}) %all-to-all-start) | async-done | bytes 1179680 | tf_op jit(solution)/shard_map/all_to_all | solution.py:448
  38.2 0.0 copy-start.2
  38.2 1.2 copy-done.2
  39.4 0.4 share.1
  39.8 0.0 copy-start.1
  39.8 37.3 %all_to_all.25 = f32[64,17,4,128]{3,2,1,0:T(4,128)S(1)} all-to-all(f32[64,17,4,128]{3,2,1,0:T(4,128)S(1)} %share.1), channel_id=1, replica_groups=mesh['yh'=2,'x'=4,'yl'=2,'z'=4,'c'=2] {'yh','x','yl','z'}, dimensions={0} | all-to-all | bytes 4456448 | tf_op jit(solution)/shard_map/all_to_all | solution.py:448
  77.1 0.0 copy-done.1
  77.1 0.1 compact.1.own_ref
  77.2 0.1 collective-permute-start.1
  77.3 2.4 %project.1 = f32[2048,128]{1,0:T(8,128)S(1)} custom-call(s32[1]{0:T(128)} %bitcast.core, f32[4352,128]{1,0:T(8,128)S(1)} %bitcast.12, f32[512,1024]{1,0:T(8,128)S(1)} %copy-done.1, f32[512,1024]{1,0:T(8,128)S(1)} %collective-permute-done.v_ref.other_ref), custom_call_target="tpu_custom_call" | custom-call | flops 2000000000 | bytes 6291456 | tf_op jit(solution)/shard_map/project/pallas_call | solution.py:403
  79.7 0.4 collective-permute-done.1.other_ref
  80.1 25.5 %all_to_all.26.p_ref = f32[64,32,128]{2,1,0:T(8,128)S(1)} all-to-all(f32[64,32,128]{2,1,0:T(8,128)S(1)} %bitcast.17), channel_id=1, replica_groups=mesh['yh'=2,'x'=4,'yl'=2,'z'=4,'c'=2] {'yh','x','yl','z'}, dimensions={0} | all-to-all | bytes 2097152 | tf_op jit(solution)/shard_map/all_to_all | solution.py:448
  105.6 3.7 %solve.1 = f32[64,32,128]{2,1,0:T(8,128)S(1)} custom-call(s32[1]{0:T(128)} %bitcast.core, f32[2304,128]{1,0:T(8,128)S(1)} %compact.1.own_ref, f32[2304,128]{1,0:T(8,128)S(1)} %collective-permute-done.1.other_ref, f32[64,32,128]{2,1,0:T(8,128)S(1)} %all_to_all.26.p_ref), custom_call_target="tpu_custom_call" | custom-call | flops 4000000000 | bytes 5242880 | tf_op jit(solution)/shard_map/solve/pallas_call | solution.py:353
  109.3 23.0 %all_to_all.27 = f32[64,32,128]{2,1,0:T(8,128)S(1)} all-to-all(f32[64,32,128]{2,1,0:T(8,128)S(1)} %solve.1), channel_id=1, replica_groups=mesh['yh'=2,'x'=4,'yl'=2,'z'=4,'c'=2] {'yh','x','yl','z'}, dimensions={0} | all-to-all | bytes 2097152 | tf_op jit(solution)/shard_map/all_to_all | solution.py:448
  132.3 3.1 %update.1 = f32[2048,128]{1,0:T(8,128)S(1)} custom-call(s32[1]{0:T(128)} %bitcast.core, f32[4352,128]{1,0:T(8,128)S(1)} %bitcast.13, f32[2048,128]{1,0:T(8,128)S(1)} %bitcast.14, f32[512,1024]{1,0:T(8,128)S(1)} %copy-done.1, f32[512,1024]{1,0:T(8,128)S(1)} %collective-permute-done.v_ref.other_ref), custom_call_target="tpu_custom_call" | custom-call | flops 2000000000 | bytes 7340032 | tf_op jit(solution)/shard_map/update/pallas_call | solution.py:429
  135.4 22.0 %all_to_all.28 = f32[64,32,128]{2,1,0:T(8,128)S(1)} all-to-all(f32[64,32,128]{2,1,0:T(8,128)S(1)} %bitcast.15), channel_id=1, replica_groups=mesh['yh'=2,'x'=4,'yl'=2,'z'=4,'c'=2] {'yh','x','yl','z'}, dimensions={0} | all-to-all | bytes 2097152 | tf_op jit(solution)/shard_map/all_to_all | solution.py:448
  157.4 1.0 finish.1
Async XLA Ops:
  0.0 4.4 %collective-permute-start = (f32[512,1024]{1,0:T(8,128)}, f32[512,1024]{1,0:T(8,128)S(1)}, u32[]{:S(2)}, u32[]{:S(2)}) collective-permute-start(f32[512,1024]{1,0:T(8,128)} %own_ref.5), channel_id=1, source_target_pairs={{0,1},{1,0},{2,3},{3,2},{4,5},{5,4},{6,7},{7,6},{8,9},{9,8},{10,11... | collective-permute-start | bytes 6291464 | tf_op jit(solution)/shard_map/ppermute | solution.py:452
  0.0 1.6 %copy-start = (f32[512,1024]{1,0:T(8,128)S(1)}, f32[512,1024]{1,0:T(8,128)}, u32[]{:S(2)}) copy-start(f32[512,1024]{1,0:T(8,128)} %own_ref.5) | copy-start | bytes 6291460
  6.5 31.7 %all-to-all-start = ((f32[64,9,4,128]{3,2,1,0:T(4,128)}), f32[64,9,4,128]{3,2,1,0:T(4,128)S(1)}, u32[]{:S(2)}, u32[]{:S(2)}) async-start(f32[64,9,4,128]{3,2,1,0:T(4,128)} %bitcast.4), calls=%async_computation | async-start | bytes 2359296 | tf_op jit(solution)/shard_map/all_to_all | solution.py:448
  38.2 1.2 copy-start.2
  39.8 37.3 %copy-start.1 = (f32[512,1024]{1,0:T(8,128)S(1)}, f32[512,1024]{1,0:T(8,128)}, u32[]{:S(2)}) copy-start(f32[512,1024]{1,0:T(8,128)} %own_ref.5) | copy-start | bytes 6291460
  77.2 2.9 %collective-permute-start.1 = (f32[2304,128]{1,0:T(8,128)S(1)}, f32[2304,128]{1,0:T(8,128)S(1)}, u32[]{:S(2)}, u32[]{:S(2)}) collective-permute-start(f32[2304,128]{1,0:T(8,128)S(1)} %compact.1.own_ref), channel_id=1, source_target_pairs={{0,1},{1,0},{2,3},{3,2},{4,5},{5,4},{6,7},{7,6},{8,9},{9,8},{10,11... | collective-permute-start | bytes 3538952 | tf_op jit(solution)/shard_map/ppermute | solution.py:452

commit v12 on v9

--- a/solution.py
+++ b/solution.py
@@ -9,6 +9,8 @@
 BF16 = jnp.bfloat16
 AXES = ("yh", "x", "yl", "z", "c")
 CHIPS = ("yh", "x", "yl", "z")
+STEPS = ("x", "yh", "yl", "z")
+CHIP_AT = [yh * 32 + x * 8 + low for x in range(4) for yh in range(2) for low in range(8)]
 VMEM_LIMIT = 20 * 1024 * 1024
 LARGE = 58 * 1024 * 1024
 
@@ -172,9 +174,15 @@
     store.wait()
 
 
-def share_kernel(e_hbm, g_ref, o_ref, sem):
-    copy = pltpu.make_async_copy(e_hbm, o_ref.at[:, pl.ds(0, 8)], sem)
-    copy.start()
+def share_kernel(e_hbm, g_ref, o_ref, sems):
+    copies = [
+        pltpu.make_async_copy(
+            e_hbm.at[pl.ds(CHIP_AT[k], 8)], o_ref.at[pl.ds(k, 8), pl.ds(0, 8)], sems.at[k // 8]
+        )
+        for k in range(0, 64, 8)
+    ]
+    for copy in copies:
+        copy.start()
     chips, count = g_ref.shape[0], g_ref.shape[1]
     sums = [g_ref[k] for k in range(4)]
     for s in range(4, chips):
@@ -182,7 +190,8 @@
     total = (sums[0] + sums[1]) + (sums[2] + sums[3])
     for s in range(chips):
         o_ref[s, 8:] = total
-    copy.wait()
+    for copy in copies:
+        copy.wait()
 
 
 def vmem():
@@ -223,7 +232,7 @@
         out_shape=jax.ShapeDtypeStruct((64, 8 + SHARE // 4, 4, 128), F32),
         in_specs=[hbm(), vmem()],
         out_specs=vmem(),
-        scratch_shapes=[pltpu.SemaphoreType.DMA],
+        scratch_shapes=[pltpu.SemaphoreType.DMA((8,))],
         compiler_params=pltpu.CompilerParams(vmem_limit_bytes=20 * 1024 * 1024),
         cost_estimate=pl.CostEstimate(flops=10**6, bytes_accessed=5 << 20, transcendentals=0),
         name="share",
@@ -369,7 +378,8 @@
 def compact_kernel(e_ref, half_ref):
     stride = 32 + SHARE
     for s in range(64):
-        half_ref[s * SHARE : (s + 1) * SHARE, :] = e_ref[s * stride + 32 : (s + 1) * stride, :]
+        chip = CHIP_AT[s]
+        half_ref[chip * SHARE : (chip + 1) * SHARE, :] = e_ref[s * stride + 32 : (s + 1) * stride, :]
 
 
 def compact(e):
@@ -439,9 +449,13 @@
 
 def finish_kernel(t_ref, o_ref):
     count = o_ref.shape[1] // 128
-    first = pl.program_id(0) * count
+    first = pl.program_id(0) * 64
     for t in range(count):
-        o_ref[:, t * 128 : (t + 1) * 128] = t_ref[first + t]
+        o_ref[:, t * 128 : (t + 1) * 128] = t_ref[first + (t // 64) * 128 + t % 64]
+
+
+def to_steps(a):
+    return lax.all_to_all(a, STEPS, split_axis=0, concat_axis=0, tiled=True)
 
 
 def to_chips(a):
@@ -458,12 +472,12 @@
     parts = to_chips(gram_more(core, other, gram(core, panels)).reshape(64, SHARE // 4, 4, 128))
     tiles = eigvecs.reshape(4, 512, 128).transpose(1, 0, 2)
     chased = chase(tiles, reflectors, offsets, lengths)
-    mine = to_chips(share(chased.reshape(64, 8, 4, 128), parts)).reshape(64 * (32 + SHARE), 128)
+    mine = to_steps(share(chased.reshape(64, 8, 4, 128), parts)).reshape(64 * (32 + SHARE), 128)
     half = compact(mine)
     theirs = swap_cores(half)
-    projected = to_chips(project(core, mine, panels, other).reshape(64, 32, 128))
-    weights = to_chips(solve(core, half, theirs, projected)).reshape(2048, 128)
-    result = to_chips(update(core, mine, weights, panels, other).reshape(64, 32, 128))
+    projected = to_steps(project(core, mine, panels, other).reshape(64, 32, 128))
+    weights = to_steps(solve(core, half, theirs, projected)).reshape(2048, 128)
+    result = to_steps(update(core, mine, weights, panels, other).reshape(64, 32, 128))
     return pl.pallas_call(
         finish_kernel,
         out_shape=jax.ShapeDtypeStruct((4, 65536), F32),

time: 158 us -> 157 us (level)
  no operation moved by 1% of the time
where the time goes in v12:
time: 157 us; the launch traced here: 156 us
  blocking collectives  105 us (67%)
  Pallas kernels  29.9 us (19%)
  starting transfers between devices  11.8 us (8%)
  waiting for transfers between devices  5.74 us (4%)
  local copies, waits for them, and re-layouts  4.22 us (3%)
    all_to_all x4, blocking collectives, to_steps(): return lax.all_to_all(a, STEPS, split_axis=0, concat_axis=0, tiled=True)  105 us
    pallas_call x1, Pallas kernels, chase(): pl.pallas_call(chase_kernel, out_shape=jax.ShapeDtypeStruct(tiles.shape,...  15.7 us
    all_to_all x1, starting transfers between devices, to_chips(): return lax.all_to_all(a, CHIPS, split_axis=0, concat_axis=0, tiled=True)  11.7 us
    all_to_all x1, waiting for transfers between devices, to_chips(): return lax.all_to_all(a, CHIPS, split_axis=0, concat_axis=0, tiled=True)  4.27 us
    unnamed x6, local copies, waits for them, and re-layouts  4.22 us
    pallas_call x1, Pallas kernels, solve(): pl.pallas_call(solve_kernel, out_shape=jax.ShapeDtypeStruct(p.shape, F32)...  3.67 us
  transfers between devices with their start and end apart: 3, of which 2 were waited for; matrix products, arithmetic and copies ran while one was open for 0% of the time, Pallas kernels for 12%

profile of v12, /device:TPU:0, one launch (start us, length us, event | category | flops | bytes accessed | tf_op | source)
XLA Modules:
  0.0 156.2 jit_solution(17406557512013676979)
XLA Ops:
  0.0 0.0 collective-permute-start
  0.0 0.0 copy-start
  0.0 1.6 %copy-done = f32[512,1024]{1,0:T(8,128)S(1)} copy-done((f32[512,1024]{1,0:T(8,128)S(1)}, f32[512,1024]{1,0:T(8,128)}, u32[]{:S(2)}) %copy-start) | copy-done | bytes 2097176
  1.6 1.3 gram.1.before_ref
  2.9 1.5 collective-permute-done.v_ref.other_ref
  4.4 2.1 %gram_more.1 = f32[2304,128]{1,0:T(8,128)} custom-call(s32[1]{0:T(128)} %bitcast.core, f32[512,1024]{1,0:T(8,128)S(1)} %collective-permute-done.v_ref.other_ref, f32[2304,128]{1,0:T(8,128)S(1)} %gram.1.before_ref), custom_call_target="tpu_custom_call" | custom-call | flops 1000000000 | bytes 4194304 | tf_op jit(solution)/shard_map/gram_more/pallas_call | solution.py:291
  6.5 11.7 %all-to-all-start = ((f32[64,9,4,128]{3,2,1,0:T(4,128)}), f32[64,9,4,128]{3,2,1,0:T(4,128)S(1)}, u32[]{:S(2)}, u32[]{:S(2)}) async-start(f32[64,9,4,128]{3,2,1,0:T(4,128)} %bitcast.4), calls=%async_computation | async-start | bytes 2359296 | tf_op jit(solution)/shard_map/all_to_all | solution.py:462
  18.2 15.7 %chase.1 = f32[512,4,128]{2,1,0:T(4,128)} custom-call(s32[24]{0:T(128)} %offsets.1, s32[24]{0:T(128)} %lengths.1, f32[512,4,128]{2,1,0:T(4,128)} %bitcast.19, f32[24,256,128]{2,1,0:T(8,128)} %m_hbm.1), custom_call_target="tpu_custom_call" | custom-call | flops 20000000000 | bytes 7340032 | tf_op jit(solution)/shard_map/chase/pallas_call | solution.py:215
  33.9 4.3 %all-to-all-done.g_ref = f32[64,9,4,128]{3,2,1,0:T(4,128)S(1)} async-done(((f32[64,9,4,128]{3,2,1,0:T(4,128)}), f32[64,9,4,128]{3,2,1,0:T(4,128)S(1)}, u32[]{:S(2)}, u32[]{:S(2)}) %all-to-all-start) | async-done | bytes 1179680 | tf_op jit(solution)/shard_map/all_to_all | solution.py:462
  38.2 0.0 copy-start.2
  38.2 1.2 copy-done.2
  39.4 0.5 share.1
  39.9 37.0 %all_to_all.25 = f32[64,17,4,128]{3,2,1,0:T(4,128)S(1)} all-to-all(f32[64,17,4,128]{3,2,1,0:T(4,128)S(1)} %share.1), channel_id=1, replica_groups=mesh['yh'=2,'x'=4,'yl'=2,'z'=4,'c'=2] {'x','yh','yl','z'}, dimensions={0} | all-to-all | bytes 4456448 | tf_op jit(solution)/shard_map/all_to_all | solution.py:458
  77.0 0.0 copy-start.1
  77.0 0.1 compact.1.own_ref
  77.0 0.1 collective-permute-start.1
  77.1 1.4 copy-done.1
  78.5 2.4 %project.1 = f32[2048,128]{1,0:T(8,128)S(1)} custom-call(s32[1]{0:T(128)} %bitcast.core, f32[4352,128]{1,0:T(8,128)S(1)} %bitcast.12, f32[512,1024]{1,0:T(8,128)S(1)} %copy-done.1, f32[512,1024]{1,0:T(8,128)S(1)} %collective-permute-done.v_ref.other_ref), custom_call_target="tpu_custom_call" | custom-call | flops 2000000000 | bytes 6291456 | tf_op jit(solution)/shard_map/project/pallas_call | solution.py:413
  81.0 23.0 %all_to_all.26.p_ref = f32[64,32,128]{2,1,0:T(8,128)S(1)} all-to-all(f32[64,32,128]{2,1,0:T(8,128)S(1)} %bitcast.17), channel_id=1, replica_groups=mesh['yh'=2,'x'=4,'yl'=2,'z'=4,'c'=2] {'x','yh','yl','z'}, dimensions={0} | all-to-all | bytes 2097152 | tf_op jit(solution)/shard_map/all_to_all | solution.py:458
  104.0 0.0 collective-permute-done.1.other_ref
  104.0 3.7 %solve.1 = f32[64,32,128]{2,1,0:T(8,128)S(1)} custom-call(s32[1]{0:T(128)} %bitcast.core, f32[2304,128]{1,0:T(8,128)S(1)} %compact.1.own_ref, f32[2304,128]{1,0:T(8,128)S(1)} %collective-permute-done.1.other_ref, f32[64,32,128]{2,1,0:T(8,128)S(1)} %all_to_all.26.p_ref), custom_call_target="tpu_custom_call" | custom-call | flops 4000000000 | bytes 5242880 | tf_op jit(solution)/shard_map/solve/pallas_call | solution.py:362
  107.7 22.2 %all_to_all.27 = f32[64,32,128]{2,1,0:T(8,128)S(1)} all-to-all(f32[64,32,128]{2,1,0:T(8,128)S(1)} %solve.1), channel_id=1, replica_groups=mesh['yh'=2,'x'=4,'yl'=2,'z'=4,'c'=2] {'x','yh','yl','z'}, dimensions={0} | all-to-all | bytes 2097152 | tf_op jit(solution)/shard_map/all_to_all | solution.py:458
  129.9 3.1 %update.1 = f32[2048,128]{1,0:T(8,128)S(1)} custom-call(s32[1]{0:T(128)} %bitcast.core, f32[4352,128]{1,0:T(8,128)S(1)} %bitcast.13, f32[2048,128]{1,0:T(8,128)S(1)} %bitcast.14, f32[512,1024]{1,0:T(8,128)S(1)} %copy-done.1, f32[512,1024]{1,0:T(8,128)S(1)} %collective-permute-done.v_ref.other_ref), custom_call_target="tpu_custom_call" | custom-call | flops 2000000000 | bytes 7340032 | tf_op jit(solution)/shard_map/update/pallas_call | solution.py:439
  133.0 22.3 %all_to_all.28 = f32[64,32,128]{2,1,0:T(8,128)S(1)} all-to-all(f32[64,32,128]{2,1,0:T(8,128)S(1)} %bitcast.15), channel_id=1, replica_groups=mesh['yh'=2,'x'=4,'yl'=2,'z'=4,'c'=2] {'x','yh','yl','z'}, dimensions={0} | all-to-all | bytes 2097152 | tf_op jit(solution)/shard_map/all_to_all | solution.py:458
  155.2 1.0 finish.1
Async XLA Ops:
  0.0 4.4 %collective-permute-start = (f32[512,1024]{1,0:T(8,128)}, f32[512,1024]{1,0:T(8,128)S(1)}, u32[]{:S(2)}, u32[]{:S(2)}) collective-permute-start(f32[512,1024]{1,0:T(8,128)} %own_ref.3), channel_id=1, source_target_pairs={{0,1},{1,0},{2,3},{3,2},{4,5},{5,4},{6,7},{7,6},{8,9},{9,8},{10,11... | collective-permute-start | bytes 6291464 | tf_op jit(solution)/shard_map/ppermute | solution.py:466
  0.0 1.6 %copy-start = (f32[512,1024]{1,0:T(8,128)S(1)}, f32[512,1024]{1,0:T(8,128)}, u32[]{:S(2)}) copy-start(f32[512,1024]{1,0:T(8,128)} %own_ref.3) | copy-start | bytes 6291460
  6.5 31.7 %all-to-all-start = ((f32[64,9,4,128]{3,2,1,0:T(4,128)}), f32[64,9,4,128]{3,2,1,0:T(4,128)S(1)}, u32[]{:S(2)}, u32[]{:S(2)}) async-start(f32[64,9,4,128]{3,2,1,0:T(4,128)} %bitcast.4), calls=%async_computation | async-start | bytes 2359296 | tf_op jit(solution)/shard_map/all_to_all | solution.py:462
  38.2 1.2 copy-start.2
  77.0 1.6 %copy-start.1 = (f32[512,1024]{1,0:T(8,128)S(1)}, f32[512,1024]{1,0:T(8,128)}, u32[]{:S(2)}) copy-start(f32[512,1024]{1,0:T(8,128)} %own_ref.3) | copy-start | bytes 6291460
  77.0 26.9 %collective-permute-start.1 = (f32[2304,128]{1,0:T(8,128)S(1)}, f32[2304,128]{1,0:T(8,128)S(1)}, u32[]{:S(2)}, u32[]{:S(2)}) collective-permute-start(f32[2304,128]{1,0:T(8,128)S(1)} %compact.1.own_ref), channel_id=1, source_target_pairs={{0,1},{1,0},{2,3},{3,2},{4,5},{5,4},{6,7},{7,6},{8,9},{9,8},{10,11... | collective-permute-start | bytes 3538952 | tf_op jit(solution)/shard_map/ppermute | solution.py:466

commit v13 on v12

--- a/solution.py
+++ b/solution.py
@@ -375,23 +375,23 @@
     return jnp.concatenate([ref[pl.ds(j * 4 + r, 64, stride=stride), :] for r in range(4)], axis=0)
 
 
-def compact_kernel(e_ref, half_ref):
+def compact_kernel(e_ref, own_ref, half_ref):
     stride = 32 + SHARE
     for s in range(64):
         chip = CHIP_AT[s]
         half_ref[chip * SHARE : (chip + 1) * SHARE, :] = e_ref[s * stride + 32 : (s + 1) * stride, :]
 
 
-def compact(e):
+def compact(e, own):
     return pl.pallas_call(
         compact_kernel,
         out_shape=jax.ShapeDtypeStruct((STARTS[-1], 128), F32),
-        in_specs=[vmem()],
+        in_specs=[vmem()] * 2,
         out_specs=vmem(),
         compiler_params=params(),
-        cost_estimate=pl.CostEstimate(flops=0, bytes_accessed=2 << 20, transcendentals=0),
+        cost_estimate=pl.CostEstimate(flops=0, bytes_accessed=6 << 20, transcendentals=0),
         name="compact",
-    )(e)
+    )(e, own)
 
 
 def project_kernel(core, e_ref, own_ref, other_ref, p_ref):
@@ -473,7 +473,7 @@
     tiles = eigvecs.reshape(4, 512, 128).transpose(1, 0, 2)
     chased = chase(tiles, reflectors, offsets, lengths)
     mine = to_steps(share(chased.reshape(64, 8, 4, 128), parts)).reshape(64 * (32 + SHARE), 128)
-    half = compact(mine)
+    half = compact(mine, panels)
     theirs = swap_cores(half)
     projected = to_steps(project(core, mine, panels, other).reshape(64, 32, 128))
     weights = to_steps(solve(core, half, theirs, projected)).reshape(2048, 128)

time: 157 us -> 157 us (level)
    all_to_all x4, blocking collectives: 105 us -> 106 us  [to_steps(): return lax.all_to_all(a, STEPS, split_axis=0, concat_axis=0, tiled=True)]
where the time goes in v13:
time: 157 us
  blocking collectives  106 us (68%)
  Pallas kernels  29.9 us (19%)
  starting transfers between devices  11.8 us (8%)
  waiting for transfers between devices  5.73 us (4%)
  local copies, waits for them, and re-layouts  2.82 us (2%)
    all_to_all x4, blocking collectives, to_steps(): return lax.all_to_all(a, STEPS, split_axis=0, concat_axis=0, tiled=True)  106 us
    pallas_call x1, Pallas kernels, chase(): pl.pallas_call(chase_kernel, out_shape=jax.ShapeDtypeStruct(tiles.shape,...  15.7 us
    all_to_all x1, starting transfers between devices, to_chips(): return lax.all_to_all(a, CHIPS, split_axis=0, concat_axis=0, tiled=True)  11.7 us
    all_to_all x1, waiting for transfers between devices, to_chips(): return lax.all_to_all(a, CHIPS, split_axis=0, concat_axis=0, tiled=True)  4.26 us
    pallas_call x1, Pallas kernels, solve(): pl.pallas_call(solve_kernel, out_shape=jax.ShapeDtypeStruct(p.shape, F32)...  3.67 us
  transfers between devices with their start and end apart: 3, of which 2 were waited for; matrix products, arithmetic and copies ran while one was open for 0% of the time, Pallas kernels for 12%

profile of v13, /device:TPU:0, one launch (start us, length us, event | category | flops | bytes accessed | tf_op | source)
XLA Modules:
  0.0 156.5 jit_solution(16990515297708585894)
XLA Ops:
  0.0 0.0 collective-permute-start
  0.0 0.0 copy-start
  0.0 1.6 %copy-done = f32[512,1024]{1,0:T(8,128)S(1)} copy-done((f32[512,1024]{1,0:T(8,128)S(1)}, f32[512,1024]{1,0:T(8,128)}, u32[]{:S(2)}) %copy-start) | copy-done | bytes 2097176
  1.6 1.3 gram.1.before_ref
  2.9 1.5 collective-permute-done.v_ref.other_ref
  4.4 2.1 %gram_more.1 = f32[2304,128]{1,0:T(8,128)} custom-call(s32[1]{0:T(128)} %bitcast.core, f32[512,1024]{1,0:T(8,128)S(1)} %collective-permute-done.v_ref.other_ref, f32[2304,128]{1,0:T(8,128)S(1)} %gram.1.before_ref), custom_call_target="tpu_custom_call" | custom-call | flops 1000000000 | bytes 4194304 | tf_op jit(solution)/shard_map/gram_more/pallas_call | solution.py:291
  6.5 11.7 %all-to-all-start = ((f32[64,9,4,128]{3,2,1,0:T(4,128)}), f32[64,9,4,128]{3,2,1,0:T(4,128)S(1)}, u32[]{:S(2)}, u32[]{:S(2)}) async-start(f32[64,9,4,128]{3,2,1,0:T(4,128)} %bitcast.4), calls=%async_computation | async-start | bytes 2359296 | tf_op jit(solution)/shard_map/all_to_all | solution.py:462
  18.2 15.7 %chase.1 = f32[512,4,128]{2,1,0:T(4,128)} custom-call(s32[24]{0:T(128)} %offsets.1, s32[24]{0:T(128)} %lengths.1, f32[512,4,128]{2,1,0:T(4,128)} %bitcast.19, f32[24,256,128]{2,1,0:T(8,128)} %m_hbm.1), custom_call_target="tpu_custom_call" | custom-call | flops 20000000000 | bytes 7340032 | tf_op jit(solution)/shard_map/chase/pallas_call | solution.py:215
  34.0 4.3 %all-to-all-done.g_ref = f32[64,9,4,128]{3,2,1,0:T(4,128)S(1)} async-done(((f32[64,9,4,128]{3,2,1,0:T(4,128)}), f32[64,9,4,128]{3,2,1,0:T(4,128)S(1)}, u32[]{:S(2)}, u32[]{:S(2)}) %all-to-all-start) | async-done | bytes 1179680 | tf_op jit(solution)/shard_map/all_to_all | solution.py:462
  38.2 0.0 copy-start.2
  38.2 1.2 copy-done.2
  39.4 0.5 share.1
  39.9 0.0 copy-start.1
  39.9 37.2 %all_to_all.25 = f32[64,17,4,128]{3,2,1,0:T(4,128)S(1)} all-to-all(f32[64,17,4,128]{3,2,1,0:T(4,128)S(1)} %share.1), channel_id=1, replica_groups=mesh['yh'=2,'x'=4,'yl'=2,'z'=4,'c'=2] {'x','yh','yl','z'}, dimensions={0} | all-to-all | bytes 4456448 | tf_op jit(solution)/shard_map/all_to_all | solution.py:458
  77.1 0.0 copy-done.1
  77.1 0.1 compact.1.own_ref
  77.2 0.1 collective-permute-start.1
  77.3 2.4 %project.1 = f32[2048,128]{1,0:T(8,128)S(1)} custom-call(s32[1]{0:T(128)} %bitcast.core, f32[4352,128]{1,0:T(8,128)S(1)} %bitcast.12, f32[512,1024]{1,0:T(8,128)S(1)} %copy-done.1, f32[512,1024]{1,0:T(8,128)S(1)} %collective-permute-done.v_ref.other_ref), custom_call_target="tpu_custom_call" | custom-call | flops 2000000000 | bytes 6291456 | tf_op jit(solution)/shard_map/project/pallas_call | solution.py:413
  79.7 24.4 %all_to_all.26.p_ref = f32[64,32,128]{2,1,0:T(8,128)S(1)} all-to-all(f32[64,32,128]{2,1,0:T(8,128)S(1)} %bitcast.17), channel_id=1, replica_groups=mesh['yh'=2,'x'=4,'yl'=2,'z'=4,'c'=2] {'x','yh','yl','z'}, dimensions={0} | all-to-all | bytes 2097152 | tf_op jit(solution)/shard_map/all_to_all | solution.py:458
  104.1 0.0 collective-permute-done.1.other_ref
  104.1 3.7 %solve.1 = f32[64,32,128]{2,1,0:T(8,128)S(1)} custom-call(s32[1]{0:T(128)} %bitcast.core, f32[2304,128]{1,0:T(8,128)S(1)} %compact.1.own_ref, f32[2304,128]{1,0:T(8,128)S(1)} %collective-permute-done.1.other_ref, f32[64,32,128]{2,1,0:T(8,128)S(1)} %all_to_all.26.p_ref), custom_call_target="tpu_custom_call" | custom-call | flops 4000000000 | bytes 5242880 | tf_op jit(solution)/shard_map/solve/pallas_call | solution.py:362
  107.8 22.4 %all_to_all.27 = f32[64,32,128]{2,1,0:T(8,128)S(1)} all-to-all(f32[64,32,128]{2,1,0:T(8,128)S(1)} %solve.1), channel_id=1, replica_groups=mesh['yh'=2,'x'=4,'yl'=2,'z'=4,'c'=2] {'x','yh','yl','z'}, dimensions={0} | all-to-all | bytes 2097152 | tf_op jit(solution)/shard_map/all_to_all | solution.py:458
  130.2 3.1 %update.1 = f32[2048,128]{1,0:T(8,128)S(1)} custom-call(s32[1]{0:T(128)} %bitcast.core, f32[4352,128]{1,0:T(8,128)S(1)} %bitcast.13, f32[2048,128]{1,0:T(8,128)S(1)} %bitcast.14, f32[512,1024]{1,0:T(8,128)S(1)} %copy-done.1, f32[512,1024]{1,0:T(8,128)S(1)} %collective-permute-done.v_ref.other_ref), custom_call_target="tpu_custom_call" | custom-call | flops 2000000000 | bytes 7340032 | tf_op jit(solution)/shard_map/update/pallas_call | solution.py:439
  133.3 22.2 %all_to_all.28 = f32[64,32,128]{2,1,0:T(8,128)S(1)} all-to-all(f32[64,32,128]{2,1,0:T(8,128)S(1)} %bitcast.15), channel_id=1, replica_groups=mesh['yh'=2,'x'=4,'yl'=2,'z'=4,'c'=2] {'x','yh','yl','z'}, dimensions={0} | all-to-all | bytes 2097152 | tf_op jit(solution)/shard_map/all_to_all | solution.py:458
  155.5 1.0 finish.1
Async XLA Ops:
  0.0 4.4 %collective-permute-start = (f32[512,1024]{1,0:T(8,128)}, f32[512,1024]{1,0:T(8,128)S(1)}, u32[]{:S(2)}, u32[]{:S(2)}) collective-permute-start(f32[512,1024]{1,0:T(8,128)} %own_ref.5), channel_id=1, source_target_pairs={{0,1},{1,0},{2,3},{3,2},{4,5},{5,4},{6,7},{7,6},{8,9},{9,8},{10,11... | collective-permute-start | bytes 6291464 | tf_op jit(solution)/shard_map/ppermute | solution.py:466
  0.0 1.6 %copy-start = (f32[512,1024]{1,0:T(8,128)S(1)}, f32[512,1024]{1,0:T(8,128)}, u32[]{:S(2)}) copy-start(f32[512,1024]{1,0:T(8,128)} %own_ref.5) | copy-start | bytes 6291460
  6.5 31.7 %all-to-all-start = ((f32[64,9,4,128]{3,2,1,0:T(4,128)}), f32[64,9,4,128]{3,2,1,0:T(4,128)S(1)}, u32[]{:S(2)}, u32[]{:S(2)}) async-start(f32[64,9,4,128]{3,2,1,0:T(4,128)} %bitcast.4), calls=%async_computation | async-start | bytes 2359296 | tf_op jit(solution)/shard_map/all_to_all | solution.py:462
  38.2 1.2 copy-start.2
  39.9 37.2 %copy-start.1 = (f32[512,1024]{1,0:T(8,128)S(1)}, f32[512,1024]{1,0:T(8,128)}, u32[]{:S(2)}) copy-start(f32[512,1024]{1,0:T(8,128)} %own_ref.5) | copy-start | bytes 6291460
  77.2 26.9 %collective-permute-start.1 = (f32[2304,128]{1,0:T(8,128)S(1)}, f32[2304,128]{1,0:T(8,128)S(1)}, u32[]{:S(2)}, u32[]{:S(2)}) collective-permute-start(f32[2304,128]{1,0:T(8,128)S(1)} %compact.1.own_ref), channel_id=1, source_target_pairs={{0,1},{1,0},{2,3},{3,2},{4,5},{5,4},{6,7},{7,6},{8,9},{9,8},{10,11... | collective-permute-start | bytes 3538952 | tf_op jit(solution)/shard_map/ppermute | solution.py:466
